TPU v7x, 256 devices: a whole 4x4x8 slice. The times are simulated.
256 devices in a mesh: ctx: 32 (over x, z), head: 8 (over y, core).
Axes of the slice: x: 4, y: 4, z: 8, core: 2. Of those that a mesh axis runs over, the one named last changes fastest.
Arguments:
- ssm_input: bfloat16 [8192, 8192], P('ctx', 'head'), may hold values from -32 to 32
- gate_input: bfloat16 [8192, 8192], P('ctx', 'head'), may hold values from -6 to 6
- write_map: bfloat16 [8192, 128], P('ctx'), may hold values from -0.5 to 0.5
- read_map: bfloat16 [8192, 128], P('ctx'), may hold values from -0.5 to 0.5
- log_decay: float32 [8192, 64], P('ctx', 'head'), may hold values from -2.2 to 0
- doc_start: int32 [8192], P('ctx'), may hold values from 0 to 8064, as said below
- ssm_grad: bfloat16 [8192, 8192], P('ctx', 'head'), may hold values from -6 to 6
- att_queries: bfloat16 [8192, 4096], P('ctx', 'head'), may hold values from -32 to 32
- att_keys: bfloat16 [8192, 4096], P('ctx', 'head'), may hold values from -20 to 20
- att_values: bfloat16 [8192, 4096], P('ctx', 'head'), may hold values from -6 to 6
- att_grad: bfloat16 [8192, 4096], P('ctx', 'head'), may hold values from -6 to 6
Outputs:
- mixer_out: bfloat16 [8192, 8192], P('ctx', 'head')
- window_out: bfloat16 [8192, 4096], P('ctx', 'head')
- input_grad: bfloat16 [8192, 8192], P('ctx', 'head')
- gate_grad: bfloat16 [8192, 8192], P('ctx', 'head')
- write_grad: bfloat16 [8192, 128], P('ctx')
- read_grad: bfloat16 [8192, 128], P('ctx')
- query_grad: bfloat16 [8192, 4096], P('ctx', 'head')
- key_grad: bfloat16 [8192, 4096], P('ctx', 'head')
- value_grad: bfloat16 [8192, 4096], P('ctx', 'head')
Inputs may be any that keep to these rules, and one draw needn't show every extreme that they name: doc_start[t] is the position of the first token of the document holding token t; the 8 documents are runs of consecutive positions, the first starts at 0 and the last at 8064; one document other than the first and the last is exactly 4608 tokens long.
All inputs are finite; a program needn't handle non-finite values.
Results may differ from a plain program's by a relative error of at most 0.007.
Values may be sent and summed in bfloat16 or wider, within the bound.
A program may use at most 128 MiB of HBM per device.

v0:
```python
import jax
import jax.numpy as jnp
from jax import lax
from jax.sharding import PartitionSpec as P

SSM_HEADS = 64
HEAD_DIM = 128
ATT_DIM = 128
WINDOW = 4096
BLOCK = 128


PRECISE = lax.Precision.HIGHEST
EPSILON = 1e-05


def entering(part, axis, combine, identity, reverse):
    count = lax.axis_size(axis)
    place = lax.axis_index(axis)
    ahead = count - 1 - place if reverse else place
    gathered = jax.tree.map(lambda a: lax.all_gather(a, axis), part)
    state = jax.tree.map(lambda a, e: jnp.zeros_like(a) + jnp.asarray(e, a.dtype), part, identity)

    def one(lap, state):
        source = count - 1 - lap if reverse else lap
        return combine(
            state, jax.tree.map(lambda a: lax.dynamic_index_in_dim(a, source, 0, False), gathered)
        )

    return lax.fori_loop(0, ahead, one, state)


def shifted(shard, axis, by):
    devices = lax.axis_size(axis)
    pairs = [(i, i + by) for i in range(devices) if 0 <= i + by < devices]
    return lax.ppermute(shard, axis, pairs)


def prepare(log_rates, doc_marks):
    block_count = doc_marks.shape[0] // BLOCK
    head_count = log_rates.shape[1]
    cumulative = jnp.cumsum(log_rates.reshape(block_count, BLOCK, head_count), axis=1)
    marks = doc_marks.reshape(block_count, BLOCK)
    lower = jnp.arange(BLOCK)[:, None] >= jnp.arange(BLOCK)[None, :]
    joined = (marks[:, :, None] == marks[:, None, :]) & lower[None]
    spread = cumulative[:, :, None, :] - cumulative[:, None, :, :]
    decay = jnp.where(joined[..., None], jnp.exp(jnp.minimum(spread, 0.0)), 0.0)
    decay = jnp.transpose(decay, (0, 3, 1, 2))
    to_end = jnp.where(
        (marks == marks[:, -1:])[..., None], jnp.exp(cumulative[:, -1:, :] - cumulative), 0.0
    )
    return (decay, to_end, jnp.exp(cumulative), marks, cumulative[:, -1, :])


def link(earlier, later):
    early_empty, early_away, early_touch, early_total, early_state = earlier
    late_vacant_state, late_away, late_touch, late_total, late_state = later
    joined = (late_away == late_touch) & (late_touch == early_touch)
    factor = jnp.where(joined, jnp.exp(late_total), 0.0)
    carried = late_state + factor[:, None, None] * early_state
    state = jnp.where(late_vacant_state > 0.5, early_state, carried)
    away = jnp.where(early_empty > 0.5, late_away, early_away)
    touch = jnp.where(late_vacant_state > 0.5, early_touch, late_touch)
    return (early_empty * late_vacant_state, away, touch, early_total + late_total, state)


def block_states(prepared, keys_in, values_in):
    return jnp.einsum("cqh,cqn,cqhp->chnp", prepared[1], keys_in, values_in, precision=PRECISE)


def run_chain(prepared, states, start):
    marks = prepared[3]
    block_count = marks.shape[0]
    piece_list = (
        jnp.zeros((block_count, 1), jnp.float32),
        marks[:, :1],
        marks[:, -1:],
        prepared[4],
        states,
    )

    def step(running, piece):
        return (link(running, piece), running)

    final, before = lax.scan(step, start, piece_list)
    return (final, before[4], before[2][:, 0])


def mix_shared(prepared, queries, keys_in, values_in, before, touch):
    decay, to_end, enter, marks, totals = prepared
    scores = jnp.einsum("ctn,csn->cts", queries, keys_in, precision=PRECISE)
    inner = jnp.einsum("chts,cshp->cthp", decay * scores[:, None], values_in, precision=PRECISE)
    opened = jnp.where((marks == touch[:, None])[..., None], enter, 0.0)
    outer = jnp.einsum("ctn,chnp->cthp", queries, before, precision=PRECISE)
    return inner + opened[..., None] * outer


def mix_heads(prepared, queries, keys_in, values_in, before, touch):
    decay, to_end, enter, marks, totals = prepared
    scores = jnp.einsum("cthp,cshp->chts", queries, keys_in, precision=PRECISE)
    inner = jnp.einsum("chts,csn->ctn", decay * scores, values_in, precision=PRECISE)
    opened = jnp.where((marks == touch[:, None])[..., None], enter, 0.0)
    outer = jnp.einsum("cth,cthp,chnp->ctn", opened, queries, before, precision=PRECISE)
    return inner + outer


def head_cols(array, head_index):
    return lax.dynamic_slice_in_dim(array, head_index * ATT_DIM, ATT_DIM, 1)


def body(
    ssm_input,
    gate_input,
    write_map,
    read_map,
    log_decay,
    doc_start,
    ssm_grad,
    att_queries,
    att_keys,
    att_values,
    att_grad,
):
    length = ssm_input.shape[0]
    head_count = ssm_input.shape[1] // HEAD_DIM
    block_count = length // BLOCK
    state_dim = write_map.shape[1]
    inputs_blk = ssm_input.astype(jnp.float32).reshape(block_count, BLOCK, head_count, HEAD_DIM)
    writes_flat = write_map.astype(jnp.float32)
    reads_flat = read_map.astype(jnp.float32)
    writes_blk = writes_flat.reshape(block_count, BLOCK, state_dim)
    reads_blk = reads_flat.reshape(block_count, BLOCK, state_dim)
    doc_marks = doc_start.astype(jnp.float32)
    blank = (
        jnp.ones((1,), jnp.float32),
        -jnp.ones((1,), jnp.float32),
        -jnp.ones((1,), jnp.float32),
        jnp.zeros((head_count,), jnp.float32),
        jnp.zeros((head_count, state_dim, HEAD_DIM), jnp.float32),
    )
    prepared = prepare(log_decay, doc_marks)
    states = block_states(prepared, writes_blk, inputs_blk)
    local_sum, _, _ = run_chain(prepared, states, blank)
    arriving = entering(local_sum, "ctx", link, blank, False)
    _, before, touch = run_chain(prepared, states, arriving)
    mixed = mix_shared(prepared, reads_blk, writes_blk, inputs_blk, before, touch).reshape(
        length, head_count * HEAD_DIM
    )
    gate_full = gate_input.astype(jnp.float32)
    sigma = jax.nn.sigmoid(gate_full)
    swish = gate_full * sigma
    gated = mixed * swish
    width_all = SSM_HEADS * HEAD_DIM
    squares = lax.psum(jnp.sum(gated * gated, axis=1), "head")
    row_scale = lax.rsqrt(squares / width_all + EPSILON)
    mixer_out = (gated * row_scale[:, None]).astype(jnp.bfloat16)
    grad_full = ssm_grad.astype(jnp.float32)
    inner = lax.psum(jnp.sum(grad_full * gated, axis=1), "head")
    dgated = row_scale[:, None] * grad_full - (row_scale**3 * inner / width_all)[:, None] * gated
    dmixed = dgated * swish
    gate_grad = (dgated * mixed * sigma * (1.0 + gate_full * (1.0 - sigma))).astype(jnp.bfloat16)
    dmixed_blk = dmixed.reshape(block_count, BLOCK, head_count, HEAD_DIM)
    read_part = mix_heads(prepared, dmixed_blk, inputs_blk, writes_blk, before, touch).reshape(
        length, state_dim
    )
    rev_rates = jnp.concatenate(
        [jnp.zeros((1, head_count), jnp.float32), log_decay[::-1][:-1]], axis=0
    )
    rev_prepared = prepare(rev_rates, doc_marks[::-1])
    rev_reads = reads_flat[::-1].reshape(block_count, BLOCK, state_dim)
    rev_writes = writes_flat[::-1].reshape(block_count, BLOCK, state_dim)
    rev_inputs = ssm_input.astype(jnp.float32)[::-1].reshape(
        block_count, BLOCK, head_count, HEAD_DIM
    )
    rev_dmixed = dmixed[::-1].reshape(block_count, BLOCK, head_count, HEAD_DIM)
    rev_states = block_states(rev_prepared, rev_reads, rev_dmixed)
    rev_local, _, _ = run_chain(rev_prepared, rev_states, blank)
    first_rate = log_decay[0]
    rev_local = (
        rev_local[0],
        rev_local[1],
        rev_local[2],
        rev_local[3] + first_rate,
        rev_local[4] * jnp.exp(first_rate)[:, None, None],
    )
    rev_arriving = entering(rev_local, "ctx", link, blank, True)
    _, reversed_prior, rev_touch = run_chain(rev_prepared, rev_states, rev_arriving)
    rev_dx = mix_shared(rev_prepared, rev_writes, rev_reads, rev_dmixed, reversed_prior, rev_touch)
    input_grad = rev_dx.reshape(length, head_count * HEAD_DIM)[::-1].astype(jnp.bfloat16)
    write_part = mix_heads(
        rev_prepared, rev_inputs, rev_dmixed, rev_reads, reversed_prior, rev_touch
    ).reshape(length, state_dim)[::-1]
    write_sum, read_sum = lax.psum((write_part, read_part), "head")
    write_grad = write_sum.astype(jnp.bfloat16)
    read_grad = read_sum.astype(jnp.bfloat16)
    shard_index = lax.axis_index("ctx")
    halo_shards = WINDOW // length
    att_count = att_queries.shape[1] // ATT_DIM
    att_width = att_queries.shape[1]
    score_scale = ATT_DIM ** (-0.5)

    def pass_keys(running, unused):
        moved = shifted((running[0], running[1]), "ctx", 1)
        return (moved, moved)

    _, earlier = lax.scan(pass_keys, (att_keys, att_values), None, length=halo_shards)
    key_all = jnp.concatenate(
        [earlier[0][::-1].reshape(halo_shards * length, att_width), att_keys], axis=0
    )
    value_all = jnp.concatenate(
        [earlier[1][::-1].reshape(halo_shards * length, att_width), att_values], axis=0
    )
    spread_rows = (halo_shards + 1) * length
    query_pos = shard_index * length + jnp.arange(length, dtype=jnp.int32)
    key_pos = (shard_index - halo_shards) * length + jnp.arange(spread_rows, dtype=jnp.int32)
    visible = (
        (key_pos[None, :] <= query_pos[:, None])
        & (query_pos[:, None] - key_pos[None, :] < WINDOW)
        & (key_pos[None, :] >= doc_start[:, None])
    )

    def forward_head(head_index, running):
        out_buf, max_buf, total_buf, delta_buf = running
        query_head = head_cols(att_queries, head_index)
        key_head = head_cols(key_all, head_index)
        value_head = head_cols(value_all, head_index)
        score = (
            jnp.einsum("td,sd->ts", query_head, key_head, preferred_element_type=jnp.float32)
            * score_scale
        )
        row_max = jnp.max(jnp.where(visible, score, -jnp.inf), axis=1)
        expo = jnp.where(visible, jnp.exp(score - row_max[:, None]), 0.0)
        row_total = jnp.sum(expo, axis=1)
        weights = (expo / row_total[:, None]).astype(jnp.bfloat16)
        attended = jnp.dot(weights, value_head, preferred_element_type=jnp.float32)
        delta = jnp.sum(head_cols(att_grad, head_index).astype(jnp.float32) * attended, axis=1)
        out_buf = lax.dynamic_update_slice_in_dim(
            out_buf, attended.astype(jnp.bfloat16), head_index * ATT_DIM, 1
        )
        return (
            out_buf,
            max_buf.at[:, head_index].set(row_max),
            total_buf.at[:, head_index].set(row_total),
            delta_buf.at[:, head_index].set(delta),
        )

    stats_zero = jnp.zeros((length, att_count), jnp.float32)
    window_out, row_maxes, row_totals, row_deltas = lax.fori_loop(
        0,
        att_count,
        forward_head,
        (jnp.zeros((length, att_width), jnp.bfloat16), stats_zero, stats_zero, stats_zero),
    )

    def query_terms(head_index):
        query_head = head_cols(att_queries, head_index)
        key_head = head_cols(key_all, head_index)
        value_head = head_cols(value_all, head_index)
        grad_head = head_cols(att_grad, head_index)
        score = (
            jnp.einsum("td,sd->ts", query_head, key_head, preferred_element_type=jnp.float32)
            * score_scale
        )
        probs = (
            jnp.where(visible, jnp.exp(score - row_maxes[:, head_index][:, None]), 0.0)
            / row_totals[:, head_index][:, None]
        )
        weights = probs.astype(jnp.bfloat16)
        dprobs = jnp.einsum("td,sd->ts", grad_head, value_head, preferred_element_type=jnp.float32)
        dscore = (probs * (dprobs - row_deltas[:, head_index][:, None]) * score_scale).astype(
            jnp.bfloat16
        )
        query_part = jnp.dot(dscore, key_head, preferred_element_type=jnp.float32)
        return (query_head, grad_head, weights, dscore, query_part)

    def backward_head(head_index, running):
        query_buf, key_buf, value_buf = running
        query_head, grad_head, weights, dscore, query_part = query_terms(head_index)
        key_part = jnp.einsum("ts,td->sd", dscore, query_head, preferred_element_type=jnp.float32)
        value_part = jnp.einsum("ts,td->sd", weights, grad_head, preferred_element_type=jnp.float32)
        query_buf = lax.dynamic_update_slice_in_dim(query_buf, query_part, head_index * ATT_DIM, 1)
        key_buf = lax.dynamic_update_slice_in_dim(key_buf, key_part, head_index * ATT_DIM, 1)
        value_buf = lax.dynamic_update_slice_in_dim(value_buf, value_part, head_index * ATT_DIM, 1)
        return (query_buf, key_buf, value_buf)

    part_zero = jnp.zeros((spread_rows, att_width), jnp.float32)
    query_sum, key_parts, value_parts = lax.fori_loop(
        0,
        att_count,
        backward_head,
        (jnp.zeros((length, att_width), jnp.float32), part_zero, part_zero),
    )
    key_blocks = key_parts.reshape(halo_shards + 1, length, att_width)
    value_blocks = value_parts.reshape(halo_shards + 1, length, att_width)

    def send_back(running, block_index):
        moved = shifted((running[0], running[1]), "ctx", -1)
        return ((moved[0] + key_blocks[block_index], moved[1] + value_blocks[block_index]), None)

    (key_sum, value_sum), _ = lax.scan(
        send_back, (key_blocks[0], value_blocks[0]), jnp.arange(1, halo_shards + 1, dtype=jnp.int32)
    )
    return (
        mixer_out,
        window_out,
        input_grad,
        gate_grad,
        write_grad,
        read_grad,
        query_sum.astype(jnp.bfloat16),
        key_sum.astype(jnp.bfloat16),
        value_sum.astype(jnp.bfloat16),
    )


def solution(mesh):
    in_specs = (
        P("ctx", "head"),
        P("ctx", "head"),
        P("ctx", None),
        P("ctx", None),
        P("ctx", "head"),
        P("ctx"),
        P("ctx", "head"),
        P("ctx", "head"),
        P("ctx", "head"),
        P("ctx", "head"),
        P("ctx", "head"),
    )
    out_specs = (
        P("ctx", "head"),
        P("ctx", "head"),
        P("ctx", "head"),
        P("ctx", "head"),
        P("ctx", None),
        P("ctx", None),
        P("ctx", "head"),
        P("ctx", "head"),
        P("ctx", "head"),
    )
    return jax.shard_map(body, mesh=mesh, in_specs=in_specs, out_specs=out_specs, check_vma=False)
```

profile of v0, /device:TPU:1, one launch (start us, length us, event | category | flops | bytes accessed | tf_op | source)
XLA Modules:
  0.0 1653.5 jit_solution(11331237473062940916)
XLA Ops:
  13.3 8.0 while.191
  32.3 65.0 %all-reduce.10 = (f32[32]{0:T(128)S(1)}, f32[32]{0:T(128)S(1)}, f32[32]{0:T(128)S(1)}, f32[256]{0:T(256)S(1)}) all-reduce(f32[32]{0:T(128)S(1)} %dynamic-update-slice.21, f32[32]{0:T(128)S(1)} %dynamic-update-slice.22, f32[32]{0:T(128)S(1)} %dynamic-update-slice.23, ...), channel_id=2, replica_groups=mesh['ctx'=32,'head'=8] {'ctx'}, use_global_device_ids=true, to_apply=%add.1 | all-reduce | flops 352 | bytes 2816
  102.1 63.9 %all-gather.13.cloned.1.call-done = f32[256,128,128]{2,1,0:T(8,128)} async-done(((f32[8,128,128]{2,1,0:T(8,128)}), f32[256,128,128]{2,1,0:T(8,128)}) %all-gather.13.cloned.1.call-update) | async-done | bytes 16777232 | tf_op jit(solution)/shard_map/all_gather | solution.py:21
  177.0 12.8 all-reduce.12
  196.1 8.3 while.192
  204.4 10.0 fusion.110
  215.4 421.2 %while.185 = (s32[]{:T(128)}, bf16[256,512]{1,0:T(8,128)(2,1)S(1)}, bf16[256,512]{1,0:T(8,128)(2,1)S(1)}, bf16[16,256,512]{2,1,0:T(8,128)(2,1)}, bf16[16,256,512]{2,1,0:T(8,128)(2,1)}, /*index=5*/s32[]{:T(128)}) while((s32[]{:T(128)}, bf16[256,512]{1,0:T(8,128)(2,1)S(1)}, bf16[256,512]{1,0:T(8,128)(2,1)S(1)}, ...), condition=%wide.region_10.11_spmd, body=%wide.region_9.10_spmd.sunk | while | flops 2 | bytes 4194469 | solution.py:206
  215.4 7.8 collective-permute-start.1
  223.2 9.5 collective-permute-start
  236.7 10.7 collective-permute-start.1
  247.4 8.6 collective-permute-start
  260.1 9.3 collective-permute-start.1
  269.4 8.6 collective-permute-start
  282.1 8.6 collective-permute-start.1
  290.7 9.7 collective-permute-start
  304.4 9.2 collective-permute-start.1
  313.6 7.8 collective-permute-start
  326.2 10.0 collective-permute-start.1
  336.2 10.2 collective-permute-start
  351.6 8.6 collective-permute-start.1
  360.2 9.3 collective-permute-start
  374.6 8.6 collective-permute-start.1
  383.2 8.6 collective-permute-start
  397.0 10.6 collective-permute-start.1
  421.3 14.8 collective-permute-start.1
  436.1 14.5 collective-permute-start
  457.5 8.9 collective-permute-start.1
  477.0 9.2 collective-permute-done
  487.0 16.3 collective-permute-start.1
  503.3 9.0 collective-permute-start
  513.3 10.6 collective-permute-done
  524.7 11.3 collective-permute-start.1
  536.0 16.9 %collective-permute-start = (bf16[256,512]{1,0:T(8,128)(2,1)S(1)}, bf16[256,512]{1,0:T(8,128)(2,1)S(1)}, u32[]{:S(2)}, u32[]{:S(2)}) collective-permute-start(bf16[256,512]{1,0:T(8,128)(2,1)S(1)} %get-tuple-element.2431), channel_id=1, source_target_pairs={{0,8},{8,16},{16,24},{24,32},{32,40},{40,48},{48,56},{56,64},{64,7... | collective-permute-start | bytes 786440 | tf_op jit(solution)/shard_map/while/body/eval_jaxpr/ppermute | solution.py:36
  553.7 9.4 collective-permute-done
  563.8 10.3 collective-permute-start.1
  574.2 11.5 collective-permute-start
  589.9 8.3 collective-permute-start.1
  598.3 9.9 collective-permute-start
  613.3 8.1 collective-permute-start.1
  621.4 10.1 collective-permute-start
  652.1 56.2 %while.189 = (s32[]{:T(128)}, bf16[256,512]{1,0:T(8,128)(2,1)S(1)}, f32[256,4]{0,1:T(4,128)S(1)}, f32[256,4]{0,1:T(4,128)S(1)}, f32[256,4]{0,1:T(4,128)S(1)}, /*...) while((s32[]{:T(128)}, bf16[256,512]{1,0:T(8,128)(2,1)S(1)}, ...), condition=%wide.region_16.17_spmd.clone, body=%wide.region_11.16_spmd.clone.sunk | while | flops 601751552 | bytes 34228496 | solution.py:248
  717.5 48.1 %while.190 = (s32[]{:T(128)}, bf16[256,512]{1,0:T(8,128)(2,1)S(1)}, f32[4352,512]{1,0:T(8,128)}, f32[4352,512]{1,0:T(8,128)}, bf16[256,512]{1,0:T(8,128)(2,1)S(1...) while((s32[]{:T(128)}, bf16[256,512]{1,0:T(8,128)(2,1)S(1)}, ...), condition=%wide.region_31.32_spmd.clone, body=%wide.region_30.31_spmd.clone.sunk | while | flops 1442775040 | bytes 28283100 | solution.py:287
  769.5 448.4 %while.188 = (s32[]{:T(128)}, f32[256,512]{1,0:T(8,128)}, f32[256,512]{1,0:T(8,128)}, s32[16]{0:T(128)S(1)}, f32[17,256,512]{2,1,0:T(8,128)}, /*index=5*/f32[17,256,512]{2,1,0:T(8,128)}, s32[]{:T(128)}, s32[]{:T(128)}, s32[]{:T(128)}) while((s32[]{:T(128)}, f32[256,512]{1,0:T(8,128)}, f32[256,512]{1,0:T(8,128)}, s32[16]{0:T(128)S(1)}, ...), condition=%wide.region_33.34_spmd, body=%wide.region_32.33_spmd.sunk | while | flops 262149 | bytes 7340259 | solution.py:300
  774.8 10.1 collective-permute-done.3
  801.1 13.4 collective-permute-done.3
  816.4 8.6 collective-permute-done.2
  854.0 18.4 %collective-permute-done.3 = f32[256,512]{1,0:T(8,128)S(1)} collective-permute-done((f32[256,512]{1,0:T(8,128)}, f32[256,512]{1,0:T(8,128)S(1)}, u32[]{:S(2)}, u32[]{:S(2)}) %collective-permute-start.3) | collective-permute-done | bytes 524320 | tf_op jit(solution)/shard_map/while/body/eval_jaxpr/ppermute | solution.py:36
  874.3 8.2 collective-permute-done.2
  889.5 12.3 collective-permute-done.3
  903.8 8.5 collective-permute-done.2
  961.2 8.1 collective-permute-done.3
  981.9 44.6 %collective-permute-done.3 = f32[256,512]{1,0:T(8,128)S(1)} collective-permute-done((f32[256,512]{1,0:T(8,128)}, f32[256,512]{1,0:T(8,128)S(1)}, u32[]{:S(2)}, u32[]{:S(2)}) %collective-permute-start.3) | collective-permute-done | bytes 524320 | tf_op jit(solution)/shard_map/while/body/eval_jaxpr/ppermute | solution.py:36
  1028.4 9.3 collective-permute-done.2
  1044.8 10.7 collective-permute-done.3
  1057.4 9.3 collective-permute-done.2
  1081.7 9.3 collective-permute-done.2
  1098.0 8.8 collective-permute-done.3
  1108.8 9.5 collective-permute-done.2
  1132.6 8.6 collective-permute-done.2
  1155.5 7.7 collective-permute-done.2
  1192.2 15.0 collective-permute-done.3
  1234.0 82.8 %all-reduce.9 = (f32[32]{0:T(128)}, f32[32]{0:T(128)}, f32[32]{0:T(128)}, f32[256]{0:T(256)}) all-reduce(f32[32]{0:T(128)} %dynamic-update-slice.25, f32[32]{0:T(128)} %dynamic-update-slice.26, f32[32]{0:T(128)} %dynamic-update-slice.27, f32[256]{0:T(256)} %copy-done.51), channel_id=7, replica_groups=mesh['ctx'=32,'head'=8] {'ctx'}, use_global_device_ids=true, to_apply=%add.5 | all-reduce | flops 352 | bytes 2816
  1327.1 216.3 %while.186 = (s32[]{:T(128)}, f32[1]{0:T(128)}, f32[8,128,128]{2,1,0:T(8,128)S(1)}, s32[]{:T(128)}, f32[32,1]{0,1:T(1,128)S(1)}, /*index=5*/f32[32,1]{0,1:T(1,12...) while((s32[]{:T(128)}, f32[1]{0:T(128)}, ...), condition=%wide.region_23.24_spmd, body=%wide.region_22.23_spmd.sunk | while | flops 393235 | bytes 1573204 | solution.py:30
  1562.4 83.9 %all-reduce.14 = (bf16[256,128]{1,0:T(8,128)(2,1)}, bf16[256,128]{1,0:T(8,128)(2,1)}) all-reduce(f32[256,128]{1,0:T(8,128)S(1)} %rev.36, f32[256,128]{1,0:T(8,128)S(1)} %bitcast.349), channel_id=1, replica_groups=mesh['ctx'=32,'head'=8] {'head'}, use_global_device_ids=true, to_apply=%region_27.28 | all-reduce | flops 65536 | bytes 393216 | tf_op jit(solution)/shard_map/psum | solution.py:193
  (662 shorter events, 620.0 us)
Async XLA Ops:
  7.2 158.8 %all-gather.13.cloned.1.call-start = ((), (), s32[]{:S(2)}) async-start(), calls=%async_computation | async-start | bytes 17301504 | tf_op jit(solution)/shard_map/all_gather | solution.py:21
  22.1 1304.8 %all-gather.15.cloned.1.call-start = ((), (), s32[]{:S(2)}) async-start(), calls=%async_computation.1 | async-start | bytes 17301504 | tf_op jit(solution)/shard_map/all_gather | solution.py:21
  215.4 17.2 %collective-permute-start.1 = (bf16[256,512]{1,0:T(8,128)(2,1)S(1)}, bf16[256,512]{1,0:T(8,128)(2,1)S(1)}, u32[]{:S(2)}, u32[]{:S(2)}) collective-permute-start(bf16[256,512]{1,0:T(8,128)(2,1)S(1)} %get-tuple-element.2432), channel_id=1, source_target_pairs={{0,8},{8,16},{16,24},{24,32},{32,40},{40,48},{48,56},{56,64},{64,7... | collective-permute-start | bytes 786440 | tf_op jit(solution)/shard_map/while/body/eval_jaxpr/ppermute | solution.py:36
  223.2 12.8 collective-permute-start
  236.7 19.3 %collective-permute-start.1 = (bf16[256,512]{1,0:T(8,128)(2,1)S(1)}, bf16[256,512]{1,0:T(8,128)(2,1)S(1)}, u32[]{:S(2)}, u32[]{:S(2)}) collective-permute-start(bf16[256,512]{1,0:T(8,128)(2,1)S(1)} %get-tuple-element.2432), channel_id=1, source_target_pairs={{0,8},{8,16},{16,24},{24,32},{32,40},{40,48},{48,56},{56,64},{64,7... | collective-permute-start | bytes 786440 | tf_op jit(solution)/shard_map/while/body/eval_jaxpr/ppermute | solution.py:36
  247.4 11.9 collective-permute-start
  260.1 17.9 %collective-permute-start.1 = (bf16[256,512]{1,0:T(8,128)(2,1)S(1)}, bf16[256,512]{1,0:T(8,128)(2,1)S(1)}, u32[]{:S(2)}, u32[]{:S(2)}) collective-permute-start(bf16[256,512]{1,0:T(8,128)(2,1)S(1)} %get-tuple-element.2432), channel_id=1, source_target_pairs={{0,8},{8,16},{16,24},{24,32},{32,40},{40,48},{48,56},{56,64},{64,7... | collective-permute-start | bytes 786440 | tf_op jit(solution)/shard_map/while/body/eval_jaxpr/ppermute | solution.py:36
  269.4 11.9 collective-permute-start
  282.1 18.3 %collective-permute-start.1 = (bf16[256,512]{1,0:T(8,128)(2,1)S(1)}, bf16[256,512]{1,0:T(8,128)(2,1)S(1)}, u32[]{:S(2)}, u32[]{:S(2)}) collective-permute-start(bf16[256,512]{1,0:T(8,128)(2,1)S(1)} %get-tuple-element.2432), channel_id=1, source_target_pairs={{0,8},{8,16},{16,24},{24,32},{32,40},{40,48},{48,56},{56,64},{64,7... | collective-permute-start | bytes 786440 | tf_op jit(solution)/shard_map/while/body/eval_jaxpr/ppermute | solution.py:36
  290.7 12.9 collective-permute-start
  304.4 17.1 %collective-permute-start.1 = (bf16[256,512]{1,0:T(8,128)(2,1)S(1)}, bf16[256,512]{1,0:T(8,128)(2,1)S(1)}, u32[]{:S(2)}, u32[]{:S(2)}) collective-permute-start(bf16[256,512]{1,0:T(8,128)(2,1)S(1)} %get-tuple-element.2432), channel_id=1, source_target_pairs={{0,8},{8,16},{16,24},{24,32},{32,40},{40,48},{48,56},{56,64},{64,7... | collective-permute-start | bytes 786440 | tf_op jit(solution)/shard_map/while/body/eval_jaxpr/ppermute | solution.py:36
  313.6 11.8 collective-permute-start
  326.2 20.2 %collective-permute-start.1 = (bf16[256,512]{1,0:T(8,128)(2,1)S(1)}, bf16[256,512]{1,0:T(8,128)(2,1)S(1)}, u32[]{:S(2)}, u32[]{:S(2)}) collective-permute-start(bf16[256,512]{1,0:T(8,128)(2,1)S(1)} %get-tuple-element.2432), channel_id=1, source_target_pairs={{0,8},{8,16},{16,24},{24,32},{32,40},{40,48},{48,56},{56,64},{64,7... | collective-permute-start | bytes 786440 | tf_op jit(solution)/shard_map/while/body/eval_jaxpr/ppermute | solution.py:36
  336.2 14.6 collective-permute-start
  351.6 17.9 %collective-permute-start.1 = (bf16[256,512]{1,0:T(8,128)(2,1)S(1)}, bf16[256,512]{1,0:T(8,128)(2,1)S(1)}, u32[]{:S(2)}, u32[]{:S(2)}) collective-permute-start(bf16[256,512]{1,0:T(8,128)(2,1)S(1)} %get-tuple-element.2432), channel_id=1, source_target_pairs={{0,8},{8,16},{16,24},{24,32},{32,40},{40,48},{48,56},{56,64},{64,7... | collective-permute-start | bytes 786440 | tf_op jit(solution)/shard_map/while/body/eval_jaxpr/ppermute | solution.py:36
  360.2 13.7 collective-permute-start
  374.6 17.2 %collective-permute-start.1 = (bf16[256,512]{1,0:T(8,128)(2,1)S(1)}, bf16[256,512]{1,0:T(8,128)(2,1)S(1)}, u32[]{:S(2)}, u32[]{:S(2)}) collective-permute-start(bf16[256,512]{1,0:T(8,128)(2,1)S(1)} %get-tuple-element.2432), channel_id=1, source_target_pairs={{0,8},{8,16},{16,24},{24,32},{32,40},{40,48},{48,56},{56,64},{64,7... | collective-permute-start | bytes 786440 | tf_op jit(solution)/shard_map/while/body/eval_jaxpr/ppermute | solution.py:36
  383.2 13.0 collective-permute-start
  397.0 18.2 %collective-permute-start.1 = (bf16[256,512]{1,0:T(8,128)(2,1)S(1)}, bf16[256,512]{1,0:T(8,128)(2,1)S(1)}, u32[]{:S(2)}, u32[]{:S(2)}) collective-permute-start(bf16[256,512]{1,0:T(8,128)(2,1)S(1)} %get-tuple-element.2432), channel_id=1, source_target_pairs={{0,8},{8,16},{16,24},{24,32},{32,40},{40,48},{48,56},{56,64},{64,7... | collective-permute-start | bytes 786440 | tf_op jit(solution)/shard_map/while/body/eval_jaxpr/ppermute | solution.py:36
  407.7 12.9 collective-permute-start
  421.3 29.3 %collective-permute-start.1 = (bf16[256,512]{1,0:T(8,128)(2,1)S(1)}, bf16[256,512]{1,0:T(8,128)(2,1)S(1)}, u32[]{:S(2)}, u32[]{:S(2)}) collective-permute-start(bf16[256,512]{1,0:T(8,128)(2,1)S(1)} %get-tuple-element.2432), channel_id=1, source_target_pairs={{0,8},{8,16},{16,24},{24,32},{32,40},{40,48},{48,56},{56,64},{64,7... | collective-permute-start | bytes 786440 | tf_op jit(solution)/shard_map/while/body/eval_jaxpr/ppermute | solution.py:36
  436.1 20.6 %collective-permute-start = (bf16[256,512]{1,0:T(8,128)(2,1)S(1)}, bf16[256,512]{1,0:T(8,128)(2,1)S(1)}, u32[]{:S(2)}, u32[]{:S(2)}) collective-permute-start(bf16[256,512]{1,0:T(8,128)(2,1)S(1)} %get-tuple-element.2431), channel_id=1, source_target_pairs={{0,8},{8,16},{16,24},{24,32},{32,40},{40,48},{48,56},{56,64},{64,7... | collective-permute-start | bytes 786440 | tf_op jit(solution)/shard_map/while/body/eval_jaxpr/ppermute | solution.py:36
  457.5 18.7 %collective-permute-start.1 = (bf16[256,512]{1,0:T(8,128)(2,1)S(1)}, bf16[256,512]{1,0:T(8,128)(2,1)S(1)}, u32[]{:S(2)}, u32[]{:S(2)}) collective-permute-start(bf16[256,512]{1,0:T(8,128)(2,1)S(1)} %get-tuple-element.2432), channel_id=1, source_target_pairs={{0,8},{8,16},{16,24},{24,32},{32,40},{40,48},{48,56},{56,64},{64,7... | collective-permute-start | bytes 786440 | tf_op jit(solution)/shard_map/while/body/eval_jaxpr/ppermute | solution.py:36
  466.5 19.7 %collective-permute-start = (bf16[256,512]{1,0:T(8,128)(2,1)S(1)}, bf16[256,512]{1,0:T(8,128)(2,1)S(1)}, u32[]{:S(2)}, u32[]{:S(2)}) collective-permute-start(bf16[256,512]{1,0:T(8,128)(2,1)S(1)} %get-tuple-element.2431), channel_id=1, source_target_pairs={{0,8},{8,16},{16,24},{24,32},{32,40},{40,48},{48,56},{56,64},{64,7... | collective-permute-start | bytes 786440 | tf_op jit(solution)/shard_map/while/body/eval_jaxpr/ppermute | solution.py:36
  487.0 25.6 %collective-permute-start.1 = (bf16[256,512]{1,0:T(8,128)(2,1)S(1)}, bf16[256,512]{1,0:T(8,128)(2,1)S(1)}, u32[]{:S(2)}, u32[]{:S(2)}) collective-permute-start(bf16[256,512]{1,0:T(8,128)(2,1)S(1)} %get-tuple-element.2432), channel_id=1, source_target_pairs={{0,8},{8,16},{16,24},{24,32},{32,40},{40,48},{48,56},{56,64},{64,7... | collective-permute-start | bytes 786440 | tf_op jit(solution)/shard_map/while/body/eval_jaxpr/ppermute | solution.py:36
  503.3 20.7 %collective-permute-start = (bf16[256,512]{1,0:T(8,128)(2,1)S(1)}, bf16[256,512]{1,0:T(8,128)(2,1)S(1)}, u32[]{:S(2)}, u32[]{:S(2)}) collective-permute-start(bf16[256,512]{1,0:T(8,128)(2,1)S(1)} %get-tuple-element.2431), channel_id=1, source_target_pairs={{0,8},{8,16},{16,24},{24,32},{32,40},{40,48},{48,56},{56,64},{64,7... | collective-permute-start | bytes 786440 | tf_op jit(solution)/shard_map/while/body/eval_jaxpr/ppermute | solution.py:36
  524.7 28.2 %collective-permute-start.1 = (bf16[256,512]{1,0:T(8,128)(2,1)S(1)}, bf16[256,512]{1,0:T(8,128)(2,1)S(1)}, u32[]{:S(2)}, u32[]{:S(2)}) collective-permute-start(bf16[256,512]{1,0:T(8,128)(2,1)S(1)} %get-tuple-element.2432), channel_id=1, source_target_pairs={{0,8},{8,16},{16,24},{24,32},{32,40},{40,48},{48,56},{56,64},{64,7... | collective-permute-start | bytes 786440 | tf_op jit(solution)/shard_map/while/body/eval_jaxpr/ppermute | solution.py:36
  536.0 27.1 %collective-permute-start = (bf16[256,512]{1,0:T(8,128)(2,1)S(1)}, bf16[256,512]{1,0:T(8,128)(2,1)S(1)}, u32[]{:S(2)}, u32[]{:S(2)}) collective-permute-start(bf16[256,512]{1,0:T(8,128)(2,1)S(1)} %get-tuple-element.2431), channel_id=1, source_target_pairs={{0,8},{8,16},{16,24},{24,32},{32,40},{40,48},{48,56},{56,64},{64,7... | collective-permute-start | bytes 786440 | tf_op jit(solution)/shard_map/while/body/eval_jaxpr/ppermute | solution.py:36
  563.8 21.9 %collective-permute-start.1 = (bf16[256,512]{1,0:T(8,128)(2,1)S(1)}, bf16[256,512]{1,0:T(8,128)(2,1)S(1)}, u32[]{:S(2)}, u32[]{:S(2)}) collective-permute-start(bf16[256,512]{1,0:T(8,128)(2,1)S(1)} %get-tuple-element.2432), channel_id=1, source_target_pairs={{0,8},{8,16},{16,24},{24,32},{32,40},{40,48},{48,56},{56,64},{64,7... | collective-permute-start | bytes 786440 | tf_op jit(solution)/shard_map/while/body/eval_jaxpr/ppermute | solution.py:36
  574.2 15.0 collective-permute-start
  589.9 18.2 %collective-permute-start.1 = (bf16[256,512]{1,0:T(8,128)(2,1)S(1)}, bf16[256,512]{1,0:T(8,128)(2,1)S(1)}, u32[]{:S(2)}, u32[]{:S(2)}) collective-permute-start(bf16[256,512]{1,0:T(8,128)(2,1)S(1)} %get-tuple-element.2432), channel_id=1, source_target_pairs={{0,8},{8,16},{16,24},{24,32},{32,40},{40,48},{48,56},{56,64},{64,7... | collective-permute-start | bytes 786440 | tf_op jit(solution)/shard_map/while/body/eval_jaxpr/ppermute | solution.py:36
  598.3 14.3 collective-permute-start
  613.3 18.2 %collective-permute-start.1 = (bf16[256,512]{1,0:T(8,128)(2,1)S(1)}, bf16[256,512]{1,0:T(8,128)(2,1)S(1)}, u32[]{:S(2)}, u32[]{:S(2)}) collective-permute-start(bf16[256,512]{1,0:T(8,128)(2,1)S(1)} %get-tuple-element.2432), channel_id=1, source_target_pairs={{0,8},{8,16},{16,24},{24,32},{32,40},{40,48},{48,56},{56,64},{64,7... | collective-permute-start | bytes 786440 | tf_op jit(solution)/shard_map/while/body/eval_jaxpr/ppermute | solution.py:36
  621.4 14.5 collective-permute-start
  769.6 15.3 collective-permute-start.3
  771.0 23.1 %collective-permute-start.2 = (f32[256,512]{1,0:T(8,128)}, f32[256,512]{1,0:T(8,128)S(1)}, u32[]{:S(2)}, u32[]{:S(2)}) collective-permute-start(f32[256,512]{1,0:T(8,128)} %get-tuple-element.2671), channel_id=1, source_target_pairs={{8,0},{16,8},{24,16},{32,24},{40,32},{48,40},{56,48},{64,56},{72,6... | collective-permute-start | bytes 1572872 | tf_op jit(solution)/shard_map/while/body/eval_jaxpr/ppermute | solution.py:36
  796.0 18.5 %collective-permute-start.3 = (f32[256,512]{1,0:T(8,128)}, f32[256,512]{1,0:T(8,128)S(1)}, u32[]{:S(2)}, u32[]{:S(2)}) collective-permute-start(f32[256,512]{1,0:T(8,128)} %get-tuple-element.2672), channel_id=1, source_target_pairs={{8,0},{16,8},{24,16},{32,24},{40,32},{48,40},{56,48},{64,56},{72,6... | collective-permute-start | bytes 1572872 | tf_op jit(solution)/shard_map/while/body/eval_jaxpr/ppermute | solution.py:36
  797.3 27.7 %collective-permute-start.2 = (f32[256,512]{1,0:T(8,128)}, f32[256,512]{1,0:T(8,128)S(1)}, u32[]{:S(2)}, u32[]{:S(2)}) collective-permute-start(f32[256,512]{1,0:T(8,128)} %get-tuple-element.2671), channel_id=1, source_target_pairs={{8,0},{16,8},{24,16},{32,24},{40,32},{48,40},{56,48},{64,56},{72,6... | collective-permute-start | bytes 1572872 | tf_op jit(solution)/shard_map/while/body/eval_jaxpr/ppermute | solution.py:36
  826.9 11.7 collective-permute-start.3
  828.1 18.8 %collective-permute-start.2 = (f32[256,512]{1,0:T(8,128)}, f32[256,512]{1,0:T(8,128)S(1)}, u32[]{:S(2)}, u32[]{:S(2)}) collective-permute-start(f32[256,512]{1,0:T(8,128)} %get-tuple-element.2671), channel_id=1, source_target_pairs={{8,0},{16,8},{24,16},{32,24},{40,32},{48,40},{56,48},{64,56},{72,6... | collective-permute-start | bytes 1572872 | tf_op jit(solution)/shard_map/while/body/eval_jaxpr/ppermute | solution.py:36
  848.8 23.5 %collective-permute-start.3 = (f32[256,512]{1,0:T(8,128)}, f32[256,512]{1,0:T(8,128)S(1)}, u32[]{:S(2)}, u32[]{:S(2)}) collective-permute-start(f32[256,512]{1,0:T(8,128)} %get-tuple-element.2672), channel_id=1, source_target_pairs={{8,0},{16,8},{24,16},{32,24},{40,32},{48,40},{56,48},{64,56},{72,6... | collective-permute-start | bytes 1572872 | tf_op jit(solution)/shard_map/while/body/eval_jaxpr/ppermute | solution.py:36
  850.1 32.4 %collective-permute-start.2 = (f32[256,512]{1,0:T(8,128)}, f32[256,512]{1,0:T(8,128)S(1)}, u32[]{:S(2)}, u32[]{:S(2)}) collective-permute-start(f32[256,512]{1,0:T(8,128)} %get-tuple-element.2671), channel_id=1, source_target_pairs={{8,0},{16,8},{24,16},{32,24},{40,32},{48,40},{56,48},{64,56},{72,6... | collective-permute-start | bytes 1572872 | tf_op jit(solution)/shard_map/while/body/eval_jaxpr/ppermute | solution.py:36
  884.4 17.4 %collective-permute-start.3 = (f32[256,512]{1,0:T(8,128)}, f32[256,512]{1,0:T(8,128)S(1)}, u32[]{:S(2)}, u32[]{:S(2)}) collective-permute-start(f32[256,512]{1,0:T(8,128)} %get-tuple-element.2672), channel_id=1, source_target_pairs={{8,0},{16,8},{24,16},{32,24},{40,32},{48,40},{56,48},{64,56},{72,6... | collective-permute-start | bytes 1572872 | tf_op jit(solution)/shard_map/while/body/eval_jaxpr/ppermute | solution.py:36
  885.7 26.6 %collective-permute-start.2 = (f32[256,512]{1,0:T(8,128)}, f32[256,512]{1,0:T(8,128)S(1)}, u32[]{:S(2)}, u32[]{:S(2)}) collective-permute-start(f32[256,512]{1,0:T(8,128)} %get-tuple-element.2671), channel_id=1, source_target_pairs={{8,0},{16,8},{24,16},{32,24},{40,32},{48,40},{56,48},{64,56},{72,6... | collective-permute-start | bytes 1572872 | tf_op jit(solution)/shard_map/while/body/eval_jaxpr/ppermute | solution.py:36
  915.5 18.4 %collective-permute-start.2 = (f32[256,512]{1,0:T(8,128)}, f32[256,512]{1,0:T(8,128)S(1)}, u32[]{:S(2)}, u32[]{:S(2)}) collective-permute-start(f32[256,512]{1,0:T(8,128)} %get-tuple-element.2671), channel_id=1, source_target_pairs={{8,0},{16,8},{24,16},{32,24},{40,32},{48,40},{56,48},{64,56},{72,6... | collective-permute-start | bytes 1572872 | tf_op jit(solution)/shard_map/while/body/eval_jaxpr/ppermute | solution.py:36
  935.8 11.0 collective-permute-start.3
  937.1 17.1 %collective-permute-start.2 = (f32[256,512]{1,0:T(8,128)}, f32[256,512]{1,0:T(8,128)S(1)}, u32[]{:S(2)}, u32[]{:S(2)}) collective-permute-start(f32[256,512]{1,0:T(8,128)} %get-tuple-element.2671), channel_id=1, source_target_pairs={{8,0},{16,8},{24,16},{32,24},{40,32},{48,40},{56,48},{64,56},{72,6... | collective-permute-start | bytes 1572872 | tf_op jit(solution)/shard_map/while/body/eval_jaxpr/ppermute | solution.py:36
  956.1 13.2 collective-permute-start.3
  957.4 17.5 %collective-permute-start.2 = (f32[256,512]{1,0:T(8,128)}, f32[256,512]{1,0:T(8,128)S(1)}, u32[]{:S(2)}, u32[]{:S(2)}) collective-permute-start(f32[256,512]{1,0:T(8,128)} %get-tuple-element.2671), channel_id=1, source_target_pairs={{8,0},{16,8},{24,16},{32,24},{40,32},{48,40},{56,48},{64,56},{72,6... | collective-permute-start | bytes 1572872 | tf_op jit(solution)/shard_map/while/body/eval_jaxpr/ppermute | solution.py:36
  976.8 49.7 %collective-permute-start.3 = (f32[256,512]{1,0:T(8,128)}, f32[256,512]{1,0:T(8,128)S(1)}, u32[]{:S(2)}, u32[]{:S(2)}) collective-permute-start(f32[256,512]{1,0:T(8,128)} %get-tuple-element.2672), channel_id=1, source_target_pairs={{8,0},{16,8},{24,16},{32,24},{40,32},{48,40},{56,48},{64,56},{72,6... | collective-permute-start | bytes 1572872 | tf_op jit(solution)/shard_map/while/body/eval_jaxpr/ppermute | solution.py:36
  978.1 59.7 %collective-permute-start.2 = (f32[256,512]{1,0:T(8,128)}, f32[256,512]{1,0:T(8,128)S(1)}, u32[]{:S(2)}, u32[]{:S(2)}) collective-permute-start(f32[256,512]{1,0:T(8,128)} %get-tuple-element.2671), channel_id=1, source_target_pairs={{8,0},{16,8},{24,16},{32,24},{40,32},{48,40},{56,48},{64,56},{72,6... | collective-permute-start | bytes 1572872 | tf_op jit(solution)/shard_map/while/body/eval_jaxpr/ppermute | solution.py:36
  1039.6 15.8 collective-permute-start.3
  1040.9 25.8 %collective-permute-start.2 = (f32[256,512]{1,0:T(8,128)}, f32[256,512]{1,0:T(8,128)S(1)}, u32[]{:S(2)}, u32[]{:S(2)}) collective-permute-start(f32[256,512]{1,0:T(8,128)} %get-tuple-element.2671), channel_id=1, source_target_pairs={{8,0},{16,8},{24,16},{32,24},{40,32},{48,40},{56,48},{64,56},{72,6... | collective-permute-start | bytes 1572872 | tf_op jit(solution)/shard_map/while/body/eval_jaxpr/ppermute | solution.py:36
  1068.6 11.2 collective-permute-start.3
  1069.9 21.1 %collective-permute-start.2 = (f32[256,512]{1,0:T(8,128)}, f32[256,512]{1,0:T(8,128)S(1)}, u32[]{:S(2)}, u32[]{:S(2)}) collective-permute-start(f32[256,512]{1,0:T(8,128)} %get-tuple-element.2671), channel_id=1, source_target_pairs={{8,0},{16,8},{24,16},{32,24},{40,32},{48,40},{56,48},{64,56},{72,6... | collective-permute-start | bytes 1572872 | tf_op jit(solution)/shard_map/while/body/eval_jaxpr/ppermute | solution.py:36
  1092.9 13.9 collective-permute-start.3
  1094.2 24.1 %collective-permute-start.2 = (f32[256,512]{1,0:T(8,128)}, f32[256,512]{1,0:T(8,128)S(1)}, u32[]{:S(2)}, u32[]{:S(2)}) collective-permute-start(f32[256,512]{1,0:T(8,128)} %get-tuple-element.2671), channel_id=1, source_target_pairs={{8,0},{16,8},{24,16},{32,24},{40,32},{48,40},{56,48},{64,56},{72,6... | collective-permute-start | bytes 1572872 | tf_op jit(solution)/shard_map/while/body/eval_jaxpr/ppermute | solution.py:36
  1121.5 19.7 %collective-permute-start.2 = (f32[256,512]{1,0:T(8,128)}, f32[256,512]{1,0:T(8,128)S(1)}, u32[]{:S(2)}, u32[]{:S(2)}) collective-permute-start(f32[256,512]{1,0:T(8,128)} %get-tuple-element.2671), channel_id=1, source_target_pairs={{8,0},{16,8},{24,16},{32,24},{40,32},{48,40},{56,48},{64,56},{72,6... | collective-permute-start | bytes 1572872 | tf_op jit(solution)/shard_map/while/body/eval_jaxpr/ppermute | solution.py:36
  1143.1 10.5 collective-permute-start.3
  1144.4 18.8 %collective-permute-start.2 = (f32[256,512]{1,0:T(8,128)}, f32[256,512]{1,0:T(8,128)S(1)}, u32[]{:S(2)}, u32[]{:S(2)}) collective-permute-start(f32[256,512]{1,0:T(8,128)} %get-tuple-element.2671), channel_id=1, source_target_pairs={{8,0},{16,8},{24,16},{32,24},{40,32},{48,40},{56,48},{64,56},{72,6... | collective-permute-start | bytes 1572872 | tf_op jit(solution)/shard_map/while/body/eval_jaxpr/ppermute | solution.py:36
  1165.1 11.0 collective-permute-start.3
  1166.4 18.8 %collective-permute-start.2 = (f32[256,512]{1,0:T(8,128)}, f32[256,512]{1,0:T(8,128)S(1)}, u32[]{:S(2)}, u32[]{:S(2)}) collective-permute-start(f32[256,512]{1,0:T(8,128)} %get-tuple-element.2671), channel_id=1, source_target_pairs={{8,0},{16,8},{24,16},{32,24},{40,32},{48,40},{56,48},{64,56},{72,6... | collective-permute-start | bytes 1572872 | tf_op jit(solution)/shard_map/while/body/eval_jaxpr/ppermute | solution.py:36
  1187.1 20.1 %collective-permute-start.3 = (f32[256,512]{1,0:T(8,128)}, f32[256,512]{1,0:T(8,128)S(1)}, u32[]{:S(2)}, u32[]{:S(2)}) collective-permute-start(f32[256,512]{1,0:T(8,128)} %get-tuple-element.2672), channel_id=1, source_target_pairs={{8,0},{16,8},{24,16},{32,24},{40,32},{48,40},{56,48},{64,56},{72,6... | collective-permute-start | bytes 1572872 | tf_op jit(solution)/shard_map/while/body/eval_jaxpr/ppermute | solution.py:36
  1188.4 27.7 %collective-permute-start.2 = (f32[256,512]{1,0:T(8,128)}, f32[256,512]{1,0:T(8,128)S(1)}, u32[]{:S(2)}, u32[]{:S(2)}) collective-permute-start(f32[256,512]{1,0:T(8,128)} %get-tuple-element.2671), channel_id=1, source_target_pairs={{8,0},{16,8},{24,16},{32,24},{40,32},{48,40},{56,48},{64,56},{72,6... | collective-permute-start | bytes 1572872 | tf_op jit(solution)/shard_map/while/body/eval_jaxpr/ppermute | solution.py:36
  (59 other events, 2577.9 us)
Sparse Core Ops, SparseCore 0:
  22.3 143.6 all-gather.12
  215.5 367.0 all-gather.14
where the time goes:
time: 1670 us; the launch traced here: 1650 us
  waiting for transfers between devices  446 us (27%)
  starting transfers between devices  361 us (22%)
  blocking collectives  245 us (15%)
  other arithmetic  202 us (12%)
  loops' own time  157 us (9%)
  local copies, waits for them, and re-layouts  125 us (7%)
  matrix products  101 us (6%)
    ppermute x64, waiting for transfers between devices, shifted(): return lax.ppermute(shard, axis, pairs)  382 us
    ppermute x64, starting transfers between devices, shifted(): return lax.ppermute(shard, axis, pairs)  361 us
    unnamed x2, blocking collectives  148 us
    another operation x2, loops' own time, entering(): return lax.fori_loop(0, ahead, one, state)  102 us
    psum x1, blocking collectives, body(): write_sum, read_sum = lax.psum((write_part, read_part), 'head')  83.9 us
    all_gather x2, waiting for transfers between devices, entering(): gathered = jax.tree.map(lambda a: lax.all_gather(a, axis), part)  63.9 us
    select_n x31, other arithmetic, link(): state = jnp.where(late_vacant_state > 0.5, early_state, carried)  56.8 us
  transfers between devices with their start and end apart: 66, of which 51 were waited for; matrix products, arithmetic and copies ran while one was open for 16% of the time, Pallas kernels for 0%

commit v1 on v0

v1 whole, which is shorter than its diff:
```python
import functools
import math

import jax
import jax.numpy as jnp
from jax import lax
from jax.experimental import pallas as pl
from jax.experimental.pallas import tpu as pltpu
from jax.sharding import PartitionSpec as P

DIM = 128
WINDOW = 4096
EPSILON = 1e-05
ROW = 8
QUAD = 4
TQ = 256
TK = 512
HIDDEN = -1e30
F32 = jnp.float32
BF16 = jnp.bfloat16
EXACT = lax.Precision.HIGHEST
SCALE = DIM**-0.5
SCALE2 = SCALE * math.log2(math.e)
VMEM_LIMIT = 60 * 2**20


def dot(a, b, precision=None):
    return jnp.dot(a, b, preferred_element_type=F32, precision=precision)


def dot_nt(a, b):
    return lax.dot_general(a, b, (((1,), (1,)), ((), ())), preferred_element_type=F32)


def dot_tn(a, b):
    return lax.dot_general(a, b, (((0,), (0,)), ((), ())), preferred_element_type=F32)


def call(kernel, outs, *args, flops, smem=0, scratch=()):
    specs = [pl.BlockSpec(memory_space=pltpu.SMEM)] * smem
    specs += [pl.BlockSpec(memory_space=pltpu.VMEM)] * (len(args) - smem)
    moved = sum(math.prod(a.shape) * a.dtype.itemsize for a in (*args, *outs))
    return pl.pallas_call(
        kernel,
        out_shape=outs,
        in_specs=specs,
        out_specs=tuple(pl.BlockSpec(memory_space=pltpu.VMEM) for _ in outs),
        scratch_shapes=list(scratch),
        compiler_params=pltpu.CompilerParams(vmem_limit_bytes=VMEM_LIMIT),
        cost_estimate=pl.CostEstimate(flops=flops, bytes_accessed=moved, transcendentals=0),
    )(*args)


def shape(dims, dtype):
    return jax.ShapeDtypeStruct(dims, dtype)


def attention_kernel(edge_ref, bound_ref, qg_ref, kv_ref, og_ref, dkv_ref, kvt, acc):
    step = pl.program_id(0)
    keys = kv_ref.shape[0]

    @pl.when(step == 0)
    def _():
        acc[...] = jnp.zeros_like(acc)

        @pl.loop(0, keys // TK)
        def _(t):
            rows = pl.ds(pl.multiple_of(t * TK, TK), TK)
            kvt[:, rows] = kv_ref[rows, :].T

    lo_first, lo_last = edge_ref[3 * step], edge_ref[3 * step + 1]
    hi_first = edge_ref[3 * step + 2]
    hi_last = hi_first + TQ - 1
    first = lo_first // TK
    last = hi_last // TK + 1
    open_first = jnp.clip((lo_last + TK - 1) // TK, first, last)
    open_last = jnp.clip((hi_first + 1) // TK, open_first, last)

    lo, hi = bound_ref[0:1, :], bound_ref[1:2, :]
    q, g = qg_ref[:, :DIM], qg_ref[:, DIM:]
    qt, gt = q.T, g.T

    def scores(t, masked):
        rows = pl.ds(pl.multiple_of(t * TK, TK), TK)
        s = dot(kv_ref[rows, :DIM], qt)
        if masked:
            at = t * TK + lax.broadcasted_iota(jnp.int32, (TK, TQ), 0)
            s = jnp.where((at >= lo) & (at <= hi), s, HIDDEN)
        return rows, s

    def forward(masked, t, state):
        top, total, out = state
        rows, s = scores(t, masked)
        new = jnp.maximum(top, jnp.max(s, axis=0, keepdims=True))
        p = jnp.exp2((s - new) * SCALE2)
        keep = jnp.exp2((top - new) * SCALE2)
        total = total * keep + jnp.sum(p, axis=0, keepdims=True)
        out = out * keep + dot(kvt[DIM:, rows], p.astype(BF16))
        return new, total, out

    def segments(one, state):
        state = lax.fori_loop(first, open_first, functools.partial(one, True), state)
        state = lax.fori_loop(open_first, open_last, functools.partial(one, False), state)
        return lax.fori_loop(open_last, last, functools.partial(one, True), state)

    top, total, out = segments(
        forward,
        (
            jnp.full((1, TQ), HIDDEN, F32),
            jnp.zeros((1, TQ), F32),
            jnp.zeros((DIM, TQ), F32),
        ),
    )
    out = out / total
    delta = jnp.sum(gt.astype(F32) * out, axis=0, keepdims=True)
    level = top * SCALE2 + jnp.log2(total)

    def backward(masked, t, dqt):
        rows, s = scores(t, masked)
        p = jnp.exp2(s * SCALE2 - level)
        dp = dot(kv_ref[rows, DIM:], gt)
        ds = (p * (dp - delta) * SCALE).astype(BF16)
        acc[rows, :DIM] += dot(ds, q)
        acc[rows, DIM:] += dot(p.astype(BF16), g)
        return dqt + dot(kvt[:DIM, rows], ds)

    dqt = segments(backward, jnp.zeros((DIM, TQ), F32))
    og_ref[:, :DIM] = out.T.astype(BF16)
    og_ref[:, DIM:] = dqt.T.astype(BF16)

    @pl.when(step == pl.num_programs(0) - 1)
    def _():
        @pl.loop(0, keys // TK)
        def _(t):
            rows = pl.ds(pl.multiple_of(t * TK, TK), TK)
            dkv_ref[rows, :] = acc[rows, :].astype(BF16)


def attention(edges, bounds, qg, kv):
    queries, keys = qg.shape[0], kv.shape[0]
    return pl.pallas_call(
        attention_kernel,
        out_shape=(shape((queries, 2 * DIM), BF16), shape((keys, 2 * DIM), BF16)),
        grid=(queries // TQ,),
        in_specs=[
            pl.BlockSpec(memory_space=pltpu.SMEM),
            pl.BlockSpec((2, TQ), lambda i: (0, i)),
            pl.BlockSpec((TQ, 2 * DIM), lambda i: (i, 0)),
            pl.BlockSpec((keys, 2 * DIM), lambda i: (0, 0), pipeline_mode=pl.Buffered(1)),
        ],
        out_specs=(
            pl.BlockSpec((TQ, 2 * DIM), lambda i: (i, 0)),
            pl.BlockSpec((keys, 2 * DIM), lambda i: (0, 0), pipeline_mode=pl.Buffered(1)),
        ),
        scratch_shapes=[
            pltpu.VMEM((2 * DIM, keys), BF16),
            pltpu.VMEM((keys, 2 * DIM), F32),
        ],
        compiler_params=pltpu.CompilerParams(
            dimension_semantics=("arbitrary",), vmem_limit_bytes=VMEM_LIMIT
        ),
        cost_estimate=pl.CostEstimate(
            flops=14 * queries * 4096 * DIM, bytes_accessed=4 * keys * DIM * 4, transcendentals=0
        ),
    )(edges, bounds, qg, kv)


def cumulate_kernel(rate_ref, rate_t_ref, doc_ref, x_ref, write_ref, cum_ref, cum_t_ref, state_ref):
    length, heads = rate_ref.shape
    row = lax.broadcasted_iota(jnp.int32, (length, length), 0)
    col = lax.broadcasted_iota(jnp.int32, (length, length), 1)
    cum = dot((row >= col).astype(F32), rate_ref[...], EXACT)
    cum_ref[...] = cum
    cum_t_ref[...] = dot(rate_t_ref[...], (row <= col).astype(F32), EXACT)
    tail = tail_decay(cum, doc_ref[...])
    write = write_ref[...]
    for h in range(heads):
        cols = slice(h * DIM, (h + 1) * DIM)
        scaled = (x_ref[:, cols].astype(F32) * tail[:, h : h + 1]).astype(BF16)
        state_ref[h] = dot_tn(write, scaled).astype(BF16)


def tail_decay(cum, doc):
    length = cum.shape[0]
    same = doc == doc[length - 1 : length, :]
    return jnp.where(same, jnp.exp(cum[length - 1 : length, :] - cum), 0.0)


def head_decay(cum, cum_t, seen, h):
    return jnp.exp(jnp.where(seen, cum[:, h : h + 1] - cum_t[h : h + 1, :], HIDDEN))


def visible(doc, start):
    length = doc.shape[0]
    row = lax.broadcasted_iota(jnp.int32, (length, length), 0)
    col = lax.broadcasted_iota(jnp.int32, (length, length), 1)
    return (row >= col) & (start + col >= doc)


def local_kernel(at_ref, cum_ref, cum_t_ref, doc_ref, x_ref, read_ref, write_ref, mixed_ref):
    cum, cum_t = cum_ref[...], cum_t_ref[...]
    seen = visible(doc_ref[...], at_ref[0])
    scores = dot_nt(read_ref[...], write_ref[...])
    for h in range(cum.shape[1]):
        cols = slice(h * DIM, (h + 1) * DIM)
        mix = (head_decay(cum, cum_t, seen, h) * scores).astype(BF16)
        mixed_ref[:, cols] = dot(mix, x_ref[:, cols])


def link_kernel(transposed, total_ref, doc_ref, part_ref, out_ref):
    n = part_ref.shape[0]
    row = lax.broadcasted_iota(jnp.int32, (n, n), 0)
    col = lax.broadcasted_iota(jnp.int32, (n, n), 1)
    late, early = (col, row) if transposed else (row, col)
    spread = jnp.zeros((n, n), F32)
    mark = jnp.zeros((n, n), jnp.int32)
    for k in range(n):
        spread += jnp.where((early < k) & (k < late), total_ref[k], 0.0)
        mark = jnp.where(late == k + 1, doc_ref[k], mark)
    joined = (late > early) & (mark < TQ * (early + 1))
    weight = jnp.exp(jnp.where(joined, spread, HIDDEN))
    out_ref[...] = dot(weight, part_ref[...].astype(F32), EXACT).astype(BF16)


def gate_terms(gate):
    sigma = jax.nn.sigmoid(gate)
    return sigma, gate * sigma


def mix_kernel(at_ref, cum_ref, doc_ref, local_ref, read_ref, prior_ref, gate_ref, grad_ref, mixed_ref, sums_ref):
    enter = jnp.where(doc_ref[...] < at_ref[0], jnp.exp(cum_ref[...]), 0.0)
    read = read_ref[...]
    length = read.shape[0]
    squares = jnp.zeros((length, 1), F32)
    inner = jnp.zeros((length, 1), F32)
    for h in range(enter.shape[1]):
        cols = slice(h * DIM, (h + 1) * DIM)
        mixed = local_ref[:, cols] + enter[:, h : h + 1] * dot(read, prior_ref[h])
        mixed_ref[:, cols] = mixed
        gated = mixed * gate_terms(gate_ref[:, cols].astype(F32))[1]
        squares += jnp.sum(gated * gated, axis=1, keepdims=True)
        inner += jnp.sum(grad_ref[:, cols].astype(F32) * gated, axis=1, keepdims=True)
    sums_ref[:, 0:1] = squares
    sums_ref[:, 1:2] = inner


def norm_kernel(width, at_ref, cum_ref, doc_ref, sums_ref, mixed_ref, read_ref, gate_ref, grad_ref,
                out_ref, gate_grad_ref, dmixed_ref, state_ref):
    enter = jnp.where(doc_ref[...] < at_ref[0], jnp.exp(cum_ref[...]), 0.0)
    rms = lax.rsqrt(sums_ref[:, 0:1] / width + EPSILON)
    pull = rms * rms * rms * sums_ref[:, 1:2] / width
    read = read_ref[...]
    for h in range(enter.shape[1]):
        cols = slice(h * DIM, (h + 1) * DIM)
        mixed = mixed_ref[:, cols]
        gate = gate_ref[:, cols].astype(F32)
        sigma, swish = gate_terms(gate)
        gated = mixed * swish
        out_ref[:, cols] = (gated * rms).astype(BF16)
        dgated = rms * grad_ref[:, cols].astype(F32) - pull * gated
        dmixed = dgated * swish
        dmixed_ref[:, cols] = dmixed.astype(BF16)
        gate_grad_ref[:, cols] = (dgated * mixed * sigma * (1.0 + gate * (1.0 - sigma))).astype(BF16)
        state_ref[h] = dot_tn(read, (enter[:, h : h + 1] * dmixed).astype(BF16)).astype(BF16)


def adjoint_kernel(at_ref, cum_ref, cum_t_ref, doc_ref, x_ref, dmixed_ref, read_ref, write_ref, prior_ref,
                   input_ref, maps_ref):
    cum, cum_t = cum_ref[...], cum_t_ref[...]
    doc = doc_ref[...]
    seen = visible(doc, at_ref[0])
    enter = jnp.where(doc < at_ref[0], jnp.exp(cum), 0.0)
    read, write = read_ref[...], write_ref[...]
    scores = dot_nt(read, write)
    pairs = jnp.zeros_like(scores)
    read_part = jnp.zeros(read.shape, F32)
    for h in range(cum.shape[1]):
        cols = slice(h * DIM, (h + 1) * DIM)
        decay = head_decay(cum, cum_t, seen, h)
        dmixed = dmixed_ref[:, cols]
        input_ref[:, cols] = dot_tn((decay * scores).astype(BF16), dmixed)
        pairs += decay * dot_nt(dmixed, x_ref[:, cols])
        entered = (enter[:, h : h + 1] * dmixed.astype(F32)).astype(BF16)
        read_part += dot_nt(entered, prior_ref[h])
    pairs = pairs.astype(BF16)
    maps_ref[:, :DIM] = dot_tn(pairs, read)
    maps_ref[:, DIM:] = read_part + dot(pairs, write)


def finish_kernel(cum_ref, doc_ref, x_ref, write_ref, after_ref, input_ref, maps_ref, input_grad_ref, out_ref):
    tail = tail_decay(cum_ref[...], doc_ref[...])
    write = write_ref[...]
    write_part = maps_ref[:, :DIM]
    for h in range(tail.shape[1]):
        cols = slice(h * DIM, (h + 1) * DIM)
        t = tail[:, h : h + 1]
        after = after_ref[h]
        input_grad_ref[:, cols] = (input_ref[:, cols] + t * dot(write, after)).astype(BF16)
        write_part += dot_nt((x_ref[:, cols].astype(F32) * t).astype(BF16), after)
    out_ref[:, :DIM] = write_part
    out_ref[:, DIM:] = maps_ref[:, DIM:]


def by_head(a, b):
    length, width = a.shape
    both = [t.reshape(length, width // DIM, DIM).transpose(1, 0, 2) for t in (a, b)]
    return jnp.concatenate(both, axis=2)


def by_token(pair, half):
    part = pair[:, :, half * DIM : (half + 1) * DIM]
    return part.transpose(1, 0, 2).reshape(part.shape[1], -1)


def body(
    ssm_input,
    gate_input,
    write_map,
    read_map,
    log_decay,
    doc_start,
    ssm_grad,
    att_queries,
    att_keys,
    att_values,
    att_grad,
):
    n = lax.axis_size("ctx")
    me = lax.axis_index("ctx")
    length, width = ssm_input.shape
    heads = width // DIM
    width_all = width * lax.axis_size("head")
    rows = [list(range(i, i + ROW)) for i in range(0, n, ROW)]
    quads = [list(range(i, i + QUAD)) for i in range(0, n, QUAD)]

    facts = jnp.concatenate([doc_start.astype(F32), jnp.sum(log_decay, axis=0)])
    facts = lax.all_gather(facts, "ctx")
    doc_all = facts[:, :length].astype(jnp.int32)
    total_all = facts[:, length:]
    share = n // heads
    totals = lax.dynamic_index_in_dim(total_all, me // share, 1, False)
    last_doc = doc_all[:, length - 1]

    start = (me * length).astype(jnp.int32).reshape(1)
    doc_col = doc_start.reshape(length, 1)
    cum, cum_t, state = call(
        cumulate_kernel,
        (shape((length, heads), F32), shape((heads, length), F32), shape((heads, DIM, DIM), BF16)),
        log_decay, log_decay.T, doc_col, ssm_input, write_map,
        flops=2 * length * DIM * width,
    )

    def exchange(state, transposed):
        parts = lax.all_to_all(state.reshape(n, -1), "ctx", 0, 0)
        (linked,) = call(
            functools.partial(link_kernel, transposed),
            (shape(parts.shape, BF16),),
            totals, last_doc, parts,
            flops=12 * n * n * parts.shape[1], smem=2,
        )
        return lax.all_to_all(linked, "ctx", 0, 0).reshape(heads, DIM, DIM)

    kv = by_head(att_keys, att_values)
    kv_row = lax.all_to_all(jnp.concatenate([kv, kv], axis=0), "ctx", 0, 0, axis_index_groups=rows)
    kv_row = kv_row.reshape(ROW * length, 2 * DIM)
    qg = lax.all_to_all(by_head(att_queries, att_grad), "ctx", 0, 0, axis_index_groups=quads)
    qg = qg.reshape(QUAD * length, 2 * DIM)

    def rotate(a, by):
        return lax.ppermute(a, "ctx", [(i, (i + by) % n) for i in range(n)])

    kv_all = jnp.concatenate([rotate(kv_row, 2 * ROW), rotate(kv_row, ROW), kv_row], axis=0)

    prior = exchange(state, False)
    (local,) = call(
        local_kernel,
        (shape((length, width), F32),),
        start, cum, cum_t, doc_col, ssm_input, read_map, write_map,
        flops=2 * length * length * width, smem=1,
    )
    mixed, sums = call(
        mix_kernel,
        (shape((length, width), F32), shape((length, 2), F32)),
        start, cum, doc_col, local, read_map, prior, gate_input, ssm_grad,
        flops=2 * length * DIM * width, smem=1,
    )
    sums = lax.psum(sums.T, "head").T
    mixer_out, gate_grad, dmixed, back = call(
        functools.partial(norm_kernel, width_all),
        (shape((length, width), BF16), shape((length, width), BF16), shape((length, width), BF16),
         shape((heads, DIM, DIM), BF16)),
        start, cum, doc_col, sums, mixed, read_map, gate_input, ssm_grad,
        flops=2 * length * DIM * width, smem=1,
    )
    after = exchange(back, True)
    input_part, maps_part = call(
        adjoint_kernel,
        (shape((length, width), F32), shape((length, 2 * DIM), F32)),
        start, cum, cum_t, doc_col, ssm_input, dmixed, read_map, write_map, prior,
        flops=6 * length * length * width, smem=1,
    )

    quad = me // QUAD
    count = QUAD * length
    base = (me // ROW - 2) * (ROW * length)
    docs = lax.dynamic_slice_in_dim(doc_all.reshape(-1), quad * count, count)
    high = 2 * ROW * length + (quad % 2) * count + jnp.arange(count, dtype=jnp.int32)
    low = jnp.maximum(docs - base, high - (WINDOW - 1))
    tiles = count // TQ
    edges = jnp.stack([low[::TQ], low[TQ - 1 :: TQ], high[::TQ]], axis=1).reshape(3 * tiles)
    og, dkv = attention(edges, jnp.stack([low, high]), qg, kv_all)
    og = lax.all_to_all(og.reshape(QUAD, length, 2 * DIM), "ctx", 0, 0, axis_index_groups=quads)
    dkv = dkv.reshape(3, ROW * length, 2 * DIM)
    dkv_sum = (
        dkv[2].astype(F32)
        + rotate(dkv[1], -ROW).astype(F32)
        + rotate(dkv[0], -2 * ROW).astype(F32)
    ).astype(BF16)
    dkv_sum = lax.all_to_all(dkv_sum.reshape(ROW, length, 2 * DIM), "ctx", 0, 0, axis_index_groups=rows)
    dkv_sum = (dkv_sum[:QUAD].astype(F32) + dkv_sum[QUAD:].astype(F32)).astype(BF16)

    input_grad, maps = call(
        finish_kernel,
        (shape((length, width), BF16), shape((length, 2 * DIM), F32)),
        cum, doc_col, ssm_input, write_map, after, input_part, maps_part,
        flops=4 * length * DIM * width,
    )
    maps = lax.psum(maps, "head").astype(BF16)
    return (
        mixer_out,
        by_token(og, 0),
        input_grad,
        gate_grad,
        maps[:, :DIM],
        maps[:, DIM:],
        by_token(og, 1),
        by_token(dkv_sum, 0),
        by_token(dkv_sum, 1),
    )


def solution(mesh):
    tokens, both = P("ctx", None), P("ctx", "head")
    in_specs = (both, both, tokens, tokens, both, P("ctx"), both, both, both, both, both)
    out_specs = (both, both, both, both, tokens, tokens, both, both, both)
    return jax.shard_map(body, mesh=mesh, in_specs=in_specs, out_specs=out_specs, check_vma=False)
```

time: 1670 us -> 438 us (0.26)
  the two profiles are of different devices: /device:TPU:1 before, /device:TPU:2 now
where the time goes in v1:
time: 438 us; the launch traced here: 437 us
  blocking collectives  229 us (52%)
  starting transfers between devices  82.3 us (19%)
  Pallas kernels  43.1 us (10%)
  waiting for transfers between devices  34.4 us (8%)
  local copies, waits for them, and re-layouts  26.6 us (6%)
  other arithmetic  19.8 us (5%)
    unnamed x1, blocking collectives  131 us
    all_to_all x1, blocking collectives, exchange(): return lax.all_to_all(linked, 'ctx', 0, 0).reshape(heads, DIM, DIM)  39.8 us
    ppermute x4, starting transfers between devices, rotate(): return lax.ppermute(a, 'ctx', [(i, (i + by) % n) for i in range(n)])  33.7 us
    psum x1, blocking collectives, body(): maps = lax.psum(maps, 'head').astype(BF16)  32.4 us
    psum x1, blocking collectives, body(): sums = lax.psum(sums.T, 'head').T  25.9 us
    pallas_call x8, Pallas kernels, call(): pl.pallas_call(kernel, out_shape=outs, in_specs=specs, out_specs=tuple((p...  25.2 us
    pallas_call x1, Pallas kernels, attention(): pl.pallas_call(attention_kernel, out_shape=(shape((queries, 2 * DIM), BF1...  17.9 us
    all_to_all x1, waiting for transfers between devices, body(): lax.all_to_all(jnp.concatenate([kv, kv], axis=0), 'ctx', 0, 0, axis_index...  17.3 us
  transfers between devices with their start and end apart: 11, of which 3 were waited for; matrix products, arithmetic and copies ran while one was open for 9% of the time, Pallas kernels for 10%

profile of v1, /device:TPU:2, one launch (start us, length us, event | category | flops | bytes accessed | tf_op | source)
XLA Modules:
  0.0 436.5 jit_solution(18322509158580204631)
XLA Ops:
  0.7 0.9 copy-done
  1.6 1.0 bitcast_bitcast_fusion
  2.7 1.0 maximum_maximum_fusion
  3.7 8.5 %all-to-all-start.3 = ((bf16[8,256,256]{2,1,0:T(8,128)(2,1)}), bf16[8,256,256]{2,1,0:T(8,128)(2,1)S(1)}, u32[]{:S(2)}, u32[]{:S(2)}) async-start(bf16[8,256,256]{2,1,0:T(8,128)(2,1)} %maximum_maximum_fusion), calls=%async_computation.3 | async-start | bytes 2097152 | tf_op jit(solution)/shard_map/all_to_all | solution.py:364
  12.2 0.8 copy.82.rate_ref
  13.1 0.8 copy.83.doc_ref
  13.9 2.9 shard_map.178
  16.8 1.9 all_to_all.52
  18.8 0.5 broadcast.20
  19.3 2.2 reduce.6
  21.5 0.9 reshape.128
  22.4 0.6 dynamic-slice
  23.6 17.3 %all-to-all-done.3 = bf16[8,256,256]{2,1,0:T(8,128)(2,1)S(1)} async-done(((bf16[8,256,256]{2,1,0:T(8,128)(2,1)}), bf16[8,256,256]{2,1,0:T(8,128)(2,1)S(1)}, u32[]{:S(2)}, u32[]{:S(2)}) %all-to-all-start.3) | async-done | bytes 1048608 | tf_op jit(solution)/shard_map/all_to_all | solution.py:364
  40.9 5.0 %all-to-all-start = ((bf16[32,2,2048]{2,1,0:T(2,128)(2,1)}), bf16[32,2,2048]{2,1,0:T(2,128)(2,1)S(1)}, u32[]{:S(2)}, u32[]{:S(2)}) async-start(bf16[32,2,2048]{2,1,0:T(2,128)(2,1)} %reshape.128), calls=%async_computation | async-start | bytes 524288 | tf_op jit(solution)/shard_map/all_to_all | solution.py:354
  46.0 130.5 %all-reduce = f32[8448]{0:T(1024)S(1)} all-reduce(f32[8448]{0:T(1024)S(1)} %maximum_dynamic-update-slice_fusion), channel_id=2, replica_groups=mesh['ctx'=32,'head'=8] {'ctx'}, use_global_device_ids=true, to_apply=%add | all-reduce | flops 8448 | bytes 67584
  176.7 1.0 collective-permute-start
  177.6 13.6 %collective-permute-start.1 = (bf16[2048,256]{1,0:T(8,128)(2,1)S(1)}, bf16[2048,256]{1,0:T(8,128)(2,1)}, u32[]{:S(2)}, u32[]{:S(2)}) collective-permute-start(bf16[2048,256]{1,0:T(8,128)(2,1)S(1)} %bitcast.76), channel_id=1, source_target_pairs={{0,64},{8,72},{16,80},{24,88},{32,96},{40,104},{48,112},{56,120},{... | collective-permute-start | bytes 3145736 | tf_op jit(solution)/shard_map/ppermute | solution.py:370
  191.3 0.8 dynamic-slice_reduce_fusion.total_ref
  192.1 0.7 slice_reduce_fusion.doc_ref
  192.8 0.3 reshape.129
  193.1 1.0 copy.128
  194.1 2.3 shard_map.180
  196.3 1.7 reduce.7
  198.1 0.9 reshape.130
  198.9 3.7 all-to-all-start.1
  202.9 0.6 pad_add_fusion.bound_ref
  203.5 1.0 bitcast_bitcast_fusion.2
  204.6 0.9 pad_maximum_fusion.1
  205.5 9.7 %all-to-all-done.1 = bf16[32,2,2048]{2,1,0:T(2,128)(2,1)S(1)} async-done(((bf16[32,2,2048]{2,1,0:T(2,128)(2,1)}), bf16[32,2,2048]{2,1,0:T(2,128)(2,1)S(1)}, u32[]{:S(2)}, u32[]{:S(2)}) %all-to-all-start.1) | async-done | bytes 262176 | tf_op jit(solution)/shard_map/all_to_all | solution.py:361
  215.2 4.3 all-to-all-start.2
  219.6 0.7 reshape.104.edge_ref
  220.2 2.8 shard_map.179.local_ref
  223.3 1.5 reduce.2
  224.8 0.8 reshape.102.prior_ref
  225.7 4.2 shard_map.181
  229.8 25.9 %psum.14.sums_ref = f32[256,2]{1,0:T(8,128)} all-reduce(f32[256,2]{1,0:T(8,128)} %get-tuple-element.27), channel_id=1, replica_groups=mesh['ctx'=32,'head'=8] {'head'}, use_global_device_ids=true, to_apply=%region_1.2 | all-reduce | flops 512 | bytes 4096 | tf_op jit(solution)/shard_map/psum | solution.py:387
  255.8 3.9 shard_map.182
  259.7 1.9 all_to_all.53
  261.6 2.2 reduce.8
  263.8 0.9 reshape.132
  264.7 2.8 pad_maximum_fusion.kv_ref
  267.5 8.6 %all-to-all-start.5 = ((bf16[32,2,2048]{2,1,0:T(2,128)(2,1)}), bf16[32,2,2048]{2,1,0:T(2,128)(2,1)S(1)}, u32[]{:S(2)}, u32[]{:S(2)}) async-start(bf16[32,2,2048]{2,1,0:T(2,128)(2,1)} %reshape.132), calls=%async_computation.5 | async-start | bytes 524288 | tf_op jit(solution)/shard_map/all_to_all | solution.py:354
  276.1 17.9 %shard_map.183 = (bf16[1024,256]{1,0:T(8,128)(2,1)}, bf16[6144,256]{1,0:T(8,128)(2,1)}) custom-call(s32[12]{0:T(128)} %reshape.104.edge_ref, s32[2,1024]{1,0:T(2,128)} %pad_add_fusion.bound_ref, bf16[1024,256]{1,0:T(8,128)(2,1)} %bitcast.11.qg_ref, bf16[6144,256]{1,0:T(8,128)(2,1)} %pad_maximum_fusion.kv_ref), custom_call_target="tpu_custom_call" | custom-call | flops 7516192768 | bytes 12582912 | tf_op jit(solution)/shard_map/pallas_call | solution.py:141
  294.0 3.0 fusion.1
  297.0 19.2 %collective-permute-start.3 = (bf16[2048,256]{1,0:T(8,128)(2,1)}, bf16[2048,256]{1,0:T(8,128)(2,1)}, u32[]{:S(2)}, u32[]{:S(2)}) collective-permute-start(bf16[2048,256]{1,0:T(8,128)(2,1)} %get-tuple-element.40), channel_id=1, source_target_pairs={{0,128},{8,136},{16,144},{24,152},{32,160},{40,168},{48,176},{56,1... | collective-permute-start | bytes 3145736 | tf_op jit(solution)/shard_map/ppermute | solution.py:370
  316.2 0.3 reshape.133
  316.4 1.0 copy.127
  317.4 2.3 shard_map.184
  319.7 1.7 reduce.9
  321.6 39.8 %all_to_all.62 = bf16[32,2,2048]{2,1,0:T(2,128)(2,1)S(1)} all-to-all(bf16[32,2,2048]{2,1,0:T(2,128)(2,1)S(1)} %reshape.134), channel_id=1, replica_groups=mesh['ctx'=32,'head'=8] {'ctx'}, dimensions={0} | all-to-all | bytes 524288 | tf_op jit(solution)/shard_map/all_to_all | solution.py:361
  361.4 4.5 %all-to-all-start.4 = ((bf16[4,256,256]{2,1,0:T(8,128)(2,1)}), bf16[4,256,256]{2,1,0:T(8,128)(2,1)S(1)}, u32[]{:S(2)}, u32[]{:S(2)}) async-start(bf16[4,256,256]{2,1,0:T(8,128)(2,1)} %bitcast.15), calls=%async_computation.4 | async-start | bytes 1048576 | tf_op jit(solution)/shard_map/all_to_all | solution.py:412
  366.0 3.2 add_convert_fusion
  369.2 7.4 %all-to-all-done.4 = bf16[4,256,256]{2,1,0:T(8,128)(2,1)S(1)} async-done(((bf16[4,256,256]{2,1,0:T(8,128)(2,1)}), bf16[4,256,256]{2,1,0:T(8,128)(2,1)S(1)}, u32[]{:S(2)}, u32[]{:S(2)}) %all-to-all-start.4) | async-done | bytes 524320 | tf_op jit(solution)/shard_map/all_to_all | solution.py:412
  376.6 14.0 %all-to-all-start.7 = ((bf16[8,256,256]{2,1,0:T(8,128)(2,1)}), bf16[8,256,256]{2,1,0:T(8,128)(2,1)S(1)}, u32[]{:S(2)}, u32[]{:S(2)}) async-start(bf16[8,256,256]{2,1,0:T(8,128)(2,1)} %bitcast.19), calls=%async_computation.7 | async-start | bytes 2097152 | tf_op jit(solution)/shard_map/all_to_all | solution.py:419
  390.5 4.0 shard_map.185
  394.8 1.5 reduce.3
  396.4 0.8 reshape.113.after_ref
  397.2 3.0 shard_map.186
  400.1 32.4 %all-reduce.2 = bf16[256,256]{1,0:T(8,128)(2,1)S(1)} all-reduce(f32[256,256]{1,0:T(8,128)} %get-tuple-element.37), channel_id=1, replica_groups=mesh['ctx'=32,'head'=8] {'head'}, use_global_device_ids=true, to_apply=%region_2.3 | all-reduce | flops 65536 | bytes 393216 | tf_op jit(solution)/shard_map/psum | solution.py:428
  432.5 0.7 fusion.2
  433.3 0.7 copy.125
  434.0 0.7 copy.126
  435.0 0.7 copy.123
  435.8 0.7 copy.124
  (39 shorter events, 1.8 us)
Async XLA Ops:
  0.6 1.0 copy-start
  0.7 11.5 %copy-start.3 = (s32[256]{0:T(256)S(1)}, s32[256]{0:T(256)}, u32[]{:S(2)}) copy-start(s32[256]{0:T(256)} %param.16) | copy-start | bytes 3076
  0.7 11.5 %copy-start.2 = (f32[256,8]{0,1:T(8,128)S(1)}, f32[256,8]{0,1:T(8,128)}, u32[]{:S(2)}) copy-start(f32[256,8]{0,1:T(8,128)} %param.15) | copy-start | bytes 24580
  2.7 19.7 %copy-start.4 = (u32[256]{0:T(256)S(1)}, u32[256]{0:T(256)}, u32[]{:S(2)}) copy-start(u32[256]{0:T(256)} %constant.69) | copy-start | bytes 3076
  3.7 37.2 %all-to-all-start.3 = ((bf16[8,256,256]{2,1,0:T(8,128)(2,1)}), bf16[8,256,256]{2,1,0:T(8,128)(2,1)S(1)}, u32[]{:S(2)}, u32[]{:S(2)}) async-start(bf16[8,256,256]{2,1,0:T(8,128)(2,1)} %maximum_maximum_fusion), calls=%async_computation.3 | async-start | bytes 2097152 | tf_op jit(solution)/shard_map/all_to_all | solution.py:364
  18.8 184.8 %copy-start.1 = (bf16[256,512]{1,0:T(8,128)(2,1)S(1)}, bf16[256,512]{1,0:T(8,128)(2,1)}, u32[]{:S(2)}) copy-start(bf16[256,512]{1,0:T(8,128)(2,1)} %param.18) | copy-start | bytes 786436
  40.9 151.9 %all-to-all-start = ((bf16[32,2,2048]{2,1,0:T(2,128)(2,1)}), bf16[32,2,2048]{2,1,0:T(2,128)(2,1)S(1)}, u32[]{:S(2)}, u32[]{:S(2)}) async-start(bf16[32,2,2048]{2,1,0:T(2,128)(2,1)} %reshape.128), calls=%async_computation | async-start | bytes 524288 | tf_op jit(solution)/shard_map/all_to_all | solution.py:354
  176.7 88.0 %collective-permute-start = (bf16[2048,256]{1,0:T(8,128)(2,1)S(1)}, bf16[2048,256]{1,0:T(8,128)(2,1)S(1)}, u32[]{:S(2)}, u32[]{:S(2)}) collective-permute-start(bf16[2048,256]{1,0:T(8,128)(2,1)S(1)} %bitcast.75), channel_id=1, source_target_pairs={{0,128},{8,136},{16,144},{24,152},{32,160},{40,168},{48,176},{56,1... | collective-permute-start | bytes 3145736 | tf_op jit(solution)/shard_map/ppermute | solution.py:370
  177.6 87.0 %collective-permute-start.1 = (bf16[2048,256]{1,0:T(8,128)(2,1)S(1)}, bf16[2048,256]{1,0:T(8,128)(2,1)}, u32[]{:S(2)}, u32[]{:S(2)}) collective-permute-start(bf16[2048,256]{1,0:T(8,128)(2,1)S(1)} %bitcast.76), channel_id=1, source_target_pairs={{0,64},{8,72},{16,80},{24,88},{32,96},{40,104},{48,112},{56,120},{... | collective-permute-start | bytes 3145736 | tf_op jit(solution)/shard_map/ppermute | solution.py:370
  198.9 16.2 %all-to-all-start.1 = ((bf16[32,2,2048]{2,1,0:T(2,128)(2,1)}), bf16[32,2,2048]{2,1,0:T(2,128)(2,1)S(1)}, u32[]{:S(2)}, u32[]{:S(2)}) async-start(bf16[32,2,2048]{2,1,0:T(2,128)(2,1)} %reshape.130), calls=%async_computation.1 | async-start | bytes 524288 | tf_op jit(solution)/shard_map/all_to_all | solution.py:361
  215.2 52.4 %all-to-all-start.2 = ((bf16[4,256,256]{2,1,0:T(8,128)(2,1)}), bf16[4,256,256]{2,1,0:T(8,128)(2,1)}, u32[]{:S(2)}, u32[]{:S(2)}) async-start(bf16[4,256,256]{2,1,0:T(8,128)(2,1)} %pad_maximum_fusion.1), calls=%async_computation.2 | async-start | bytes 1048576 | tf_op jit(solution)/shard_map/all_to_all | solution.py:366
  267.5 48.7 %all-to-all-start.5 = ((bf16[32,2,2048]{2,1,0:T(2,128)(2,1)}), bf16[32,2,2048]{2,1,0:T(2,128)(2,1)S(1)}, u32[]{:S(2)}, u32[]{:S(2)}) async-start(bf16[32,2,2048]{2,1,0:T(2,128)(2,1)} %reshape.132), calls=%async_computation.5 | async-start | bytes 524288 | tf_op jit(solution)/shard_map/all_to_all | solution.py:354
  297.0 69.0 %collective-permute-start.2 = (bf16[2048,256]{1,0:T(8,128)(2,1)}, bf16[2048,256]{1,0:T(8,128)(2,1)}, u32[]{:S(2)}, u32[]{:S(2)}) collective-permute-start(bf16[2048,256]{1,0:T(8,128)(2,1)} %get-tuple-element.39), channel_id=1, source_target_pairs={{0,192},{8,200},{16,208},{24,216},{32,224},{40,232},{48,240},{56,2... | collective-permute-start | bytes 3145736 | tf_op jit(solution)/shard_map/ppermute | solution.py:370
  297.0 69.0 %collective-permute-start.3 = (bf16[2048,256]{1,0:T(8,128)(2,1)}, bf16[2048,256]{1,0:T(8,128)(2,1)}, u32[]{:S(2)}, u32[]{:S(2)}) collective-permute-start(bf16[2048,256]{1,0:T(8,128)(2,1)} %get-tuple-element.40), channel_id=1, source_target_pairs={{0,128},{8,136},{16,144},{24,152},{32,160},{40,168},{48,176},{56,1... | collective-permute-start | bytes 3145736 | tf_op jit(solution)/shard_map/ppermute | solution.py:370
  361.4 15.1 %all-to-all-start.4 = ((bf16[4,256,256]{2,1,0:T(8,128)(2,1)}), bf16[4,256,256]{2,1,0:T(8,128)(2,1)S(1)}, u32[]{:S(2)}, u32[]{:S(2)}) async-start(bf16[4,256,256]{2,1,0:T(8,128)(2,1)} %bitcast.15), calls=%async_computation.4 | async-start | bytes 1048576 | tf_op jit(solution)/shard_map/all_to_all | solution.py:412
  376.6 58.2 %all-to-all-start.7 = ((bf16[8,256,256]{2,1,0:T(8,128)(2,1)}), bf16[8,256,256]{2,1,0:T(8,128)(2,1)S(1)}, u32[]{:S(2)}, u32[]{:S(2)}) async-start(bf16[8,256,256]{2,1,0:T(8,128)(2,1)} %bitcast.19), calls=%async_computation.7 | async-start | bytes 2097152 | tf_op jit(solution)/shard_map/all_to_all | solution.py:419

commit v2 on v1

v2 whole, which is shorter than its diff:
```python
import functools
import math

import jax
import jax.numpy as jnp
from jax import lax
from jax.experimental import pallas as pl
from jax.experimental.pallas import tpu as pltpu
from jax.sharding import PartitionSpec as P

DIM = 128
WINDOW = 4096
EPSILON = 1e-05
ROW = 8
QUAD = 4
TQ = 256
TK = 512
HIDDEN = -1e30
F32 = jnp.float32
BF16 = jnp.bfloat16
EXACT = lax.Precision.HIGHEST
SCALE = DIM**-0.5
SCALE2 = SCALE * math.log2(math.e)
VMEM_LIMIT = 60 * 2**20
MESH = pl.DeviceIdType.MESH
TOK = 256
SPAN = ROW * TOK


def dot(a, b, precision=None):
    return jnp.dot(a, b, preferred_element_type=F32, precision=precision)


def dot_nt(a, b):
    return lax.dot_general(a, b, (((1,), (1,)), ((), ())), preferred_element_type=F32)


def dot_tn(a, b):
    return lax.dot_general(a, b, (((0,), (0,)), ((), ())), preferred_element_type=F32)


def shape(dims, dtype):
    return jax.ShapeDtypeStruct(dims, dtype)


def attention_kernel(facts_ref, qg_ref, kv_ref, og_ref, dkv_ref, kvt, acc):
    step = pl.program_id(0)
    me = lax.axis_index("ctx")
    quad = me // QUAD
    keys = kv_ref.shape[0]

    @pl.when(step == 0)
    def _():
        acc[...] = jnp.zeros_like(acc)

        @pl.loop(0, keys // TK)
        def _(t):
            rows = pl.ds(pl.multiple_of(t * TK, TK), TK)
            kvt[:, rows] = kv_ref[rows, :].T

    docs = facts_ref[quad * QUAD + step]
    docs = jnp.concatenate([docs[0:1, :], docs[1:2, :]], axis=1).astype(jnp.int32)
    hi_first = 2 * SPAN + (quad % 2) * (QUAD * TOK) + step * TQ
    hi_last = hi_first + TQ - 1
    hi = hi_first + lax.broadcasted_iota(jnp.int32, (1, TQ), 1)
    lo = jnp.maximum(docs - (me // ROW - 2) * SPAN, hi - (WINDOW - 1))
    lo_first, lo_last = jnp.min(lo), jnp.max(lo)
    first = lo_first // TK
    last = hi_last // TK + 1
    open_first = jnp.clip((lo_last + TK - 1) // TK, first, last)
    open_last = jnp.clip((hi_first + 1) // TK, open_first, last)

    q, g = qg_ref[:, :DIM], qg_ref[:, DIM:]
    qt, gt = q.T, g.T

    def scores(t, masked):
        rows = pl.ds(pl.multiple_of(t * TK, TK), TK)
        s = dot(kv_ref[rows, :DIM], qt)
        if masked:
            at = t * TK + lax.broadcasted_iota(jnp.int32, (TK, TQ), 0)
            s = jnp.where((at >= lo) & (at <= hi), s, HIDDEN)
        return rows, s

    def forward(masked, t, state):
        top, total, out = state
        rows, s = scores(t, masked)
        new = jnp.maximum(top, jnp.max(s, axis=0, keepdims=True))
        p = jnp.exp2((s - new) * SCALE2)
        keep = jnp.exp2((top - new) * SCALE2)
        total = total * keep + jnp.sum(p, axis=0, keepdims=True)
        out = out * keep + dot(kvt[DIM:, rows], p.astype(BF16))
        return new, total, out

    def segments(one, state):
        state = lax.fori_loop(first, open_first, functools.partial(one, True), state)
        state = lax.fori_loop(open_first, open_last, functools.partial(one, False), state)
        return lax.fori_loop(open_last, last, functools.partial(one, True), state)

    top, total, out = segments(
        forward,
        (
            jnp.full((1, TQ), HIDDEN, F32),
            jnp.zeros((1, TQ), F32),
            jnp.zeros((DIM, TQ), F32),
        ),
    )
    out = out / total
    delta = jnp.sum(gt.astype(F32) * out, axis=0, keepdims=True)
    level = top * SCALE2 + jnp.log2(total)

    def backward(masked, t, dqt):
        rows, s = scores(t, masked)
        p = jnp.exp2(s * SCALE2 - level)
        dp = dot(kv_ref[rows, DIM:], gt)
        ds = (p * (dp - delta) * SCALE).astype(BF16)
        acc[rows, :DIM] += dot(ds, q)
        acc[rows, DIM:] += dot(p.astype(BF16), g)
        return dqt + dot(kvt[:DIM, rows], ds)

    dqt = segments(backward, jnp.zeros((DIM, TQ), F32))
    og_ref[:, :DIM] = out.T.astype(BF16)
    og_ref[:, DIM:] = dqt.T.astype(BF16)

    @pl.when(step == pl.num_programs(0) - 1)
    def _():
        @pl.loop(0, keys // TK)
        def _(t):
            rows = pl.ds(pl.multiple_of(t * TK, TK), TK)
            dkv_ref[rows, :] = acc[rows, :].astype(BF16)


def attention(facts, qg, kv):
    queries, keys = qg.shape[0], kv.shape[0]
    return pl.pallas_call(
        attention_kernel,
        out_shape=(shape((queries, 2 * DIM), BF16), shape((keys, 2 * DIM), BF16)),
        grid=(queries // TQ,),
        in_specs=[
            pl.BlockSpec(facts.shape, lambda i: (0, 0, 0), pipeline_mode=pl.Buffered(1)),
            pl.BlockSpec((TQ, 2 * DIM), lambda i: (i, 0)),
            pl.BlockSpec((keys, 2 * DIM), lambda i: (0, 0), pipeline_mode=pl.Buffered(1)),
        ],
        out_specs=(
            pl.BlockSpec((TQ, 2 * DIM), lambda i: (i, 0)),
            pl.BlockSpec((keys, 2 * DIM), lambda i: (0, 0), pipeline_mode=pl.Buffered(1)),
        ),
        scratch_shapes=[
            pltpu.VMEM((2 * DIM, keys), BF16),
            pltpu.VMEM((keys, 2 * DIM), F32),
        ],
        compiler_params=pltpu.CompilerParams(
            dimension_semantics=("arbitrary",), vmem_limit_bytes=VMEM_LIMIT
        ),
        cost_estimate=pl.CostEstimate(
            flops=14 * queries * 4096 * DIM, bytes_accessed=4 * keys * DIM * 4, transcendentals=0
        ),
    )(facts, qg, kv)


def send(src, dst, sent, arrived, **where):
    return pltpu.make_async_remote_copy(
        src_ref=src, dst_ref=dst, send_sem=sent, recv_sem=arrived, device_id=where, device_id_type=MESH
    )


def ring(at, by, size):
    return lax.rem(at + by + size, size)


def greet():
    barrier = pltpu.get_barrier_semaphore()
    ctx, head = lax.axis_size("ctx"), lax.axis_size("head")
    for axis, size in (("ctx", ctx), ("head", head)):
        if size == 1:
            continue
        me = lax.axis_index(axis)

        @pl.loop(1, size)
        def _(d):
            pl.semaphore_signal(
                barrier, inc=1, device_id={axis: ring(me, d, size)}, device_id_type=MESH
            )

    pl.semaphore_wait(barrier, ctx + head - 2)


def scatter(axis, src, dst, sent, arrived):
    size, me = lax.axis_size(axis), lax.axis_index(axis)

    @pl.loop(1, size)
    def _(d):
        to = ring(me, d, size)
        send(src.at[to], dst.at[me], sent.at[d], arrived.at[d], **{axis: to}).start()


def spread(axis, src, dst, sent, arrived):
    size, me = lax.axis_size(axis), lax.axis_index(axis)

    @pl.loop(1, size)
    def _(d):
        send(src, dst.at[me], sent.at[d], arrived.at[d], **{axis: ring(me, d, size)}).start()


def collect(axis, dst, sent, arrived):
    size, me = lax.axis_size(axis), lax.axis_index(axis)

    @pl.loop(1, size)
    def _(d):
        block = dst.at[ring(me, -d, size)]
        send(block, block, sent.at[d], arrived.at[d], **{axis: ring(me, d, size)}).wait_recv()


def settle(axis, src, sent, arrived):
    size, me = lax.axis_size(axis), lax.axis_index(axis)

    @pl.loop(1, size)
    def _(d):
        send(src, src, sent.at[d], arrived.at[d], **{axis: ring(me, d, size)}).wait_send()


def column(row):
    n = row.shape[1]
    same = lax.broadcasted_iota(jnp.int32, (n, n), 0) == lax.broadcasted_iota(jnp.int32, (n, n), 1)
    return jnp.sum(jnp.where(same, row, 0.0), axis=1, keepdims=True)


def tail_decay(cum, doc):
    length = cum.shape[0]
    same = doc == doc[length - 1 : length, :]
    return jnp.where(same, jnp.exp(cum[length - 1 : length, :] - cum), 0.0)


def head_decay(cum, cum_t, seen, h):
    return jnp.exp(jnp.where(seen, cum[:, h : h + 1] - cum_t[h : h + 1, :], HIDDEN))


def visible(doc, start):
    length = doc.shape[0]
    row = lax.broadcasted_iota(jnp.int32, (length, length), 0)
    col = lax.broadcasted_iota(jnp.int32, (length, length), 1)
    return (row >= col) & ((start + col).astype(F32) >= doc)


def gate_terms(gate):
    sigma = jax.nn.sigmoid(gate)
    return sigma, gate * sigma


def cols_of(h):
    return slice(h * DIM, (h + 1) * DIM)


def head_state(buf, h, heads):
    share = buf.shape[0] // heads
    return buf[h * share : (h + 1) * share].reshape(DIM, DIM)


def put_state(buf, h, heads, value):
    share = buf.shape[0] // heads
    buf[h * share : (h + 1) * share] = value.astype(BF16).reshape(share, DIM // share, DIM)


def chain(parts, linked, factor, reverse):
    n = parts.shape[0]
    edge = n - 1 if reverse else 0
    linked[edge] = jnp.zeros(linked.shape[1:], BF16)

    def one(step, total):
        i = n - 1 - step if reverse else step
        total = total * factor[pl.ds(i, 1), :] + parts[i].astype(F32)
        linked[i - 1 if reverse else i + 1] = total.astype(BF16)
        return total

    lax.fori_loop(0, n - 1, one, jnp.zeros(parts.shape[1:], F32))


def forward_kernel(
    doc_ref, rate_ref, x_ref, gate_ref, grad_ref, write_ref, read_ref, q_ref, k_ref, v_ref, g_ref,
    kv_ref, qg_ref, facts_ref, factor_ref, cum_ref, cum_t_ref, doc_col_ref, prior_ref, mixed_ref, sums_ref,
    fact, wide, parts_out, parts_in, linked, sums_out, sums_in,
    kv_s, kv_r, qg_s, qg_r, one_s, one_r, two_s, two_r,
    fact_s, fact_r, part_s, part_r, link_s, link_r, sum_s, sum_r,
):
    ctx = lax.axis_size("ctx")
    me, head = lax.axis_index("ctx"), lax.axis_index("head")
    x, z = me // ROW, lax.rem(me, ROW)
    spot = lax.rem(me, QUAD)
    length, heads = rate_ref.shape
    start = me * length

    docs = doc_ref[...].astype(F32)
    fact[...] = jnp.zeros_like(fact)
    fact[0:2, :] = docs
    rate = rate_ref[...]
    fact[2:3, :heads] = jnp.sum(rate, axis=0, keepdims=True)
    facts_ref[me] = fact[...]

    greet()
    spread("ctx", fact, facts_ref, fact_s, fact_r)

    def block(ref, a):
        return ref.at[:, pl.ds(pl.multiple_of(a * DIM, DIM), DIM)]

    def rows_of(first, z_from):
        return pl.ds(pl.multiple_of(first + z_from * TOK, TOK), TOK)

    halves = (slice(0, DIM), slice(DIM, 2 * DIM))

    def key_copies(d, z_from, z_to):
        out = []
        for i, ref in enumerate((k_ref, v_ref)):
            src = block(ref, lax.rem(z_to, QUAD))
            dst = kv_ref.at[rows_of(2 * SPAN, z_from), halves[i]]
            if d == 0:
                out.append(pltpu.make_async_copy(src, dst, kv_r.at[d, i]))
            else:
                out.append(send(src, dst, kv_s.at[d, i], kv_r.at[d, i], ctx=x * ROW + z_to))
        return out

    def query_copies(d, from_, to):
        out = []
        for i, ref in enumerate((q_ref, g_ref)):
            src = block(ref, to)
            dst = qg_ref.at[rows_of(0, from_), halves[i]]
            if d == 0:
                out.append(pltpu.make_async_copy(src, dst, qg_r.at[d, i]))
            else:
                out.append(send(src, dst, qg_s.at[d, i], qg_r.at[d, i], ctx=me - spot + to))
        return out

    for d in range(ROW):
        for copy in key_copies(d, z, ring(z, d, ROW)):
            copy.start()
    for d in range(QUAD):
        for copy in query_copies(d, spot, ring(spot, d, QUAD)):
            copy.start()

    row = lax.broadcasted_iota(jnp.int32, (length, length), 0)
    col = lax.broadcasted_iota(jnp.int32, (length, length), 1)
    cum = dot((row >= col).astype(F32), rate, EXACT)
    cum_ref[...] = cum
    wide[...] = jnp.zeros_like(wide)
    wide[:, :heads] = cum
    cum_t = wide[...].T[:heads]
    cum_t_ref[...] = cum_t
    doc = jnp.concatenate([column(docs[0:1, :]), column(docs[1:2, :])], axis=0)
    doc_col_ref[...] = doc
    tail = tail_decay(cum, doc)
    write, read = write_ref[...], read_ref[...]
    for h in range(heads):
        scaled = (x_ref[:, cols_of(h)].astype(F32) * tail[:, h : h + 1]).astype(BF16)
        put_state(parts_out, h, heads, dot_tn(write, scaled))
    parts_in[me] = parts_out[me]
    scatter("ctx", parts_out, parts_in, part_s, part_r)

    seen = visible(doc, start)
    scores = dot_nt(read, write)
    for h in range(heads):
        mix = (head_decay(cum, cum_t, seen, h) * scores).astype(BF16)
        mixed_ref[:, cols_of(h)] = dot(mix, x_ref[:, cols_of(h)])

    collect("ctx", facts_ref, fact_s, fact_r)
    at = lax.broadcasted_iota(jnp.int32, (ctx, 1), 0)
    lane = lax.broadcasted_iota(jnp.int32, (ctx, DIM), 1)
    mine = me // (ctx // heads)
    total = jnp.sum(jnp.where(lane == mine, facts_ref[:, 2, :], 0.0), axis=1, keepdims=True)
    final = jnp.sum(jnp.where(lane == DIM - 1, facts_ref[:, 1, :], 0.0), axis=1, keepdims=True)
    factor = jnp.where(final < (at * length).astype(F32), jnp.exp(total), 0.0)
    factor_ref[...] = jnp.broadcast_to(factor, factor_ref.shape)

    collect("ctx", parts_in, part_s, part_r)
    chain(parts_in, linked, factor_ref, False)
    prior_ref[me] = linked[me]
    scatter("ctx", linked, prior_ref, link_s, link_r)

    def pass_on(d, first, sent, arrived):
        z_from = ring(z, -d, ROW)
        return send(
            kv_ref.at[rows_of(first, z_from), :],
            kv_ref.at[rows_of(first - SPAN, z_from), :],
            sent.at[d], arrived.at[d], ctx=lax.rem(me + ROW, ctx),
        )

    last_row = ctx // ROW - 1
    for d in range(ROW):
        for copy in key_copies(d, ring(z, -d, ROW), z):
            if d == 0:
                copy.wait()
            else:
                copy.wait_recv()

        @pl.when(x < last_row)
        def _():
            pass_on(d, 2 * SPAN, one_s, one_r).start()

    collect("ctx", prior_ref, link_s, link_r)
    enter = jnp.where(doc < start.astype(F32), jnp.exp(cum), 0.0)
    squares = jnp.zeros((length, 1), F32)
    inner = jnp.zeros((length, 1), F32)
    for h in range(heads):
        mixed = mixed_ref[:, cols_of(h)] + enter[:, h : h + 1] * dot(read, head_state(prior_ref, h, heads))
        mixed_ref[:, cols_of(h)] = mixed
        gated = mixed * gate_terms(gate_ref[:, cols_of(h)].astype(F32))[1]
        squares += jnp.sum(gated * gated, axis=1, keepdims=True)
        inner += jnp.sum(grad_ref[:, cols_of(h)].astype(F32) * gated, axis=1, keepdims=True)
    wide[:, 0:1] = squares
    wide[:, 1:2] = inner
    sums_out[...] = wide[...].T[:8]
    sums_in[head] = sums_out[...]
    spread("head", sums_out, sums_in, sum_s, sum_r)

    def wanted(d):
        return (z < QUAD) | (ring(z, -d, ROW) >= QUAD)

    for d in range(ROW):

        @pl.when(x >= 1)
        def _():
            pass_on(d, 2 * SPAN, one_s, one_r).wait_recv()

        @pl.when((x >= 1) & (x < last_row) & wanted(d))
        def _():
            pass_on(d, SPAN, two_s, two_r).start()

    collect("head", sums_in, sum_s, sum_r)
    sums = sums_in[0]
    for i in range(1, sums_in.shape[0]):
        sums += sums_in[i]
    sums_ref[...] = jnp.concatenate([sums, jnp.zeros((DIM - 8, length), F32)], axis=0).T

    for d in range(QUAD):
        for copy in query_copies(d, ring(spot, -d, QUAD), spot):
            if d == 0:
                copy.wait()
            else:
                copy.wait_recv()
    for d in range(ROW):

        @pl.when((x >= 2) & wanted(d))
        def _():
            pass_on(d, SPAN, two_s, two_r).wait_recv()

    for d in range(1, ROW):
        for copy in key_copies(d, z, ring(z, d, ROW)):
            copy.wait_send()
    for d in range(1, QUAD):
        for copy in query_copies(d, spot, ring(spot, d, QUAD)):
            copy.wait_send()
    for d in range(ROW):

        @pl.when(x < last_row)
        def _():
            pass_on(d, 2 * SPAN, one_s, one_r).wait_send()

        @pl.when((x >= 1) & (x < last_row) & wanted(d))
        def _():
            pass_on(d, SPAN, two_s, two_r).wait_send()

    settle("ctx", fact, fact_s, fact_r)
    settle("ctx", parts_out.at[0], part_s, part_r)
    settle("ctx", linked.at[0], link_s, link_r)
    settle("head", sums_out, sum_s, sum_r)


def backward_kernel(
    width, sums_ref, mixed_ref, x_ref, gate_ref, grad_ref, write_ref, read_ref, cum_ref, cum_t_ref, doc_col_ref,
    prior_ref, factor_ref, og_ref, dkv_ref,
    out_ref, window_ref, input_grad_ref, gate_grad_ref, write_grad_ref, read_grad_ref,
    query_grad_ref, key_grad_ref, value_grad_ref,
    dmixed_ref, input_ref, parts_out, parts_in, linked, after_ref, maps, maps_in, maps_sum, maps_all,
    far_in, near_out, near_in, row_out, row_in,
    og_s, og_r, far_s, far_r, near_s, near_r, row_s, row_r,
    part_s, part_r, link_s, link_r, map_s, map_r, all_s, all_r,
):
    ctx, crew = lax.axis_size("ctx"), lax.axis_size("head")
    me, head = lax.axis_index("ctx"), lax.axis_index("head")
    x, z = me // ROW, lax.rem(me, ROW)
    spot = lax.rem(me, QUAD)
    length, heads = cum_ref.shape
    start = me * length
    last_row = ctx // ROW - 1
    greet()

    def rows_of(first, z_from):
        return pl.ds(pl.multiple_of(first + z_from * TOK, TOK), TOK)

    halves = (slice(0, DIM), slice(DIM, 2 * DIM))

    def result_copies(d, a, to):
        out = []
        for i, ref in enumerate((window_ref, query_grad_ref)):
            src = og_ref.at[rows_of(0, to), halves[i]]
            dst = ref.at[:, pl.ds(pl.multiple_of(a * DIM, DIM), DIM)]
            if d == 0:
                out.append(pltpu.make_async_copy(src, dst, og_r.at[d, i]))
            else:
                out.append(send(src, dst, og_s.at[d, i], og_r.at[d, i], ctx=me - spot + to))
        return out

    def wanted(b):
        return (z < QUAD) | (b >= QUAD)

    def back(src, dst, b, sent, arrived):
        return send(src, dst, sent.at[b], arrived.at[b], ctx=lax.rem(me + ctx - ROW, ctx))

    def far(b):
        return back(dkv_ref.at[rows_of(0, b), :], far_in.at[b], b, far_s, far_r)

    def near(b):
        return back(near_out.at[b], near_in.at[b], b, near_s, near_r)

    @pl.when(x >= 2)
    def _():
        @pl.loop(0, ROW)
        def _(b):
            @pl.when(wanted(b))
            def _():
                far(b).start()

    for d in range(QUAD):
        for copy in result_copies(d, spot, ring(spot, d, QUAD)):
            copy.start()

    cum, cum_t, doc = cum_ref[...], cum_t_ref[...], doc_col_ref[...]
    enter = jnp.where(doc < start.astype(F32), jnp.exp(cum), 0.0)
    rms = lax.rsqrt(sums_ref[:, 0:1] / width + EPSILON)
    pull = rms * rms * rms * sums_ref[:, 1:2] / width
    write, read = write_ref[...], read_ref[...]
    for h in range(heads):
        cols = cols_of(h)
        mixed = mixed_ref[:, cols]
        gate = gate_ref[:, cols].astype(F32)
        sigma, swish = gate_terms(gate)
        gated = mixed * swish
        out_ref[:, cols] = (gated * rms).astype(BF16)
        dgated = rms * grad_ref[:, cols].astype(F32) - pull * gated
        dmixed = dgated * swish
        dmixed_ref[:, cols] = dmixed.astype(BF16)
        gate_grad_ref[:, cols] = (dgated * mixed * sigma * (1.0 + gate * (1.0 - sigma))).astype(BF16)
        put_state(parts_out, h, heads, dot_tn(read, (enter[:, h : h + 1] * dmixed).astype(BF16)))
    parts_in[me] = parts_out[me]
    scatter("ctx", parts_out, parts_in, part_s, part_r)

    @pl.loop(0, ROW)
    def _(b):
        own = dkv_ref[rows_of(SPAN, b), :]
        more = (x >= 1) & (x < last_row) & wanted(b)

        @pl.when(more)
        def _():
            far(b).wait_recv()
            near_out[b] = (own.astype(F32) + far_in[b].astype(F32)).astype(BF16)

        @pl.when(jnp.logical_not(more))
        def _():
            near_out[b] = own

        @pl.when(x >= 1)
        def _():
            near(b).start()

    seen = visible(doc, start)
    scores = dot_nt(read, write)
    pairs = jnp.zeros_like(scores)
    read_part = jnp.zeros(read.shape, F32)
    for h in range(heads):
        cols = cols_of(h)
        decay = head_decay(cum, cum_t, seen, h)
        dmixed = dmixed_ref[:, cols]
        input_ref[:, cols] = dot_tn((decay * scores).astype(BF16), dmixed)
        pairs += decay * dot_nt(dmixed, x_ref[:, cols])
        entered = (enter[:, h : h + 1] * dmixed.astype(F32)).astype(BF16)
        read_part += dot_nt(entered, head_state(prior_ref, h, heads))
    pairs = pairs.astype(BF16)
    write_part = dot_tn(pairs, read)
    read_part += dot(pairs, write)

    collect("ctx", parts_in, part_s, part_r)
    chain(parts_in, linked, factor_ref, True)
    after_ref[me] = linked[me]
    scatter("ctx", linked, after_ref, link_s, link_r)

    def row_copy(d, b):
        return send(row_out.at[b], row_in.at[z], row_s.at[d], row_r.at[d], ctx=x * ROW + b)

    for d in range(ROW):
        b = ring(z, d, ROW)
        own = dkv_ref[rows_of(2 * SPAN, b), :]

        @pl.when(x < last_row)
        def _():
            near(b).wait_recv()
            row_out[b] = (own.astype(F32) + near_in[b].astype(F32)).astype(BF16)

        @pl.when(x == last_row)
        def _():
            row_out[b] = own

        if d:
            row_copy(d, b).start()
        else:
            row_in[z] = row_out[b]

    collect("ctx", after_ref, link_s, link_r)
    tail = tail_decay(cum, doc)
    for h in range(heads):
        cols = cols_of(h)
        t = tail[:, h : h + 1]
        after = head_state(after_ref, h, heads)
        input_grad_ref[:, cols] = (input_ref[:, cols] + t * dot(write, after)).astype(BF16)
        write_part += dot_nt((x_ref[:, cols].astype(F32) * t).astype(BF16), after)

    share = length // crew
    maps[:, :, :DIM] = write_part.reshape(crew, share, DIM)
    maps[:, :, DIM:] = read_part.reshape(crew, share, DIM)
    maps_in[head] = maps[head]
    scatter("head", maps, maps_in, map_s, map_r)
    collect("head", maps_in, map_s, map_r)
    added = maps_in[0]
    for i in range(1, crew):
        added += maps_in[i]
    maps_sum[...] = added.astype(BF16)
    maps_all[head] = maps_sum[...]
    spread("head", maps_sum, maps_all, all_s, all_r)

    for d in range(1, ROW):
        z_from = ring(z, -d, ROW)
        send(row_out.at[z], row_in.at[z_from], row_s.at[d], row_r.at[d], ctx=x * ROW + z_from).wait_recv()
    for a in range(QUAD):
        both = row_in[a].astype(F32) + row_in[QUAD + a].astype(F32)
        key_grad_ref[:, cols_of(a)] = both[:, :DIM].astype(BF16)
        value_grad_ref[:, cols_of(a)] = both[:, DIM:].astype(BF16)

    collect("head", maps_all, all_s, all_r)
    both = maps_all[...].reshape(length, 2 * DIM)
    write_grad_ref[...] = both[:, :DIM]
    read_grad_ref[...] = both[:, DIM:]

    for d in range(QUAD):
        for copy in result_copies(d, ring(spot, -d, QUAD), spot):
            if d == 0:
                copy.wait()
            else:
                copy.wait_recv()

    for d in range(1, QUAD):
        for copy in result_copies(d, spot, ring(spot, d, QUAD)):
            copy.wait_send()
    for d in range(1, ROW):
        row_copy(d, ring(z, d, ROW)).wait_send()

    @pl.loop(0, ROW)
    def _(b):
        @pl.when((x >= 2) & wanted(b))
        def _():
            far(b).wait_send()

        @pl.when(x >= 1)
        def _():
            near(b).wait_send()

    settle("ctx", parts_out.at[0], part_s, part_r)
    settle("ctx", linked.at[0], link_s, link_r)
    settle("head", maps.at[0], map_s, map_r)
    settle("head", maps_sum, all_s, all_r)


def remote_call(kernel, number, outs, kept, args, far, scratch, sems):
    vmem, stay = pl.BlockSpec(memory_space=pltpu.VMEM), pl.BlockSpec(memory_space=pl.ANY)
    return pl.pallas_call(
        kernel,
        out_shape=tuple(outs),
        in_specs=[stay if i in far else vmem for i in range(len(args))],
        out_specs=tuple(stay if i in kept else vmem for i in range(len(outs))),
        scratch_shapes=[pltpu.VMEM(s, t) for s, t in scratch] + [pltpu.SemaphoreType.DMA(s) for s in sems],
        compiler_params=pltpu.CompilerParams(
            collective_id=number, has_side_effects=True, vmem_limit_bytes=VMEM_LIMIT
        ),
    )(*args)


def body(
    ssm_input,
    gate_input,
    write_map,
    read_map,
    log_decay,
    doc_start,
    ssm_grad,
    att_queries,
    att_keys,
    att_values,
    att_grad,
):
    ctx, crew = lax.axis_size("ctx"), lax.axis_size("head")
    length, width = ssm_input.shape
    heads = width // DIM
    att_width = att_queries.shape[1]
    part = (ctx, heads * DIM // ctx, DIM)
    flat, tall = (length, width), (length, DIM)

    kv, qg, facts, factor, cum, cum_t, doc_col, prior, mixed, sums = remote_call(
        forward_kernel,
        0,
        [
            shape((3 * SPAN, 2 * DIM), BF16), shape((QUAD * length, 2 * DIM), BF16),
            shape((ctx, 8, DIM), F32), shape((ctx, DIM), F32), shape((length, heads), F32),
            shape((heads, length), F32), shape((length, 1), F32), shape(part, BF16), shape(flat, F32),
            shape(tall, F32),
        ],
        (0, 1),
        (
            doc_start.reshape(2, length // 2), log_decay, ssm_input, gate_input, ssm_grad, write_map, read_map,
            att_queries, att_keys, att_values, att_grad,
        ),
        (7, 8, 9, 10),
        [((8, DIM), F32), (tall, F32), (part, BF16), (part, BF16), (part, BF16),
         ((8, length), F32), ((crew, 8, length), F32)],
        [(ROW, 2), (ROW, 2), (QUAD, 2), (QUAD, 2), (ROW,), (ROW,), (ROW,), (ROW,),
         (ctx,), (ctx,), (ctx,), (ctx,), (ctx,), (ctx,), (crew,), (crew,)],
    )

    og, dkv = attention(facts, qg, kv)

    block = (ROW, TOK, 2 * DIM)
    share = (crew, length // crew, 2 * DIM)
    return tuple(
        remote_call(
            functools.partial(backward_kernel, width * crew),
            1,
            [shape(flat, BF16), shape((length, att_width), BF16), shape(flat, BF16), shape(flat, BF16),
             shape(tall, BF16), shape(tall, BF16), shape((length, att_width), BF16),
             shape((length, att_width), BF16), shape((length, att_width), BF16)],
            (),
            (sums, mixed, ssm_input, gate_input, ssm_grad, write_map, read_map, cum, cum_t, doc_col, prior, factor,
             og, dkv),
            (),
            [(flat, BF16), (flat, F32), (part, BF16), (part, BF16), (part, BF16), (part, BF16),
             (share, F32), (share, F32), (share[1:], BF16), (share, BF16),
             (block, BF16), (block, BF16), (block, BF16), (block, BF16), (block, BF16)],
            [(QUAD, 2), (QUAD, 2), (ROW,), (ROW,), (ROW,), (ROW,), (ROW,), (ROW,),
             (ctx,), (ctx,), (ctx,), (ctx,), (crew,), (crew,), (crew,), (crew,)],
        )
    )


def solution(mesh):
    tokens, both = P("ctx", None), P("ctx", "head")
    in_specs = (both, both, tokens, tokens, both, P("ctx"), both, both, both, both, both)
    out_specs = (both, both, both, both, tokens, tokens, both, both, both)
    return jax.shard_map(body, mesh=mesh, in_specs=in_specs, out_specs=out_specs, check_vma=False)
```

time: 438 us -> 246 us (0.56)
  blocking collectives: 229 us -> 0 us
  Pallas kernels: 43.1 us -> 232 us
  starting transfers between devices: 82.3 us -> 0 us
  waiting for transfers between devices: 34.4 us -> 0 us
  other arithmetic: 19.8 us -> 0 us
  local copies, waits for them, and re-layouts: 26.6 us -> 12.2 us
    pallas_call x8 -> x2, Pallas kernels: 25.2 us -> 209 us  [remote_call(): pl.pallas_call(kernel, out_shape=tuple(outs), in_specs=[stay if i in far...]
    unnamed x1 -> x0, blocking collectives: 131 us -> none
    psum x2 -> x0, blocking collectives: 58.3 us -> none  [the longest x1 32.4 us: body(): maps = lax.psum(maps, 'head').astype(BF16)]
    all_to_all x7 -> x0, starting transfers between devices: 48.5 us -> none  [the longest x1 14 us: body(): lax.all_to_all(dkv_sum.reshape(ROW, length, 2 * DIM), 'ctx', 0, 0, axis_i...]
    all_to_all x1 -> x0, blocking collectives: 39.8 us -> none  [exchange(): return lax.all_to_all(linked, 'ctx', 0, 0).reshape(heads, DIM, DIM)]
    all_to_all x7 -> x0, waiting for transfers between devices: 34.4 us -> none  [the longest x1 17.3 us: body(): lax.all_to_all(jnp.concatenate([kv, kv], axis=0), 'ctx', 0, 0, axis_index...]
    ppermute x4 -> x0, starting transfers between devices: 33.7 us -> none  [rotate(): return lax.ppermute(a, 'ctx', [(i, (i + by) % n) for i in range(n)])]
    all_to_all x6 -> x0, other arithmetic: 10.8 us -> none  [the longest x4 6.49 us: exchange(): return lax.all_to_all(linked, 'ctx', 0, 0).reshape(heads, DIM, DIM)]
  transfers between devices with their start and end apart: 11 -> 0, of which waited for: 3 -> 0; matrix products, arithmetic and copies ran while one was open for 9% -> 0% of each run, Pallas kernels for 10% -> 0%
where the time goes in v2:
time: 246 us; the launch traced here: 245 us
  Pallas kernels  232 us (94%)
  local copies, waits for them, and re-layouts  12.2 us (5%)
    pallas_call x2, Pallas kernels, remote_call(): pl.pallas_call(kernel, out_shape=tuple(outs), in_specs=[stay if i in far...  209 us
    pallas_call x1, Pallas kernels, attention(): pl.pallas_call(attention_kernel, out_shape=(shape((queries, 2 * DIM), BF1...  22.7 us
    unnamed x20, local copies, waits for them, and re-layouts  12.2 us

profile of v2, /device:TPU:2, one launch (start us, length us, event | category | flops | bytes accessed | tf_op | source)
XLA Modules:
  0.0 244.7 jit_solution(10461853946313395084)
XLA Ops:
  0.6 1.5 copy.20.rate_ref
  2.1 108.4 %shard_map.178 = (bf16[6144,256]{1,0:T(8,128)(2,1)}, bf16[1024,256]{1,0:T(8,128)(2,1)}, f32[32,8,128]{2,1,0:T(8,128)}, f32[32,128]{1,0:T(8,128)}, f32[256,8]{1,0...) custom-call(s32[2,128]{1,0:T(2,128)} %bitcast.1, ...), custom_call_target="tpu_custom_call" | custom-call | tf_op jit(solution)/shard_map/pallas_call | solution.py:670
  110.5 22.7 %shard_map.179 = (bf16[1024,256]{1,0:T(8,128)(2,1)}, bf16[6144,256]{1,0:T(8,128)(2,1)}) custom-call(f32[32,8,128]{2,1,0:T(8,128)} %get-tuple-element.28.facts_ref, bf16[1024,256]{1,0:T(8,128)(2,1)} %get-tuple-element.29.qg_ref, bf16[6144,256]{1,0:T(8,128)(2,1)} %get-tuple-element.30.kv_ref), custom_call_target="tpu_custom_call" | custom-call | flops 7516192768 | bytes 12582912 | tf_op jit(solution)/shard_map/pallas_call | solution.py:134
  133.2 100.7 %shard_map.180 = (bf16[256,1024]{1,0:T(8,128)(2,1)}, bf16[256,512]{1,0:T(8,128)(2,1)}, bf16[256,1024]{1,0:T(8,128)(2,1)}, bf16[256,1024]{1,0:T(8,128)(2,1)}, bf1...) custom-call(f32[256,128]{1,0:T(8,128)} %get-tuple-element.21.sums_re, ...), custom_call_target="tpu_custom_call" | custom-call | tf_op jit(solution)/shard_map/pallas_call | solution.py:670
  233.9 0.0 copy-start.4
  233.9 0.0 copy-start.3
  234.0 0.0 copy-start.2
  234.0 0.0 copy-start.1
  234.0 0.0 copy-start
  234.0 1.9 copy.30
  235.9 1.7 copy.31
  237.6 1.9 copy.32
  239.5 1.9 copy.33
  241.3 0.0 copy-done.4
  241.3 0.6 copy.34
  242.0 0.0 copy-done.3
  242.0 0.6 copy.35
  242.6 0.0 copy-done.2
  242.6 0.7 copy.36
  243.3 0.0 copy-done.1
  243.3 0.7 copy.37
  244.0 0.0 copy-done
  244.0 0.7 copy.38
Async XLA Ops:
  233.9 7.4 %copy-start.4 = (bf16[256,128]{1,0:T(8,128)(2,1)S(1)}, bf16[256,128]{1,0:T(8,128)(2,1)}, u32[]{:S(2)}) copy-start(bf16[256,128]{1,0:T(8,128)(2,1)} %get-tuple-element.46) | copy-start | bytes 196612
  233.9 8.0 %copy-start.3 = (bf16[256,128]{1,0:T(8,128)(2,1)S(1)}, bf16[256,128]{1,0:T(8,128)(2,1)}, u32[]{:S(2)}) copy-start(bf16[256,128]{1,0:T(8,128)(2,1)} %get-tuple-element.47) | copy-start | bytes 196612
  234.0 8.6 %copy-start.2 = (bf16[256,512]{1,0:T(8,128)(2,1)S(1)}, bf16[256,512]{1,0:T(8,128)(2,1)}, u32[]{:S(2)}) copy-start(bf16[256,512]{1,0:T(8,128)(2,1)} %get-tuple-element.48) | copy-start | bytes 786436
  234.0 9.3 %copy-start.1 = (bf16[256,512]{1,0:T(8,128)(2,1)S(1)}, bf16[256,512]{1,0:T(8,128)(2,1)}, u32[]{:S(2)}) copy-start(bf16[256,512]{1,0:T(8,128)(2,1)} %get-tuple-element.49) | copy-start | bytes 786436
  234.0 10.0 %copy-start = (bf16[256,512]{1,0:T(8,128)(2,1)S(1)}, bf16[256,512]{1,0:T(8,128)(2,1)}, u32[]{:S(2)}) copy-start(bf16[256,512]{1,0:T(8,128)(2,1)} %get-tuple-element.50) | copy-start | bytes 786436

commit v3 on v2

v3 whole, which is shorter than its diff:
```python
import functools
import math

import jax
import jax.numpy as jnp
from jax import lax
from jax.experimental import pallas as pl
from jax.experimental.pallas import tpu as pltpu
from jax.sharding import PartitionSpec as P

DIM = 128
WINDOW = 4096
EPSILON = 1e-05
ROW = 8
QUAD = 4
TQ = 256
TK = 512
QUERIES = QUAD * 256
HIDDEN = -1e30
F32 = jnp.float32
BF16 = jnp.bfloat16
EXACT = lax.Precision.HIGHEST
SCALE = DIM**-0.5
SCALE2 = SCALE * math.log2(math.e)
VMEM_LIMIT = 60 * 2**20
MESH = pl.DeviceIdType.MESH
TOK = 256
SPAN = ROW * TOK


def dot(a, b, precision=None):
    return jnp.dot(a, b, preferred_element_type=F32, precision=precision)


def dot_nt(a, b):
    return lax.dot_general(a, b, (((1,), (1,)), ((), ())), preferred_element_type=F32)


def dot_tn(a, b):
    return lax.dot_general(a, b, (((0,), (0,)), ((), ())), preferred_element_type=F32)


def shape(dims, dtype):
    return jax.ShapeDtypeStruct(dims, dtype)


def send(src, dst, sent, arrived, **where):
    return pltpu.make_async_remote_copy(
        src_ref=src, dst_ref=dst, send_sem=sent, recv_sem=arrived, device_id=where, device_id_type=MESH
    )


def ring(at, by, size):
    return lax.rem(at + by + size, size)


def greet():
    barrier = pltpu.get_barrier_semaphore()
    ctx, head = lax.axis_size("ctx"), lax.axis_size("head")
    for axis, size in (("ctx", ctx), ("head", head)):
        if size == 1:
            continue
        me = lax.axis_index(axis)

        @pl.loop(1, size)
        def _(d):
            pl.semaphore_signal(
                barrier, inc=1, device_id={axis: ring(me, d, size)}, device_id_type=MESH
            )

    pl.semaphore_wait(barrier, ctx + head - 2)


def scatter(axis, src, dst, sent, arrived):
    size, me = lax.axis_size(axis), lax.axis_index(axis)

    @pl.loop(1, size)
    def _(d):
        to = ring(me, d, size)
        send(src.at[to], dst.at[me], sent.at[d], arrived.at[d], **{axis: to}).start()


def spread(axis, src, dst, sent, arrived):
    size, me = lax.axis_size(axis), lax.axis_index(axis)

    @pl.loop(1, size)
    def _(d):
        send(src, dst.at[me], sent.at[d], arrived.at[d], **{axis: ring(me, d, size)}).start()


def collect(axis, dst, sent, arrived):
    size, me = lax.axis_size(axis), lax.axis_index(axis)

    @pl.loop(1, size)
    def _(d):
        block = dst.at[ring(me, -d, size)]
        send(block, block, sent.at[d], arrived.at[d], **{axis: ring(me, d, size)}).wait_recv()


def settle(axis, src, sent, arrived):
    size, me = lax.axis_size(axis), lax.axis_index(axis)

    @pl.loop(1, size)
    def _(d):
        send(src, src, sent.at[d], arrived.at[d], **{axis: ring(me, d, size)}).wait_send()


def column(row):
    n = row.shape[1]
    same = lax.broadcasted_iota(jnp.int32, (n, n), 0) == lax.broadcasted_iota(jnp.int32, (n, n), 1)
    return jnp.sum(jnp.where(same, row, 0.0), axis=1, keepdims=True)


def tail_decay(cum, doc):
    length = cum.shape[0]
    same = doc == doc[length - 1 : length, :]
    return jnp.where(same, jnp.exp(cum[length - 1 : length, :] - cum), 0.0)


def head_decay(cum, cum_t, seen, h):
    return jnp.exp(jnp.where(seen, cum[:, h : h + 1] - cum_t[h : h + 1, :], HIDDEN))


def visible(doc, start):
    length = doc.shape[0]
    row = lax.broadcasted_iota(jnp.int32, (length, length), 0)
    col = lax.broadcasted_iota(jnp.int32, (length, length), 1)
    return (row >= col) & ((start + col).astype(F32) >= doc)


def gate_terms(gate):
    sigma = jax.nn.sigmoid(gate)
    return sigma, gate * sigma


def cols_of(h):
    return slice(h * DIM, (h + 1) * DIM)


def head_state(buf, h, heads):
    share = buf.shape[0] // heads
    return buf[h * share : (h + 1) * share].reshape(DIM, DIM)


def put_state(buf, h, heads, value):
    share = buf.shape[0] // heads
    buf[h * share : (h + 1) * share] = value.astype(BF16).reshape(share, DIM // share, DIM)


def chain(parts, linked, factor, reverse):
    n = parts.shape[0]
    edge = n - 1 if reverse else 0
    linked[edge] = jnp.zeros(linked.shape[1:], BF16)

    def one(step, total):
        i = n - 1 - step if reverse else step
        total = total * factor[pl.ds(i, 1), :] + parts[i].astype(F32)
        linked[i - 1 if reverse else i + 1] = total.astype(BF16)
        return total

    lax.fori_loop(0, n - 1, one, jnp.zeros(parts.shape[1:], F32))


def rows_of(first, block):
    return pl.ds(pl.multiple_of(first + block * TOK, TOK), TOK)


def head_block(ref, a):
    return ref.at[:, pl.ds(pl.multiple_of(a * DIM, DIM), DIM)]


HALVES = (slice(0, DIM), slice(DIM, 2 * DIM))


def mixer_kernel(
    width, doc_ref, rate_ref, x_ref, gate_ref, grad_ref, write_ref, read_ref, q_ref, k_ref, v_ref, g_ref,
    out_ref, window_ref, input_grad_ref, gate_grad_ref, write_grad_ref, read_grad_ref,
    query_grad_ref, key_grad_ref, value_grad_ref,
    kv_ref, qg_ref, og_ref, facts_ref, factor_ref, fact, wide, mixed_ref, dmixed_ref, input_ref,
    parts_out, parts_in, linked, prior_ref, back_out, back_in, relinked, after_ref,
    sums_out, sums_in, maps, maps_in, maps_sum, maps_all,
    far_out, far_in, near_out, near_in, row_out, row_in,
    qt_ref, gt_ref, stat_ref, low_ref, out_t, dq_t, p_ref, ds_ref,
    kv_s, kv_r, qg_s, qg_r, one_s, one_r, two_s, two_r, og_s, og_r, far_s, far_r, near_s, near_r, row_s, row_r,
    fact_s, fact_r, part_s, part_r, link_s, link_r, back_s, back_r, relink_s, relink_r,
    sum_s, sum_r, map_s, map_r, all_s, all_r,
):
    ctx, crew = lax.axis_size("ctx"), lax.axis_size("head")
    me, head = lax.axis_index("ctx"), lax.axis_index("head")
    x, z = me // ROW, lax.rem(me, ROW)
    spot = lax.rem(me, QUAD)
    half = z // QUAD
    last_row = ctx // ROW - 1
    length, heads = rate_ref.shape
    start = me * length

    def key_copies(d, z_from, z_to):
        out = []
        for i, ref in enumerate((k_ref, v_ref)):
            src = head_block(ref, lax.rem(z_to, QUAD))
            dst = kv_ref.at[rows_of(2 * SPAN, z_from), HALVES[i]]
            if d == 0:
                out.append(pltpu.make_async_copy(src, dst, kv_r.at[d, i]))
            else:
                out.append(send(src, dst, kv_s.at[d, i], kv_r.at[d, i], ctx=x * ROW + z_to))
        return out

    def query_copies(d, from_, to):
        out = []
        for i, ref in enumerate((q_ref, g_ref)):
            src = head_block(ref, to)
            dst = qg_ref.at[rows_of(0, from_), HALVES[i]]
            if d == 0:
                out.append(pltpu.make_async_copy(src, dst, qg_r.at[d, i]))
            else:
                out.append(send(src, dst, qg_s.at[d, i], qg_r.at[d, i], ctx=me - spot + to))
        return out

    def pass_on(d, first, sent, arrived):
        z_from = ring(z, -d, ROW)
        return send(
            kv_ref.at[rows_of(first, z_from), :],
            kv_ref.at[rows_of(first - SPAN, z_from), :],
            sent.at[d], arrived.at[d], ctx=lax.rem(me + ROW, ctx),
        )

    def result_copy(i, d, a, to):
        src = og_ref.at[rows_of(0, to), HALVES[i]]
        dst = head_block((window_ref, query_grad_ref)[i], a)
        if d == 0:
            return pltpu.make_async_copy(src, dst, og_r.at[d, i])
        return send(src, dst, og_s.at[d, i], og_r.at[d, i], ctx=me - spot + to)

    def far(b):
        return send(far_out.at[b], far_in.at[b], far_s.at[b], far_r.at[b], ctx=lax.rem(me + ctx - ROW, ctx))

    def near(b):
        return send(near_out.at[b], near_in.at[b], near_s.at[b], near_r.at[b], ctx=lax.rem(me + ctx - ROW, ctx))

    def row_copy(d, b):
        return send(row_out.at[b], row_in.at[z], row_s.at[d], row_r.at[d], ctx=x * ROW + b)

    def wanted(b):
        return (z < QUAD) | (b >= QUAD)

    docs = doc_ref[...].astype(F32)
    rate = rate_ref[...]
    fact[...] = jnp.zeros_like(fact)
    fact[0:2, :] = docs
    fact[2:3, :heads] = jnp.sum(rate, axis=0, keepdims=True)
    facts_ref[me] = fact[...]

    greet()
    for d in range(ROW):
        for copy in key_copies(d, z, ring(z, d, ROW)):
            copy.start()
    spread("ctx", fact, facts_ref, fact_s, fact_r)

    row = lax.broadcasted_iota(jnp.int32, (length, length), 0)
    col = lax.broadcasted_iota(jnp.int32, (length, length), 1)
    cum = dot((row >= col).astype(F32), rate, EXACT)
    wide[...] = jnp.zeros_like(wide)
    wide[:, :heads] = cum
    cum_t = wide[...].T[:heads]
    doc = jnp.concatenate([column(docs[0:1, :]), column(docs[1:2, :])], axis=0)
    tail = tail_decay(cum, doc)
    enter = jnp.where(doc < start.astype(F32), jnp.exp(cum), 0.0)
    write, read = write_ref[...], read_ref[...]
    for h in range(heads):
        scaled = (x_ref[:, cols_of(h)].astype(F32) * tail[:, h : h + 1]).astype(BF16)
        put_state(parts_out, h, heads, dot_tn(write, scaled))
    parts_in[me] = parts_out[me]
    scatter("ctx", parts_out, parts_in, part_s, part_r)
    for d in range(QUAD):
        for copy in query_copies(d, spot, ring(spot, d, QUAD)):
            copy.start()

    def keys_arrived(d):
        for copy in key_copies(d, ring(z, -d, ROW), z):
            if d == 0:
                copy.wait()
            else:
                copy.wait_recv()

        @pl.when(x < last_row)
        def _():
            pass_on(d, 2 * SPAN, one_s, one_r).start()

    keys_arrived(0)

    seen = visible(doc, start)
    scores = dot_nt(read, write)
    for h in range(heads):
        mix = (head_decay(cum, cum_t, seen, h) * scores).astype(BF16)
        mixed_ref[:, cols_of(h)] = dot(mix, x_ref[:, cols_of(h)])

    collect("ctx", facts_ref, fact_s, fact_r)
    at = lax.broadcasted_iota(jnp.int32, (ctx, 1), 0)
    lane = lax.broadcasted_iota(jnp.int32, (ctx, DIM), 1)
    mine = me // (ctx // heads)
    total = jnp.sum(jnp.where(lane == mine, facts_ref[:, 2, :], 0.0), axis=1, keepdims=True)
    final = jnp.sum(jnp.where(lane == DIM - 1, facts_ref[:, 1, :], 0.0), axis=1, keepdims=True)
    factor = jnp.where(final < (at * length).astype(F32), jnp.exp(total), 0.0)
    factor_ref[...] = jnp.broadcast_to(factor, factor_ref.shape)

    for d in (1, 7, 2, 6):
        keys_arrived(d)
    collect("ctx", parts_in, part_s, part_r)
    chain(parts_in, linked, factor_ref, False)
    prior_ref[me] = linked[me]
    scatter("ctx", linked, prior_ref, link_s, link_r)
    for d in (3, 5, 4):
        keys_arrived(d)
    for d in range(QUAD):
        for copy in query_copies(d, ring(spot, -d, QUAD), spot):
            if d == 0:
                copy.wait()
            else:
                copy.wait_recv()

    first_key = half * QUERIES

    def keys_of(u):
        return pl.ds(pl.multiple_of(first_key + u * TK, TK), TK)

    def tile(j):
        return pl.ds(pl.multiple_of(j * TQ, TQ), TQ)

    for j in range(QUAD):
        cols = slice(j * TQ, (j + 1) * TQ)
        qt_ref[:, cols] = qg_ref[cols, :DIM].T
        gt_ref[:, cols] = qg_ref[cols, DIM:].T
        own = facts_ref[me - spot + j]
        own = jnp.concatenate([own[0:1, :], own[1:2, :]], axis=1).astype(jnp.int32)
        high = 2 * SPAN + first_key + j * TQ + lax.broadcasted_iota(jnp.int32, (1, TQ), 1)
        low_ref[0:1, cols] = jnp.maximum(own - (x - 2) * SPAN, high - (WINDOW - 1))
        low_ref[1:2, cols] = high
    stat_ref[0:1, :] = jnp.full((1, QUERIES), HIDDEN, F32)
    stat_ref[1:2, :] = jnp.zeros((1, QUERIES), F32)
    out_t[...] = jnp.zeros_like(out_t)
    dq_t[...] = jnp.zeros_like(dq_t)

    def score(u, j, edge):
        s = dot(kv_ref[keys_of(u), :DIM], qt_ref[:, tile(j)])
        at = first_key + u * TK + lax.broadcasted_iota(jnp.int32, (TK, TQ), 0)
        shown = at >= low_ref[0:1, tile(j)]
        if edge:
            shown = shown & (at <= low_ref[1:2, tile(j)])
        return jnp.where(shown, s, HIDDEN)

    def forward(u, j, values_t, edge):
        cols = tile(j)
        s = score(u, j, edge)
        top = stat_ref[0:1, cols]
        new = jnp.maximum(top, jnp.max(s, axis=0, keepdims=True))
        p = jnp.exp2((s - new) * SCALE2)
        keep = jnp.exp2((top - new) * SCALE2)
        stat_ref[0:1, cols] = new
        stat_ref[1:2, cols] = stat_ref[1:2, cols] * keep + jnp.sum(p, axis=0, keepdims=True)
        out_t[:, cols] = out_t[:, cols] * keep + dot(values_t, p.astype(BF16))

    def whole_forward(begin, end):
        @pl.loop(begin, end)
        def _(u):
            values_t = kv_ref[keys_of(u), DIM:].T
            for j in range(QUAD):
                forward(u, j, values_t, False)

    def tiles_of_edge(u):
        return (0, 2 * u + 2) if u < 2 else (2 * (u - 8), QUAD)

    def edge_forward(u):
        values_t = kv_ref[keys_of(u), DIM:].T

        @pl.loop(*tiles_of_edge(u))
        def _(j):
            forward(u, j, values_t, True)

    near_first, here_first = QUAD - 2 * half, 8 - 2 * half

    edge_forward(8)
    edge_forward(9)
    whole_forward(here_first, 8)

    collect("ctx", prior_ref, link_s, link_r)
    squares = jnp.zeros((length, 1), F32)
    inner = jnp.zeros((length, 1), F32)
    for h in range(heads):
        mixed = mixed_ref[:, cols_of(h)] + enter[:, h : h + 1] * dot(read, head_state(prior_ref, h, heads))
        mixed_ref[:, cols_of(h)] = mixed
        gated = mixed * gate_terms(gate_ref[:, cols_of(h)].astype(F32))[1]
        squares += jnp.sum(gated * gated, axis=1, keepdims=True)
        inner += jnp.sum(grad_ref[:, cols_of(h)].astype(F32) * gated, axis=1, keepdims=True)
    wide[:, 0:1] = squares
    wide[:, 1:2] = inner
    sums_out[...] = wide[...].T[:8]
    sums_in[head] = sums_out[...]
    spread("head", sums_out, sums_in, sum_s, sum_r)

    for d in (0, 1, 7, 2, 6, 3, 5, 4):

        @pl.when(x >= 1)
        def _():
            pass_on(d, 2 * SPAN, one_s, one_r).wait_recv()

        @pl.when((x >= 1) & (x < last_row) & wanted(ring(z, -d, ROW)))
        def _():
            pass_on(d, SPAN, two_s, two_r).start()

    @pl.when(x >= 1)
    def _():
        whole_forward(near_first, here_first)

    collect("head", sums_in, sum_s, sum_r)
    sums = sums_in[0]
    for i in range(1, crew):
        sums += sums_in[i]
    sums = jnp.concatenate([sums, jnp.zeros((DIM - 8, length), F32)], axis=0).T
    rms = lax.rsqrt(sums[:, 0:1] / width + EPSILON)
    pull = rms * rms * rms * sums[:, 1:2] / width
    for h in range(heads):
        cols = cols_of(h)
        mixed = mixed_ref[:, cols]
        gate = gate_ref[:, cols].astype(F32)
        sigma, swish = gate_terms(gate)
        gated = mixed * swish
        out_ref[:, cols] = (gated * rms).astype(BF16)
        dgated = rms * grad_ref[:, cols].astype(F32) - pull * gated
        dmixed = dgated * swish
        dmixed_ref[:, cols] = dmixed.astype(BF16)
        gate_grad_ref[:, cols] = (dgated * mixed * sigma * (1.0 + gate * (1.0 - sigma))).astype(BF16)
        put_state(back_out, h, heads, dot_tn(read, (enter[:, h : h + 1] * dmixed).astype(BF16)))
    back_in[me] = back_out[me]
    scatter("ctx", back_out, back_in, back_s, back_r)

    pairs = jnp.zeros_like(scores)
    read_part = jnp.zeros(read.shape, F32)
    for h in range(heads):
        cols = cols_of(h)
        decay = head_decay(cum, cum_t, seen, h)
        dmixed = dmixed_ref[:, cols]
        input_ref[:, cols] = dot_tn((decay * scores).astype(BF16), dmixed)
        pairs += decay * dot_nt(dmixed, x_ref[:, cols])
        entered = (enter[:, h : h + 1] * dmixed.astype(F32)).astype(BF16)
        read_part += dot_nt(entered, head_state(prior_ref, h, heads))
    pairs = pairs.astype(BF16)
    share = length // crew
    maps[:, :, :DIM] = dot_tn(pairs, read).reshape(crew, share, DIM)
    maps[:, :, DIM:] = (read_part + dot(pairs, write)).reshape(crew, share, DIM)

    collect("ctx", back_in, back_s, back_r)
    chain(back_in, relinked, factor_ref, True)
    after_ref[me] = relinked[me]
    scatter("ctx", relinked, after_ref, relink_s, relink_r)

    for d in (0, 1, 7, 2, 6, 3, 5, 4):

        @pl.when((x >= 2) & wanted(ring(z, -d, ROW)))
        def _():
            pass_on(d, SPAN, two_s, two_r).wait_recv()

    @pl.when(x >= 2)
    def _():
        whole_forward(2, near_first)
        edge_forward(0)
        edge_forward(1)

    for j in range(QUAD):
        cols = slice(j * TQ, (j + 1) * TQ)
        total = stat_ref[1:2, cols]
        attended = out_t[:, cols] / total
        og_ref[cols, :DIM] = attended.T.astype(BF16)
        stat_ref[2:3, cols] = stat_ref[0:1, cols] * SCALE2 + jnp.log2(total)
        stat_ref[3:4, cols] = jnp.sum(gt_ref[:, cols].astype(F32) * attended, axis=0, keepdims=True)
    for d in range(QUAD):
        result_copy(0, d, spot, ring(spot, d, QUAD)).start()

    def backward(u, j, edge):
        cols = tile(j)
        p = jnp.exp2(score(u, j, edge) * SCALE2 - stat_ref[2:3, cols])
        dp = dot(kv_ref[keys_of(u), DIM:], gt_ref[:, cols])
        p_ref[:, cols] = p.astype(BF16)
        ds_ref[:, cols] = (p * (dp - stat_ref[3:4, cols])).astype(BF16)

    def gather_backward(u):
        dq_t[...] += dot(kv_ref[keys_of(u), :DIM].T, ds_ref[...])
        return dot(ds_ref[...], qg_ref[:, :DIM]) * SCALE, dot(p_ref[...], qg_ref[:, DIM:])

    def whole_backward(begin, end, emit):
        @pl.loop(begin, end)
        def _(u):
            for j in range(QUAD):
                backward(u, j, False)
            emit(u, *gather_backward(u))

    def edge_backward(u, emit):
        begin, end = tiles_of_edge(u)
        if end - begin < QUAD:
            p_ref[...] = jnp.zeros_like(p_ref)
            ds_ref[...] = jnp.zeros_like(ds_ref)

        @pl.loop(begin, end)
        def _(j):
            backward(u, j, True)

        emit(u, *gather_backward(u))

    def blocks_of(u, dk, dv):
        b = lax.rem(2 * u + QUAD * half, ROW)
        both = jnp.concatenate([dk, dv], axis=1)
        return (b, both[:TOK]), (b + 1, both[TOK:])

    def emit_far(u, dk, dv):
        for b, part in blocks_of(u, dk, dv):
            far_out[b] = part.astype(BF16)
            far(b).start()

    def pass_near(b, part):
        more = (x < last_row) & wanted(b)
        near_out[b] = part.astype(BF16)

        @pl.when(more)
        def _():
            far(b).wait_recv()
            near_out[b] = (part + far_in[b].astype(F32)).astype(BF16)

        near(b).start()

    def emit_near(u, dk, dv):
        for b, part in blocks_of(u, dk, dv):
            pass_near(b, part)

    def pass_row(b, part):
        row_out[b] = part.astype(BF16)

        @pl.when(x < last_row)
        def _():
            near(b).wait_recv()
            row_out[b] = (part + near_in[b].astype(F32)).astype(BF16)

        @pl.when(b != z)
        def _():
            row_copy(ring(b, -z, ROW), b).start()

        @pl.when(b == z)
        def _():
            row_in[z] = row_out[b]

    def emit_row(u, dk, dv):
        for b, part in blocks_of(u, dk, dv):
            pass_row(b, part)

    @pl.when(x >= 2)
    def _():
        edge_backward(0, emit_far)
        edge_backward(1, emit_far)
        whole_backward(2, near_first, emit_far)

    @pl.when(x >= 1)
    def _():
        whole_backward(near_first, here_first, emit_near)

    collect("ctx", after_ref, relink_s, relink_r)
    write_part = maps[:, :, :DIM].reshape(length, DIM)
    for h in range(heads):
        cols = cols_of(h)
        t = tail[:, h : h + 1]
        after = head_state(after_ref, h, heads)
        input_grad_ref[:, cols] = (input_ref[:, cols] + t * dot(write, after)).astype(BF16)
        write_part += dot_nt((x_ref[:, cols].astype(F32) * t).astype(BF16), after)

    maps[:, :, :DIM] = write_part.reshape(crew, share, DIM)
    maps_in[head] = maps[head]
    scatter("head", maps, maps_in, map_s, map_r)

    whole_backward(here_first, 8, emit_row)
    edge_backward(8, emit_row)
    edge_backward(9, emit_row)

    for j in range(QUAD):
        cols = slice(j * TQ, (j + 1) * TQ)
        og_ref[cols, DIM:] = (dq_t[:, cols] * SCALE).T.astype(BF16)
    for d in range(QUAD):
        result_copy(1, d, spot, ring(spot, d, QUAD)).start()

    @pl.when(half == 0)
    def _():
        @pl.loop(QUAD, ROW)
        def _(b):
            pass_row(b, jnp.zeros((TOK, 2 * DIM), F32))

    collect("head", maps_in, map_s, map_r)
    added = maps_in[0]
    for i in range(1, crew):
        added += maps_in[i]
    maps_sum[...] = added.astype(BF16)
    maps_all[head] = maps_sum[...]
    spread("head", maps_sum, maps_all, all_s, all_r)

    for d in range(1, ROW):
        z_from = ring(z, -d, ROW)
        send(row_out.at[z], row_in.at[z_from], row_s.at[d], row_r.at[d], ctx=x * ROW + z_from).wait_recv()
    for a in range(QUAD):
        both = row_in[a].astype(F32) + row_in[QUAD + a].astype(F32)
        key_grad_ref[:, cols_of(a)] = both[:, :DIM].astype(BF16)
        value_grad_ref[:, cols_of(a)] = both[:, DIM:].astype(BF16)

    collect("head", maps_all, all_s, all_r)
    both = maps_all[...].reshape(length, 2 * DIM)
    write_grad_ref[...] = both[:, :DIM]
    read_grad_ref[...] = both[:, DIM:]

    for i in range(2):
        for d in range(QUAD):
            copy = result_copy(i, d, ring(spot, -d, QUAD), spot)
            if d == 0:
                copy.wait()
            else:
                copy.wait_recv()

    for d in range(1, ROW):
        for copy in key_copies(d, z, ring(z, d, ROW)):
            copy.wait_send()
        row_copy(d, ring(z, d, ROW)).wait_send()
    for d in range(1, QUAD):
        for copy in query_copies(d, spot, ring(spot, d, QUAD)):
            copy.wait_send()
        for i in range(2):
            result_copy(i, d, spot, ring(spot, d, QUAD)).wait_send()

    @pl.loop(0, ROW)
    def _(d):
        @pl.when(x < last_row)
        def _():
            pass_on(d, 2 * SPAN, one_s, one_r).wait_send()

        @pl.when((x >= 1) & (x < last_row) & wanted(ring(z, -d, ROW)))
        def _():
            pass_on(d, SPAN, two_s, two_r).wait_send()

        @pl.when((x >= 2) & wanted(d))
        def _():
            far(d).wait_send()

        @pl.when(x >= 1)
        def _():
            near(d).wait_send()

    settle("ctx", fact, fact_s, fact_r)
    settle("ctx", parts_out.at[0], part_s, part_r)
    settle("ctx", linked.at[0], link_s, link_r)
    settle("ctx", back_out.at[0], back_s, back_r)
    settle("ctx", relinked.at[0], relink_s, relink_r)
    settle("head", sums_out, sum_s, sum_r)
    settle("head", maps.at[0], map_s, map_r)
    settle("head", maps_sum, all_s, all_r)


def deliver_kernel(*refs):
    n = len(refs) // 2
    for src, dst in zip(refs[:n], refs[n:]):
        dst[...] = src[...]


def body(
    ssm_input,
    gate_input,
    write_map,
    read_map,
    log_decay,
    doc_start,
    ssm_grad,
    att_queries,
    att_keys,
    att_values,
    att_grad,
):
    ctx, crew = lax.axis_size("ctx"), lax.axis_size("head")
    length, width = ssm_input.shape
    heads = width // DIM
    flat, tall, attended = (length, width), (length, DIM), att_queries.shape
    part = (ctx, heads * DIM // ctx, DIM)
    block = (ROW, TOK, 2 * DIM)
    share = (crew, length // crew, 2 * DIM)
    outs = [shape(s, BF16) for s in (flat, attended, flat, flat, tall, tall, attended, attended, attended)]
    vmem, stay = pl.BlockSpec(memory_space=pltpu.VMEM), pl.BlockSpec(memory_space=pl.ANY)
    scratch = [
        ((3 * SPAN, 2 * DIM), BF16), ((QUERIES, 2 * DIM), BF16), ((QUERIES, 2 * DIM), BF16),
        ((ctx, 8, DIM), F32), ((ctx, DIM), F32), ((8, DIM), F32), (tall, F32), (flat, F32), (flat, BF16), (flat, F32),
        *[(part, BF16)] * 8,
        ((8, length), F32), ((crew, 8, length), F32), (share, F32), (share, F32), (share[1:], BF16), (share, BF16),
        *[(block, BF16)] * 6,
        ((DIM, QUERIES), BF16), ((DIM, QUERIES), BF16), ((8, QUERIES), F32), ((8, QUERIES), jnp.int32),
        ((DIM, QUERIES), F32), ((DIM, QUERIES), F32), ((TK, QUERIES), BF16), ((TK, QUERIES), BF16),
    ]
    sems = [(ROW, 2)] * 2 + [(QUAD, 2)] * 2 + [(ROW,)] * 4 + [(QUAD, 2)] * 2 + [(ROW,)] * 6
    sems += [(ctx,)] * 10 + [(crew,)] * 6
    found = pl.pallas_call(
        functools.partial(mixer_kernel, width * crew),
        out_shape=tuple(outs),
        in_specs=[vmem] * 7 + [stay] * 4,
        out_specs=(vmem,) * len(outs),
        scratch_shapes=[pltpu.VMEM(s, t) for s, t in scratch] + [pltpu.SemaphoreType.DMA(s) for s in sems],
        compiler_params=pltpu.CompilerParams(
            collective_id=0, has_side_effects=True, vmem_limit_bytes=VMEM_LIMIT
        ),
    )(
        doc_start.reshape(2, length // 2), log_decay, ssm_input, gate_input, ssm_grad, write_map, read_map,
        att_queries, att_keys, att_values, att_grad,
    )
    return pl.pallas_call(
        deliver_kernel,
        out_shape=tuple(outs),
        in_specs=[vmem] * len(outs),
        out_specs=(vmem,) * len(outs),
    )(*found)


def solution(mesh):
    tokens, both = P("ctx", None), P("ctx", "head")
    in_specs = (both, both, tokens, tokens, both, P("ctx"), both, both, both, both, both)
    out_specs = (both, both, both, both, tokens, tokens, both, both, both)
    return jax.shard_map(body, mesh=mesh, in_specs=in_specs, out_specs=out_specs, check_vma=False)
```

time: 246 us -> 174 us (0.71)
  Pallas kernels: 232 us -> 172 us
  local copies, waits for them, and re-layouts: 12.2 us -> 1.49 us
    pallas_call x3 -> x2, Pallas kernels: 232 us -> 172 us  [the longest x1 168 us: body(): pl.pallas_call(functools.partial(mixer_kernel, width * crew), out_shape=t...]
    unnamed x20 -> x1, local copies, waits for them, and re-layouts: 12.2 us -> 1.49 us
where the time goes in v3:
time: 174 us
  Pallas kernels  172 us (99%)
    pallas_call x1, Pallas kernels, body(): pl.pallas_call(functools.partial(mixer_kernel, width * crew), out_shape=t...  168 us

profile of v3, /device:TPU:2, one launch (start us, length us, event | category | flops | bytes accessed | tf_op | source)
XLA Modules:
  0.0 173.7 jit_solution(13939626303418791145)
XLA Ops:
  0.6 1.5 copy.20.rate_ref
  2.1 168.3 %shard_map.178 = (bf16[256,1024]{1,0:T(8,128)(2,1)}, bf16[256,512]{1,0:T(8,128)(2,1)}, bf16[256,1024]{1,0:T(8,128)(2,1)}, bf16[256,1024]{1,0:T(8,128)(2,1)}, bf1...) custom-call(s32[2,128]{1,0:T(2,128)} %bitcast.1, ...), custom_call_target="tpu_custom_call" | custom-call | tf_op jit(solution)/shard_map/pallas_call | solution.py:698
  170.4 3.2 %shard_map.179 = (bf16[256,1024]{1,0:T(8,128)(2,1)}, bf16[256,512]{1,0:T(8,128)(2,1)}, bf16[256,1024]{1,0:T(8,128)(2,1)}, bf16[256,1024]{1,0:T(8,128)(2,1)}, bf1...) custom-call(bf16[256,1024]{1,0:T(8,128)(2,1)} %get-tuple-element.18., ...), custom_call_target="tpu_custom_call" | custom-call | tf_op jit(solution)/shard_map/pallas_call | solution.py:711

commit v4 on v3

--- a/solution.py
+++ b/solution.py
@@ -68,7 +68,9 @@
                 barrier, inc=1, device_id={axis: ring(me, d, size)}, device_id_type=MESH
             )
 
-    pl.semaphore_wait(barrier, ctx + head - 2)
+
+def await_greetings():
+    pl.semaphore_wait(pltpu.get_barrier_semaphore(), lax.axis_size("ctx") + lax.axis_size("head") - 2)
 
 
 def scatter(axis, src, dst, sent, arrived):
@@ -170,18 +172,20 @@
 
 
 HALVES = (slice(0, DIM), slice(DIM, 2 * DIM))
+NEAREST = (0, 1, 7, 2, 6, 3, 5, 4)
 
 
 def mixer_kernel(
     width, doc_ref, rate_ref, x_ref, gate_ref, grad_ref, write_ref, read_ref, q_ref, k_ref, v_ref, g_ref,
     out_ref, window_ref, input_grad_ref, gate_grad_ref, write_grad_ref, read_grad_ref,
     query_grad_ref, key_grad_ref, value_grad_ref,
-    kv_ref, qg_ref, og_ref, facts_ref, factor_ref, fact, wide, mixed_ref, dmixed_ref, input_ref,
+    kv_ref, relay_ref, qg_ref, og_ref, facts_ref, factor_ref, fact, wide, turned, mixed_ref, dmixed_ref, input_ref,
     parts_out, parts_in, linked, prior_ref, back_out, back_in, relinked, after_ref,
     sums_out, sums_in, maps, maps_in, maps_sum, maps_all,
-    far_out, far_in, near_out, near_in, row_out, row_in,
+    far_out, far_in, bend_ref, near_out, near_in, row_out, row_in,
     qt_ref, gt_ref, stat_ref, low_ref, out_t, dq_t, p_ref, ds_ref,
-    kv_s, kv_r, qg_s, qg_r, one_s, one_r, two_s, two_r, og_s, og_r, far_s, far_r, near_s, near_r, row_s, row_r,
+    kv_s, kv_r, qg_s, qg_r, one_s, one_r, two_s, two_r, turn_s, turn_r, og_s, og_r,
+    far_s, far_r, bend_s, bend_r, near_s, near_r, row_s, row_r,
     fact_s, fact_r, part_s, part_r, link_s, link_r, back_s, back_r, relink_s, relink_r,
     sum_s, sum_r, map_s, map_r, all_s, all_r,
 ):
@@ -191,7 +195,7 @@
     spot = lax.rem(me, QUAD)
     half = z // QUAD
     last_row = ctx // ROW - 1
-    length, heads = rate_ref.shape
+    heads, length = rate_ref.shape
     start = me * length
 
     def key_copies(d, z_from, z_to):
@@ -216,13 +220,37 @@
                 out.append(send(src, dst, qg_s.at[d, i], qg_r.at[d, i], ctx=me - spot + to))
         return out
 
-    def pass_on(d, first, sent, arrived):
-        z_from = ring(z, -d, ROW)
+    def row_at(by):
+        return lax.rem(me + by * ROW + ctx, ctx)
+
+    def one_on(b):
         return send(
-            kv_ref.at[rows_of(first, z_from), :],
-            kv_ref.at[rows_of(first - SPAN, z_from), :],
-            sent.at[d], arrived.at[d], ctx=lax.rem(me + ROW, ctx),
+            kv_ref.at[rows_of(2 * SPAN, b), :], kv_ref.at[rows_of(SPAN, b), :],
+            one_s.at[b], one_r.at[b], ctx=row_at(1),
         )
+
+    def two_on(b):
+        return send(
+            kv_ref.at[rows_of(2 * SPAN, b), :], kv_ref.at[rows_of(0, b), :],
+            two_s.at[b], two_r.at[b], ctx=row_at(2),
+        )
+
+    def turn_in(b):
+        return send(
+            kv_ref.at[rows_of(2 * SPAN, b), :], relay_ref.at[lax.rem(b, QUAD)],
+            turn_s.at[b], turn_r.at[b], ctx=row_at(-1),
+        )
+
+    def turn_out(b):
+        return send(
+            relay_ref.at[lax.rem(b, QUAD)], kv_ref.at[rows_of(0, b), :],
+            two_s.at[b], two_r.at[b], ctx=row_at(-1),
+        )
+
+    def relayed(b):
+        return (z < QUAD) & (b >= QUAD)
+
+    relays = (x == last_row) | (x + 1 < last_row - 1)
 
     def result_copy(i, d, a, to):
         src = og_ref.at[rows_of(0, to), HALVES[i]]
@@ -232,10 +260,16 @@
         return send(src, dst, og_s.at[d, i], og_r.at[d, i], ctx=me - spot + to)
 
     def far(b):
-        return send(far_out.at[b], far_in.at[b], far_s.at[b], far_r.at[b], ctx=lax.rem(me + ctx - ROW, ctx))
+        return send(far_out.at[b], far_in.at[b], far_s.at[b], far_r.at[b], ctx=row_at(-2))
+
+    def bend_in(b):
+        return send(far_out.at[b], bend_ref.at[lax.rem(b, QUAD)], bend_s.at[b], bend_r.at[b], ctx=row_at(1))
+
+    def bend_out(b):
+        return send(bend_ref.at[lax.rem(b, QUAD)], far_in.at[b], far_s.at[b], far_r.at[b], ctx=row_at(1))
 
     def near(b):
-        return send(near_out.at[b], near_in.at[b], near_s.at[b], near_r.at[b], ctx=lax.rem(me + ctx - ROW, ctx))
+        return send(near_out.at[b], near_in.at[b], near_s.at[b], near_r.at[b], ctx=row_at(-1))
 
     def row_copy(d, b):
         return send(row_out.at[b], row_in.at[z], row_s.at[d], row_r.at[d], ctx=x * ROW + b)
@@ -243,25 +277,20 @@
     def wanted(b):
         return (z < QUAD) | (b >= QUAD)
 
+    greet()
+
     docs = doc_ref[...].astype(F32)
-    rate = rate_ref[...]
+    row = lax.broadcasted_iota(jnp.int32, (length, length), 0)
+    col = lax.broadcasted_iota(jnp.int32, (length, length), 1)
+    cum_t = dot(rate_ref[...], (row <= col).astype(F32), EXACT)
+    turned[...] = jnp.zeros_like(turned)
+    turned[:heads, :] = cum_t
+    cum = turned[...].T[:, :heads]
     fact[...] = jnp.zeros_like(fact)
     fact[0:2, :] = docs
-    fact[2:3, :heads] = jnp.sum(rate, axis=0, keepdims=True)
+    fact[2:3, :heads] = cum[length - 1 : length, :]
     facts_ref[me] = fact[...]
 
-    greet()
-    for d in range(ROW):
-        for copy in key_copies(d, z, ring(z, d, ROW)):
-            copy.start()
-    spread("ctx", fact, facts_ref, fact_s, fact_r)
-
-    row = lax.broadcasted_iota(jnp.int32, (length, length), 0)
-    col = lax.broadcasted_iota(jnp.int32, (length, length), 1)
-    cum = dot((row >= col).astype(F32), rate, EXACT)
-    wide[...] = jnp.zeros_like(wide)
-    wide[:, :heads] = cum
-    cum_t = wide[...].T[:heads]
     doc = jnp.concatenate([column(docs[0:1, :]), column(docs[1:2, :])], axis=0)
     tail = tail_decay(cum, doc)
     enter = jnp.where(doc < start.astype(F32), jnp.exp(cum), 0.0)
@@ -270,23 +299,12 @@
         scaled = (x_ref[:, cols_of(h)].astype(F32) * tail[:, h : h + 1]).astype(BF16)
         put_state(parts_out, h, heads, dot_tn(write, scaled))
     parts_in[me] = parts_out[me]
+    await_greetings()
     scatter("ctx", parts_out, parts_in, part_s, part_r)
-    for d in range(QUAD):
-        for copy in query_copies(d, spot, ring(spot, d, QUAD)):
+    spread("ctx", fact, facts_ref, fact_s, fact_r)
+    for d in NEAREST[:5]:
+        for copy in key_copies(d, z, ring(z, d, ROW)):
             copy.start()
-
-    def keys_arrived(d):
-        for copy in key_copies(d, ring(z, -d, ROW), z):
-            if d == 0:
-                copy.wait()
-            else:
-                copy.wait_recv()
-
-        @pl.when(x < last_row)
-        def _():
-            pass_on(d, 2 * SPAN, one_s, one_r).start()
-
-    keys_arrived(0)
 
     seen = visible(doc, start)
     scores = dot_nt(read, write)
@@ -303,84 +321,39 @@
     factor = jnp.where(final < (at * length).astype(F32), jnp.exp(total), 0.0)
     factor_ref[...] = jnp.broadcast_to(factor, factor_ref.shape)
 
-    for d in (1, 7, 2, 6):
-        keys_arrived(d)
     collect("ctx", parts_in, part_s, part_r)
     chain(parts_in, linked, factor_ref, False)
     prior_ref[me] = linked[me]
     scatter("ctx", linked, prior_ref, link_s, link_r)
-    for d in (3, 5, 4):
-        keys_arrived(d)
+    for d in NEAREST[5:]:
+        for copy in key_copies(d, z, ring(z, d, ROW)):
+            copy.start()
     for d in range(QUAD):
-        for copy in query_copies(d, ring(spot, -d, QUAD), spot):
+        for copy in query_copies(d, spot, ring(spot, d, QUAD)):
+            copy.start()
+
+    def keys_arrived(d):
+        b = ring(z, -d, ROW)
+        for copy in key_copies(d, b, z):
             if d == 0:
                 copy.wait()
             else:
                 copy.wait_recv()
 
-    first_key = half * QUERIES
-
-    def keys_of(u):
-        return pl.ds(pl.multiple_of(first_key + u * TK, TK), TK)
-
-    def tile(j):
-        return pl.ds(pl.multiple_of(j * TQ, TQ), TQ)
-
-    for j in range(QUAD):
-        cols = slice(j * TQ, (j + 1) * TQ)
-        qt_ref[:, cols] = qg_ref[cols, :DIM].T
-        gt_ref[:, cols] = qg_ref[cols, DIM:].T
-        own = facts_ref[me - spot + j]
-        own = jnp.concatenate([own[0:1, :], own[1:2, :]], axis=1).astype(jnp.int32)
-        high = 2 * SPAN + first_key + j * TQ + lax.broadcasted_iota(jnp.int32, (1, TQ), 1)
-        low_ref[0:1, cols] = jnp.maximum(own - (x - 2) * SPAN, high - (WINDOW - 1))
-        low_ref[1:2, cols] = high
-    stat_ref[0:1, :] = jnp.full((1, QUERIES), HIDDEN, F32)
-    stat_ref[1:2, :] = jnp.zeros((1, QUERIES), F32)
-    out_t[...] = jnp.zeros_like(out_t)
-    dq_t[...] = jnp.zeros_like(dq_t)
-
-    def score(u, j, edge):
-        s = dot(kv_ref[keys_of(u), :DIM], qt_ref[:, tile(j)])
-        at = first_key + u * TK + lax.broadcasted_iota(jnp.int32, (TK, TQ), 0)
-        shown = at >= low_ref[0:1, tile(j)]
-        if edge:
-            shown = shown & (at <= low_ref[1:2, tile(j)])
-        return jnp.where(shown, s, HIDDEN)
-
-    def forward(u, j, values_t, edge):
-        cols = tile(j)
-        s = score(u, j, edge)
-        top = stat_ref[0:1, cols]
-        new = jnp.maximum(top, jnp.max(s, axis=0, keepdims=True))
-        p = jnp.exp2((s - new) * SCALE2)
-        keep = jnp.exp2((top - new) * SCALE2)
-        stat_ref[0:1, cols] = new
-        stat_ref[1:2, cols] = stat_ref[1:2, cols] * keep + jnp.sum(p, axis=0, keepdims=True)
-        out_t[:, cols] = out_t[:, cols] * keep + dot(values_t, p.astype(BF16))
-
-    def whole_forward(begin, end):
-        @pl.loop(begin, end)
-        def _(u):
-            values_t = kv_ref[keys_of(u), DIM:].T
-            for j in range(QUAD):
-                forward(u, j, values_t, False)
-
-    def tiles_of_edge(u):
-        return (0, 2 * u + 2) if u < 2 else (2 * (u - 8), QUAD)
-
-    def edge_forward(u):
-        values_t = kv_ref[keys_of(u), DIM:].T
-
-        @pl.loop(*tiles_of_edge(u))
-        def _(j):
-            forward(u, j, values_t, True)
-
-    near_first, here_first = QUAD - 2 * half, 8 - 2 * half
-
-    edge_forward(8)
-    edge_forward(9)
-    whole_forward(here_first, 8)
+        @pl.when((x < last_row - 1) & relayed(b))
+        def _():
+            turn_in(b).start()
+
+        @pl.when(x < last_row)
+        def _():
+            one_on(b).start()
+
+        @pl.when((x < last_row - 1) & wanted(b) & jnp.logical_not(relayed(b)))
+        def _():
+            two_on(b).start()
+
+    for d in NEAREST[:5]:
+        keys_arrived(d)
 
     collect("ctx", prior_ref, link_s, link_r)
     squares = jnp.zeros((length, 1), F32)
@@ -391,25 +364,15 @@
         gated = mixed * gate_terms(gate_ref[:, cols_of(h)].astype(F32))[1]
         squares += jnp.sum(gated * gated, axis=1, keepdims=True)
         inner += jnp.sum(grad_ref[:, cols_of(h)].astype(F32) * gated, axis=1, keepdims=True)
+    wide[...] = jnp.zeros_like(wide)
     wide[:, 0:1] = squares
     wide[:, 1:2] = inner
     sums_out[...] = wide[...].T[:8]
     sums_in[head] = sums_out[...]
     spread("head", sums_out, sums_in, sum_s, sum_r)
 
-    for d in (0, 1, 7, 2, 6, 3, 5, 4):
-
-        @pl.when(x >= 1)
-        def _():
-            pass_on(d, 2 * SPAN, one_s, one_r).wait_recv()
-
-        @pl.when((x >= 1) & (x < last_row) & wanted(ring(z, -d, ROW)))
-        def _():
-            pass_on(d, SPAN, two_s, two_r).start()
-
-    @pl.when(x >= 1)
-    def _():
-        whole_forward(near_first, here_first)
+    for d in NEAREST[5:]:
+        keys_arrived(d)
 
     collect("head", sums_in, sum_s, sum_r)
     sums = sums_in[0]
@@ -433,6 +396,13 @@
     back_in[me] = back_out[me]
     scatter("ctx", back_out, back_in, back_s, back_r)
 
+    @pl.loop(QUAD, ROW)
+    def _(b):
+        @pl.when(relays & relayed(b))
+        def _():
+            turn_in(b).wait_recv()
+            turn_out(b).start()
+
     pairs = jnp.zeros_like(scores)
     read_part = jnp.zeros(read.shape, F32)
     for h in range(heads):
@@ -453,14 +423,94 @@
     after_ref[me] = relinked[me]
     scatter("ctx", relinked, after_ref, relink_s, relink_r)
 
-    for d in (0, 1, 7, 2, 6, 3, 5, 4):
-
-        @pl.when((x >= 2) & wanted(ring(z, -d, ROW)))
-        def _():
-            pass_on(d, SPAN, two_s, two_r).wait_recv()
+    for d in range(QUAD):
+        for copy in query_copies(d, ring(spot, -d, QUAD), spot):
+            if d == 0:
+                copy.wait()
+            else:
+                copy.wait_recv()
+
+    first_key = half * QUERIES
+
+    def keys_of(u):
+        return pl.ds(pl.multiple_of(first_key + u * TK, TK), TK)
+
+    def tile(j):
+        return pl.ds(pl.multiple_of(j * TQ, TQ), TQ)
+
+    for j in range(QUAD):
+        cols = slice(j * TQ, (j + 1) * TQ)
+        qt_ref[:, cols] = qg_ref[cols, :DIM].T
+        gt_ref[:, cols] = qg_ref[cols, DIM:].T
+        own = facts_ref[me - spot + j]
+        own = jnp.concatenate([own[0:1, :], own[1:2, :]], axis=1).astype(jnp.int32)
+        high = 2 * SPAN + first_key + j * TQ + lax.broadcasted_iota(jnp.int32, (1, TQ), 1)
+        low_ref[0:1, cols] = jnp.maximum(own - (x - 2) * SPAN, high - (WINDOW - 1))
+        low_ref[1:2, cols] = high
+    stat_ref[0:1, :] = jnp.full((1, QUERIES), HIDDEN, F32)
+    stat_ref[1:2, :] = jnp.zeros((1, QUERIES), F32)
+    out_t[...] = jnp.zeros_like(out_t)
+    dq_t[...] = jnp.zeros_like(dq_t)
+
+    def score(u, j, edge):
+        s = dot(kv_ref[keys_of(u), :DIM], qt_ref[:, tile(j)])
+        at = first_key + u * TK + lax.broadcasted_iota(jnp.int32, (TK, TQ), 0)
+        shown = at >= low_ref[0:1, tile(j)]
+        if edge:
+            shown = shown & (at <= low_ref[1:2, tile(j)])
+        return jnp.where(shown, s, HIDDEN)
+
+    def forward(u, j, values_t, edge):
+        cols = tile(j)
+        s = score(u, j, edge)
+        top = stat_ref[0:1, cols]
+        new = jnp.maximum(top, jnp.max(s, axis=0, keepdims=True))
+        p = jnp.exp2((s - new) * SCALE2)
+        keep = jnp.exp2((top - new) * SCALE2)
+        stat_ref[0:1, cols] = new
+        stat_ref[1:2, cols] = stat_ref[1:2, cols] * keep + jnp.sum(p, axis=0, keepdims=True)
+        out_t[:, cols] = out_t[:, cols] * keep + dot(values_t, p.astype(BF16))
+
+    def whole_forward(begin, end):
+        @pl.loop(begin, end)
+        def _(u):
+            values_t = kv_ref[keys_of(u), DIM:].T
+            for j in range(QUAD):
+                forward(u, j, values_t, False)
+
+    def tiles_of_edge(u):
+        return (0, 2 * u + 2) if u < 2 else (2 * (u - 8), QUAD)
+
+    def edge_forward(u):
+        values_t = kv_ref[keys_of(u), DIM:].T
+
+        @pl.loop(*tiles_of_edge(u))
+        def _(j):
+            forward(u, j, values_t, True)
+
+    near_first, here_first = QUAD - 2 * half, 8 - 2 * half
+
+    edge_forward(8)
+    edge_forward(9)
+
+    whole_forward(here_first, 8)
+
+    @pl.when(x >= 1)
+    def _():
+        @pl.loop(0, ROW)
+        def _(b):
+            one_on(b).wait_recv()
+
+        whole_forward(near_first, here_first)
 
     @pl.when(x >= 2)
     def _():
+        @pl.loop(0, ROW)
+        def _(b):
+            @pl.when(wanted(b))
+            def _():
+                two_on(b).wait_recv()
+
         whole_forward(2, near_first)
         edge_forward(0)
         edge_forward(1)
@@ -513,30 +563,32 @@
     def emit_far(u, dk, dv):
         for b, part in blocks_of(u, dk, dv):
             far_out[b] = part.astype(BF16)
-            far(b).start()
-
-    def pass_near(b, part):
-        more = (x < last_row) & wanted(b)
-        near_out[b] = part.astype(BF16)
-
-        @pl.when(more)
-        def _():
-            far(b).wait_recv()
-            near_out[b] = (part + far_in[b].astype(F32)).astype(BF16)
-
-        near(b).start()
+            direct = jnp.logical_not(relayed(b))
+            pl.when(direct)(far(b).start)
+            pl.when(relayed(b))(bend_in(b).start)
 
     def emit_near(u, dk, dv):
         for b, part in blocks_of(u, dk, dv):
-            pass_near(b, part)
+            near_out[b] = part.astype(BF16)
+            near(b).start()
 
     def pass_row(b, part):
-        row_out[b] = part.astype(BF16)
-
-        @pl.when(x < last_row)
+        two = (x < last_row - 1) & wanted(b)
+
+        @pl.when(two)
+        def _():
+            near(b).wait_recv()
+            far(b).wait_recv()
+            row_out[b] = (part + near_in[b].astype(F32) + far_in[b].astype(F32)).astype(BF16)
+
+        @pl.when((x < last_row) & jnp.logical_not(two))
         def _():
             near(b).wait_recv()
             row_out[b] = (part + near_in[b].astype(F32)).astype(BF16)
+
+        @pl.when(x == last_row)
+        def _():
+            row_out[b] = part.astype(BF16)
 
         @pl.when(b != z)
         def _():
@@ -552,13 +604,36 @@
 
     @pl.when(x >= 2)
     def _():
+        whole_backward(2, near_first, emit_far)
         edge_backward(0, emit_far)
         edge_backward(1, emit_far)
-        whole_backward(2, near_first, emit_far)
 
     @pl.when(x >= 1)
     def _():
         whole_backward(near_first, here_first, emit_near)
+
+    @pl.loop(QUAD, ROW)
+    def _(b):
+        @pl.when(relays & relayed(b))
+        def _():
+            bend_in(b).wait_recv()
+            bend_out(b).start()
+
+    whole_backward(here_first, 8, emit_row)
+    edge_backward(8, emit_row)
+    edge_backward(9, emit_row)
+
+    for j in range(QUAD):
+        cols = slice(j * TQ, (j + 1) * TQ)
+        og_ref[cols, DIM:] = (dq_t[:, cols] * SCALE).T.astype(BF16)
+    for d in range(QUAD):
+        result_copy(1, d, spot, ring(spot, d, QUAD)).start()
+
+    @pl.when(half == 0)
+    def _():
+        @pl.loop(QUAD, ROW)
+        def _(b):
+            pass_row(b, jnp.zeros((TOK, 2 * DIM), F32))
 
     collect("ctx", after_ref, relink_s, relink_r)
     write_part = maps[:, :, :DIM].reshape(length, DIM)
@@ -572,22 +647,6 @@
     maps[:, :, :DIM] = write_part.reshape(crew, share, DIM)
     maps_in[head] = maps[head]
     scatter("head", maps, maps_in, map_s, map_r)
-
-    whole_backward(here_first, 8, emit_row)
-    edge_backward(8, emit_row)
-    edge_backward(9, emit_row)
-
-    for j in range(QUAD):
-        cols = slice(j * TQ, (j + 1) * TQ)
-        og_ref[cols, DIM:] = (dq_t[:, cols] * SCALE).T.astype(BF16)
-    for d in range(QUAD):
-        result_copy(1, d, spot, ring(spot, d, QUAD)).start()
-
-    @pl.when(half == 0)
-    def _():
-        @pl.loop(QUAD, ROW)
-        def _(b):
-            pass_row(b, jnp.zeros((TOK, 2 * DIM), F32))
 
     collect("head", maps_in, map_s, map_r)
     added = maps_in[0]
@@ -629,22 +688,37 @@
             result_copy(i, d, spot, ring(spot, d, QUAD)).wait_send()
 
     @pl.loop(0, ROW)
-    def _(d):
+    def _(b):
+        direct = wanted(b) & jnp.logical_not(relayed(b))
+
         @pl.when(x < last_row)
         def _():
-            pass_on(d, 2 * SPAN, one_s, one_r).wait_send()
-
-        @pl.when((x >= 1) & (x < last_row) & wanted(ring(z, -d, ROW)))
-        def _():
-            pass_on(d, SPAN, two_s, two_r).wait_send()
-
-        @pl.when((x >= 2) & wanted(d))
-        def _():
-            far(d).wait_send()
+            one_on(b).wait_send()
+
+        @pl.when((x < last_row - 1) & direct)
+        def _():
+            two_on(b).wait_send()
+
+        @pl.when((x < last_row - 1) & relayed(b))
+        def _():
+            turn_in(b).wait_send()
+
+        @pl.when(relays & relayed(b))
+        def _():
+            turn_out(b).wait_send()
+            bend_out(b).wait_send()
+
+        @pl.when((x >= 2) & direct)
+        def _():
+            far(b).wait_send()
+
+        @pl.when((x >= 2) & relayed(b))
+        def _():
+            bend_in(b).wait_send()
 
         @pl.when(x >= 1)
         def _():
-            near(d).wait_send()
+            near(b).wait_send()
 
     settle("ctx", fact, fact_s, fact_r)
     settle("ctx", parts_out.at[0], part_s, part_r)
@@ -685,15 +759,15 @@
     outs = [shape(s, BF16) for s in (flat, attended, flat, flat, tall, tall, attended, attended, attended)]
     vmem, stay = pl.BlockSpec(memory_space=pltpu.VMEM), pl.BlockSpec(memory_space=pl.ANY)
     scratch = [
-        ((3 * SPAN, 2 * DIM), BF16), ((QUERIES, 2 * DIM), BF16), ((QUERIES, 2 * DIM), BF16),
-        ((ctx, 8, DIM), F32), ((ctx, DIM), F32), ((8, DIM), F32), (tall, F32), (flat, F32), (flat, BF16), (flat, F32),
+        ((3 * SPAN, 2 * DIM), BF16), ((QUAD, TOK, 2 * DIM), BF16), ((QUERIES, 2 * DIM), BF16), ((QUERIES, 2 * DIM), BF16),
+        ((ctx, 8, DIM), F32), ((ctx, DIM), F32), ((8, DIM), F32), (tall, F32), (tall[::-1], F32), (flat, F32), (flat, BF16), (flat, F32),
         *[(part, BF16)] * 8,
         ((8, length), F32), ((crew, 8, length), F32), (share, F32), (share, F32), (share[1:], BF16), (share, BF16),
-        *[(block, BF16)] * 6,
+        *[(block, BF16)] * 2, ((QUAD, TOK, 2 * DIM), BF16), *[(block, BF16)] * 4,
         ((DIM, QUERIES), BF16), ((DIM, QUERIES), BF16), ((8, QUERIES), F32), ((8, QUERIES), jnp.int32),
         ((DIM, QUERIES), F32), ((DIM, QUERIES), F32), ((TK, QUERIES), BF16), ((TK, QUERIES), BF16),
     ]
-    sems = [(ROW, 2)] * 2 + [(QUAD, 2)] * 2 + [(ROW,)] * 4 + [(QUAD, 2)] * 2 + [(ROW,)] * 6
+    sems = [(ROW, 2)] * 2 + [(QUAD, 2)] * 2 + [(ROW,)] * 6 + [(QUAD, 2)] * 2 + [(ROW,)] * 8
     sems += [(ctx,)] * 10 + [(crew,)] * 6
     found = pl.pallas_call(
         functools.partial(mixer_kernel, width * crew),
@@ -705,7 +779,7 @@
             collective_id=0, has_side_effects=True, vmem_limit_bytes=VMEM_LIMIT
         ),
     )(
-        doc_start.reshape(2, length // 2), log_decay, ssm_input, gate_input, ssm_grad, write_map, read_map,
+        doc_start.reshape(2, length // 2), log_decay.T, ssm_input, gate_input, ssm_grad, write_map, read_map,
         att_queries, att_keys, att_values, att_grad,
     )
     return pl.pallas_call(

time: 174 us -> 155 us (0.89)
  Pallas kernels: 172 us -> 154 us
    pallas_call x1, Pallas kernels: 168 us -> 151 us  [body(): pl.pallas_call(functools.partial(mixer_kernel, width * crew), out_shape=t...]
where the time goes in v4:
time: 155 us
  Pallas kernels  154 us (99%)
    pallas_call x1, Pallas kernels, body(): pl.pallas_call(functools.partial(mixer_kernel, width * crew), out_shape=t...  151 us
    pallas_call x1, Pallas kernels, body(): pl.pallas_call(deliver_kernel, out_shape=tuple(outs), in_specs=[vmem] * l...  3.25 us

profile of v4, /device:TPU:2, one launch (start us, length us, event | category | flops | bytes accessed | tf_op | source)
XLA Modules:
  0.0 154.5 jit_solution(943472694132564400)
XLA Ops:
  0.6 150.6 %shard_map.178 = (bf16[256,1024]{1,0:T(8,128)(2,1)}, bf16[256,512]{1,0:T(8,128)(2,1)}, bf16[256,1024]{1,0:T(8,128)(2,1)}, bf16[256,1024]{1,0:T(8,128)(2,1)}, bf1...) custom-call(s32[2,128]{1,0:T(2,128)} %bitcast.3, ...), custom_call_target="tpu_custom_call" | custom-call | tf_op jit(solution)/shard_map/pallas_call | solution.py:772
  151.3 3.2 %shard_map.179 = (bf16[256,1024]{1,0:T(8,128)(2,1)}, bf16[256,512]{1,0:T(8,128)(2,1)}, bf16[256,1024]{1,0:T(8,128)(2,1)}, bf16[256,1024]{1,0:T(8,128)(2,1)}, bf1...) custom-call(bf16[256,1024]{1,0:T(8,128)(2,1)} %get-tuple-element.18., ...), custom_call_target="tpu_custom_call" | custom-call | tf_op jit(solution)/shard_map/pallas_call | solution.py:785

commit v5 on v4

--- a/solution.py
+++ b/solution.py
@@ -403,6 +403,223 @@
             turn_in(b).wait_recv()
             turn_out(b).start()
 
+    for d in range(QUAD):
+        for copy in query_copies(d, ring(spot, -d, QUAD), spot):
+            if d == 0:
+                copy.wait()
+            else:
+                copy.wait_recv()
+
+    first_key = half * QUERIES
+
+    def keys_of(u):
+        return pl.ds(pl.multiple_of(first_key + u * TK, TK), TK)
+
+    def tile(j):
+        return pl.ds(pl.multiple_of(j * TQ, TQ), TQ)
+
+    for j in range(QUAD):
+        cols = slice(j * TQ, (j + 1) * TQ)
+        qt_ref[:, cols] = qg_ref[cols, :DIM].T
+        gt_ref[:, cols] = qg_ref[cols, DIM:].T
+        own = facts_ref[me - spot + j]
+        own = jnp.concatenate([own[0:1, :], own[1:2, :]], axis=1).astype(jnp.int32)
+        high = 2 * SPAN + first_key + j * TQ + lax.broadcasted_iota(jnp.int32, (1, TQ), 1)
+        low_ref[0:1, cols] = jnp.maximum(own - (x - 2) * SPAN, high - (WINDOW - 1))
+        low_ref[1:2, cols] = high
+    stat_ref[0:1, :] = jnp.full((1, QUERIES), HIDDEN, F32)
+    stat_ref[1:2, :] = jnp.zeros((1, QUERIES), F32)
+    out_t[...] = jnp.zeros_like(out_t)
+    dq_t[...] = jnp.zeros_like(dq_t)
+
+    def score(u, j, edge):
+        s = dot(kv_ref[keys_of(u), :DIM], qt_ref[:, tile(j)])
+        at = first_key + u * TK + lax.broadcasted_iota(jnp.int32, (TK, TQ), 0)
+        shown = at >= low_ref[0:1, tile(j)]
+        if edge:
+            shown = shown & (at <= low_ref[1:2, tile(j)])
+        return jnp.where(shown, s, HIDDEN)
+
+    def forward(u, j, values_t, edge):
+        cols = tile(j)
+        s = score(u, j, edge)
+        top = stat_ref[0:1, cols]
+        new = jnp.maximum(top, jnp.max(s, axis=0, keepdims=True))
+        p = jnp.exp2((s - new) * SCALE2)
+        keep = jnp.exp2((top - new) * SCALE2)
+        stat_ref[0:1, cols] = new
+        stat_ref[1:2, cols] = stat_ref[1:2, cols] * keep + jnp.sum(p, axis=0, keepdims=True)
+        out_t[:, cols] = out_t[:, cols] * keep + dot(values_t, p.astype(BF16))
+
+    def whole_forward(begin, end):
+        @pl.loop(begin, end)
+        def _(u):
+            values_t = kv_ref[keys_of(u), DIM:].T
+            for j in range(QUAD):
+                forward(u, j, values_t, False)
+
+    def tiles_of_edge(u):
+        return (0, 2 * u + 2) if u < 2 else (2 * (u - 8), QUAD)
+
+    def edge_forward(u):
+        values_t = kv_ref[keys_of(u), DIM:].T
+
+        @pl.loop(*tiles_of_edge(u))
+        def _(j):
+            forward(u, j, values_t, True)
+
+    near_first, here_first = QUAD - 2 * half, 8 - 2 * half
+
+    edge_forward(8)
+    edge_forward(9)
+
+    whole_forward(here_first, 8)
+
+    @pl.when(x >= 1)
+    def _():
+        @pl.loop(0, ROW)
+        def _(b):
+            one_on(b).wait_recv()
+
+        whole_forward(near_first, here_first)
+
+    collect("ctx", back_in, back_s, back_r)
+    chain(back_in, relinked, factor_ref, True)
+    after_ref[me] = relinked[me]
+    scatter("ctx", relinked, after_ref, relink_s, relink_r)
+
+    @pl.when(x >= 2)
+    def _():
+        @pl.loop(0, ROW)
+        def _(b):
+            @pl.when(wanted(b))
+            def _():
+                two_on(b).wait_recv()
+
+        whole_forward(2, near_first)
+        edge_forward(0)
+        edge_forward(1)
+
+    for j in range(QUAD):
+        cols = slice(j * TQ, (j + 1) * TQ)
+        total = stat_ref[1:2, cols]
+        attended = out_t[:, cols] / total
+        og_ref[cols, :DIM] = attended.T.astype(BF16)
+        stat_ref[2:3, cols] = stat_ref[0:1, cols] * SCALE2 + jnp.log2(total)
+        stat_ref[3:4, cols] = jnp.sum(gt_ref[:, cols].astype(F32) * attended, axis=0, keepdims=True)
+    for d in range(QUAD):
+        result_copy(0, d, spot, ring(spot, d, QUAD)).start()
+
+    def backward(u, j, edge):
+        cols = tile(j)
+        p = jnp.exp2(score(u, j, edge) * SCALE2 - stat_ref[2:3, cols])
+        dp = dot(kv_ref[keys_of(u), DIM:], gt_ref[:, cols])
+        p_ref[:, cols] = p.astype(BF16)
+        ds_ref[:, cols] = (p * (dp - stat_ref[3:4, cols])).astype(BF16)
+
+    def gather_backward(u):
+        dq_t[...] += dot(kv_ref[keys_of(u), :DIM].T, ds_ref[...])
+        return dot(ds_ref[...], qg_ref[:, :DIM]) * SCALE, dot(p_ref[...], qg_ref[:, DIM:])
+
+    def whole_backward(begin, end, emit):
+        @pl.loop(begin, end)
+        def _(u):
+            for j in range(QUAD):
+                backward(u, j, False)
+            emit(u, *gather_backward(u))
+
+    def edge_backward(u, emit):
+        begin, end = tiles_of_edge(u)
+        if end - begin < QUAD:
+            p_ref[...] = jnp.zeros_like(p_ref)
+            ds_ref[...] = jnp.zeros_like(ds_ref)
+
+        @pl.loop(begin, end)
+        def _(j):
+            backward(u, j, True)
+
+        emit(u, *gather_backward(u))
+
+    def blocks_of(u, dk, dv):
+        b = lax.rem(2 * u + QUAD * half, ROW)
+        both = jnp.concatenate([dk, dv], axis=1)
+        return (b, both[:TOK]), (b + 1, both[TOK:])
+
+    def emit_far(u, dk, dv):
+        for b, part in blocks_of(u, dk, dv):
+            far_out[b] = part.astype(BF16)
+            direct = jnp.logical_not(relayed(b))
+            pl.when(direct)(far(b).start)
+            pl.when(relayed(b))(bend_in(b).start)
+
+    def emit_near(u, dk, dv):
+        for b, part in blocks_of(u, dk, dv):
+            near_out[b] = part.astype(BF16)
+            near(b).start()
+
+    def pass_row(b, part):
+        two = (x < last_row - 1) & wanted(b)
+
+        @pl.when(two)
+        def _():
+            near(b).wait_recv()
+            far(b).wait_recv()
+            row_out[b] = (part + near_in[b].astype(F32) + far_in[b].astype(F32)).astype(BF16)
+
+        @pl.when((x < last_row) & jnp.logical_not(two))
+        def _():
+            near(b).wait_recv()
+            row_out[b] = (part + near_in[b].astype(F32)).astype(BF16)
+
+        @pl.when(x == last_row)
+        def _():
+            row_out[b] = part.astype(BF16)
+
+        @pl.when(b != z)
+        def _():
+            row_copy(ring(b, -z, ROW), b).start()
+
+        @pl.when(b == z)
+        def _():
+            row_in[z] = row_out[b]
+
+    def emit_row(u, dk, dv):
+        for b, part in blocks_of(u, dk, dv):
+            pass_row(b, part)
+
+    @pl.when(x >= 2)
+    def _():
+        whole_backward(2, near_first, emit_far)
+        edge_backward(0, emit_far)
+        edge_backward(1, emit_far)
+
+    @pl.when(x >= 1)
+    def _():
+        whole_backward(near_first, here_first, emit_near)
+
+    @pl.loop(QUAD, ROW)
+    def _(b):
+        @pl.when(relays & relayed(b))
+        def _():
+            bend_in(b).wait_recv()
+            bend_out(b).start()
+
+    whole_backward(here_first, 8, emit_row)
+    edge_backward(8, emit_row)
+    edge_backward(9, emit_row)
+
+    for j in range(QUAD):
+        cols = slice(j * TQ, (j + 1) * TQ)
+        og_ref[cols, DIM:] = (dq_t[:, cols] * SCALE).T.astype(BF16)
+    for d in range(QUAD):
+        result_copy(1, d, spot, ring(spot, d, QUAD)).start()
+
+    @pl.when(half == 0)
+    def _():
+        @pl.loop(QUAD, ROW)
+        def _(b):
+            pass_row(b, jnp.zeros((TOK, 2 * DIM), F32))
+
     pairs = jnp.zeros_like(scores)
     read_part = jnp.zeros(read.shape, F32)
     for h in range(heads):
@@ -417,223 +634,6 @@
     share = length // crew
     maps[:, :, :DIM] = dot_tn(pairs, read).reshape(crew, share, DIM)
     maps[:, :, DIM:] = (read_part + dot(pairs, write)).reshape(crew, share, DIM)
-
-    collect("ctx", back_in, back_s, back_r)
-    chain(back_in, relinked, factor_ref, True)
-    after_ref[me] = relinked[me]
-    scatter("ctx", relinked, after_ref, relink_s, relink_r)
-
-    for d in range(QUAD):
-        for copy in query_copies(d, ring(spot, -d, QUAD), spot):
-            if d == 0:
-                copy.wait()
-            else:
-                copy.wait_recv()
-
-    first_key = half * QUERIES
-
-    def keys_of(u):
-        return pl.ds(pl.multiple_of(first_key + u * TK, TK), TK)
-
-    def tile(j):
-        return pl.ds(pl.multiple_of(j * TQ, TQ), TQ)
-
-    for j in range(QUAD):
-        cols = slice(j * TQ, (j + 1) * TQ)
-        qt_ref[:, cols] = qg_ref[cols, :DIM].T
-        gt_ref[:, cols] = qg_ref[cols, DIM:].T
-        own = facts_ref[me - spot + j]
-        own = jnp.concatenate([own[0:1, :], own[1:2, :]], axis=1).astype(jnp.int32)
-        high = 2 * SPAN + first_key + j * TQ + lax.broadcasted_iota(jnp.int32, (1, TQ), 1)
-        low_ref[0:1, cols] = jnp.maximum(own - (x - 2) * SPAN, high - (WINDOW - 1))
-        low_ref[1:2, cols] = high
-    stat_ref[0:1, :] = jnp.full((1, QUERIES), HIDDEN, F32)
-    stat_ref[1:2, :] = jnp.zeros((1, QUERIES), F32)
-    out_t[...] = jnp.zeros_like(out_t)
-    dq_t[...] = jnp.zeros_like(dq_t)
-
-    def score(u, j, edge):
-        s = dot(kv_ref[keys_of(u), :DIM], qt_ref[:, tile(j)])
-        at = first_key + u * TK + lax.broadcasted_iota(jnp.int32, (TK, TQ), 0)
-        shown = at >= low_ref[0:1, tile(j)]
-        if edge:
-            shown = shown & (at <= low_ref[1:2, tile(j)])
-        return jnp.where(shown, s, HIDDEN)
-
-    def forward(u, j, values_t, edge):
-        cols = tile(j)
-        s = score(u, j, edge)
-        top = stat_ref[0:1, cols]
-        new = jnp.maximum(top, jnp.max(s, axis=0, keepdims=True))
-        p = jnp.exp2((s - new) * SCALE2)
-        keep = jnp.exp2((top - new) * SCALE2)
-        stat_ref[0:1, cols] = new
-        stat_ref[1:2, cols] = stat_ref[1:2, cols] * keep + jnp.sum(p, axis=0, keepdims=True)
-        out_t[:, cols] = out_t[:, cols] * keep + dot(values_t, p.astype(BF16))
-
-    def whole_forward(begin, end):
-        @pl.loop(begin, end)
-        def _(u):
-            values_t = kv_ref[keys_of(u), DIM:].T
-            for j in range(QUAD):
-                forward(u, j, values_t, False)
-
-    def tiles_of_edge(u):
-        return (0, 2 * u + 2) if u < 2 else (2 * (u - 8), QUAD)
-
-    def edge_forward(u):
-        values_t = kv_ref[keys_of(u), DIM:].T
-
-        @pl.loop(*tiles_of_edge(u))
-        def _(j):
-            forward(u, j, values_t, True)
-
-    near_first, here_first = QUAD - 2 * half, 8 - 2 * half
-
-    edge_forward(8)
-    edge_forward(9)
-
-    whole_forward(here_first, 8)
-
-    @pl.when(x >= 1)
-    def _():
-        @pl.loop(0, ROW)
-        def _(b):
-            one_on(b).wait_recv()
-
-        whole_forward(near_first, here_first)
-
-    @pl.when(x >= 2)
-    def _():
-        @pl.loop(0, ROW)
-        def _(b):
-            @pl.when(wanted(b))
-            def _():
-                two_on(b).wait_recv()
-
-        whole_forward(2, near_first)
-        edge_forward(0)
-        edge_forward(1)
-
-    for j in range(QUAD):
-        cols = slice(j * TQ, (j + 1) * TQ)
-        total = stat_ref[1:2, cols]
-        attended = out_t[:, cols] / total
-        og_ref[cols, :DIM] = attended.T.astype(BF16)
-        stat_ref[2:3, cols] = stat_ref[0:1, cols] * SCALE2 + jnp.log2(total)
-        stat_ref[3:4, cols] = jnp.sum(gt_ref[:, cols].astype(F32) * attended, axis=0, keepdims=True)
-    for d in range(QUAD):
-        result_copy(0, d, spot, ring(spot, d, QUAD)).start()
-
-    def backward(u, j, edge):
-        cols = tile(j)
-        p = jnp.exp2(score(u, j, edge) * SCALE2 - stat_ref[2:3, cols])
-        dp = dot(kv_ref[keys_of(u), DIM:], gt_ref[:, cols])
-        p_ref[:, cols] = p.astype(BF16)
-        ds_ref[:, cols] = (p * (dp - stat_ref[3:4, cols])).astype(BF16)
-
-    def gather_backward(u):
-        dq_t[...] += dot(kv_ref[keys_of(u), :DIM].T, ds_ref[...])
-        return dot(ds_ref[...], qg_ref[:, :DIM]) * SCALE, dot(p_ref[...], qg_ref[:, DIM:])
-
-    def whole_backward(begin, end, emit):
-        @pl.loop(begin, end)
-        def _(u):
-            for j in range(QUAD):
-                backward(u, j, False)
-            emit(u, *gather_backward(u))
-
-    def edge_backward(u, emit):
-        begin, end = tiles_of_edge(u)
-        if end - begin < QUAD:
-            p_ref[...] = jnp.zeros_like(p_ref)
-            ds_ref[...] = jnp.zeros_like(ds_ref)
-
-        @pl.loop(begin, end)
-        def _(j):
-            backward(u, j, True)
-
-        emit(u, *gather_backward(u))
-
-    def blocks_of(u, dk, dv):
-        b = lax.rem(2 * u + QUAD * half, ROW)
-        both = jnp.concatenate([dk, dv], axis=1)
-        return (b, both[:TOK]), (b + 1, both[TOK:])
-
-    def emit_far(u, dk, dv):
-        for b, part in blocks_of(u, dk, dv):
-            far_out[b] = part.astype(BF16)
-            direct = jnp.logical_not(relayed(b))
-            pl.when(direct)(far(b).start)
-            pl.when(relayed(b))(bend_in(b).start)
-
-    def emit_near(u, dk, dv):
-        for b, part in blocks_of(u, dk, dv):
-            near_out[b] = part.astype(BF16)
-            near(b).start()
-
-    def pass_row(b, part):
-        two = (x < last_row - 1) & wanted(b)
-
-        @pl.when(two)
-        def _():
-            near(b).wait_recv()
-            far(b).wait_recv()
-            row_out[b] = (part + near_in[b].astype(F32) + far_in[b].astype(F32)).astype(BF16)
-
-        @pl.when((x < last_row) & jnp.logical_not(two))
-        def _():
-            near(b).wait_recv()
-            row_out[b] = (part + near_in[b].astype(F32)).astype(BF16)
-
-        @pl.when(x == last_row)
-        def _():
-            row_out[b] = part.astype(BF16)
-
-        @pl.when(b != z)
-        def _():
-            row_copy(ring(b, -z, ROW), b).start()
-
-        @pl.when(b == z)
-        def _():
-            row_in[z] = row_out[b]
-
-    def emit_row(u, dk, dv):
-        for b, part in blocks_of(u, dk, dv):
-            pass_row(b, part)
-
-    @pl.when(x >= 2)
-    def _():
-        whole_backward(2, near_first, emit_far)
-        edge_backward(0, emit_far)
-        edge_backward(1, emit_far)
-
-    @pl.when(x >= 1)
-    def _():
-        whole_backward(near_first, here_first, emit_near)
-
-    @pl.loop(QUAD, ROW)
-    def _(b):
-        @pl.when(relays & relayed(b))
-        def _():
-            bend_in(b).wait_recv()
-            bend_out(b).start()
-
-    whole_backward(here_first, 8, emit_row)
-    edge_backward(8, emit_row)
-    edge_backward(9, emit_row)
-
-    for j in range(QUAD):
-        cols = slice(j * TQ, (j + 1) * TQ)
-        og_ref[cols, DIM:] = (dq_t[:, cols] * SCALE).T.astype(BF16)
-    for d in range(QUAD):
-        result_copy(1, d, spot, ring(spot, d, QUAD)).start()
-
-    @pl.when(half == 0)
-    def _():
-        @pl.loop(QUAD, ROW)
-        def _(b):
-            pass_row(b, jnp.zeros((TOK, 2 * DIM), F32))
 
     collect("ctx", after_ref, relink_s, relink_r)
     write_part = maps[:, :, :DIM].reshape(length, DIM)

time: 155 us -> 147 us (0.948)
  Pallas kernels: 154 us -> 146 us
    pallas_call x1, Pallas kernels: 151 us -> 142 us  [body(): pl.pallas_call(functools.partial(mixer_kernel, width * crew), out_shape=t...]
where the time goes in v5:
time: 147 us; the launch traced here: 146 us
  Pallas kernels  146 us (99%)
    pallas_call x1, Pallas kernels, body(): pl.pallas_call(functools.partial(mixer_kernel, width * crew), out_shape=t...  142 us
    pallas_call x1, Pallas kernels, body(): pl.pallas_call(deliver_kernel, out_shape=tuple(outs), in_specs=[vmem] * l...  3.25 us

profile of v5, /device:TPU:2, one launch (start us, length us, event | category | flops | bytes accessed | tf_op | source)
XLA Modules:
  0.0 146.4 jit_solution(4253009915341313751)
XLA Ops:
  0.6 142.5 %shard_map.178 = (bf16[256,1024]{1,0:T(8,128)(2,1)}, bf16[256,512]{1,0:T(8,128)(2,1)}, bf16[256,1024]{1,0:T(8,128)(2,1)}, bf16[256,1024]{1,0:T(8,128)(2,1)}, bf1...) custom-call(s32[2,128]{1,0:T(2,128)} %bitcast.3, ...), custom_call_target="tpu_custom_call" | custom-call | tf_op jit(solution)/shard_map/pallas_call | solution.py:772
  143.2 3.2 %shard_map.179 = (bf16[256,1024]{1,0:T(8,128)(2,1)}, bf16[256,512]{1,0:T(8,128)(2,1)}, bf16[256,1024]{1,0:T(8,128)(2,1)}, bf16[256,1024]{1,0:T(8,128)(2,1)}, bf1...) custom-call(bf16[256,1024]{1,0:T(8,128)(2,1)} %get-tuple-element.18., ...), custom_call_target="tpu_custom_call" | custom-call | tf_op jit(solution)/shard_map/pallas_call | solution.py:785
